TPU v7x, 32 devices: a whole 2x2x4 slice. The times are simulated.
32 devices in a mesh: dp: 8 (over z, y), tensor: 4 (over x, core).
Axes of the slice: x: 2, y: 2, z: 4, core: 2. Of those that a mesh axis runs over, the one named last changes fastest.
Arguments:
- layer_input: bfloat16 [2048, 768], P('dp'), may hold values from -6 to 6
- encoder_states: bfloat16 [2048, 768], P('dp'), may hold values from -6 to 6
- output_grad: bfloat16 [2048, 768], P('dp'), may hold values from -6 to 6
- segments: int32 [8, 256], P('dp'), may hold values from 0 to 7, never falling along the last dimension, each value on 1 to 128 neighbouring positions
- buckets: int32 [256], replicated, may hold values from 0 to 31
- bias_table: bfloat16 [32, 12], P(None, 'tensor'), may hold values from -4 to 4
- gain_self: float32 [768], replicated, may hold values from 0.25 to 1.75
- self_query: bfloat16 [768, 768], P(None, 'tensor'), may hold values from -0.02734375 to 0.02734375
- self_key: bfloat16 [768, 768], P(None, 'tensor'), may hold values from -0.21875 to 0.21875
- self_value: bfloat16 [768, 768], P(None, 'tensor'), may hold values from -0.21875 to 0.21875
- self_out: bfloat16 [768, 768], P('tensor'), may hold values from -0.4375 to 0.4375
- gain_cross: float32 [768], replicated, may hold values from 0.25 to 1.75
- cross_query: bfloat16 [768, 768], P(None, 'tensor'), may hold values from -0.02734375 to 0.02734375
- cross_key: bfloat16 [768, 768], P(None, 'tensor'), may hold values from -0.21875 to 0.21875
- cross_value: bfloat16 [768, 768], P(None, 'tensor'), may hold values from -0.21875 to 0.21875
- cross_out: bfloat16 [768, 768], P('tensor'), may hold values from -0.4375 to 0.4375
- gain_ff: float32 [768], replicated, may hold values from 0.25 to 1.75
- ff_gate: bfloat16 [768, 2048], P(None, 'tensor'), may hold values from -0.21875 to 0.21875
- ff_up: bfloat16 [768, 2048], P(None, 'tensor'), may hold values from -0.21875 to 0.21875
- ff_down: bfloat16 [2048, 768], P('tensor'), may hold values from -0.125 to 0.125
Outputs:
- layer_output: bfloat16 [2048, 768], P('dp', 'tensor')
- d_layer_input: float32 [2048, 768], P('dp')
- d_encoder_states: float32 [2048, 768], P('dp', 'tensor')
- d_bias_table: float32 [32, 12], P(None, 'tensor')
- d_gain_self: float32 [768], P('dp')
- d_self_query: float32 [768, 768], P('dp', 'tensor')
- d_self_key: float32 [768, 768], P('dp', 'tensor')
- d_self_value: float32 [768, 768], P('dp', 'tensor')
- d_self_out: float32 [768, 768], P('tensor', 'dp')
- d_gain_cross: float32 [768], P('dp')
- d_cross_query: float32 [768, 768], P('dp', 'tensor')
- d_cross_key: float32 [768, 768], P('dp', 'tensor')
- d_cross_value: float32 [768, 768], P('dp', 'tensor')
- d_cross_out: float32 [768, 768], P('tensor', 'dp')
- d_gain_ff: float32 [768], P('dp')
- d_ff_gate: float32 [768, 2048], P('dp', 'tensor')
- d_ff_up: float32 [768, 2048], P('dp', 'tensor')
- d_ff_down: float32 [2048, 768], P('tensor', 'dp')
All inputs are finite; a program needn't handle non-finite values.
Results may differ from a plain program's by a relative error of at most 0.029.
Values sent between devices are 32-bit elements; how exact they have to be, the bound alone decides.
No kernel may reach another device: no remote copies, remote signals or barrier semaphores. Data moves between devices by JAX's collectives and lax.ppermute only.
A program may use at most 128 MiB of HBM per device.

v0:
```python
import jax
import jax.numpy as jnp
from jax import lax
from jax.sharding import PartitionSpec as P

epsilon = 1e-06
masked_value = -1000000000.0


def rms_norm(values, gain_vec):
    return (
        values * lax.rsqrt(jnp.mean(values * values, axis=-1, keepdims=True) + epsilon) * gain_vec
    )


def gelu_tanh(values):
    return jax.nn.gelu(values, approximate=True)


def product(left, right):
    return jnp.dot(left, right, preferred_element_type=jnp.float32)


def product_left(left, right):
    return lax.dot_general(
        left, right, (((0,), (0,)), ((), ())), preferred_element_type=jnp.float32
    )


def product_right(left, right):
    return lax.dot_general(
        left, right, (((1,), (1,)), ((), ())), preferred_element_type=jnp.float32
    )


def allowed_pairs(segment_row, row_count):
    position = jnp.arange(row_count, dtype=jnp.int32)
    causal = position[:, None] >= position[None, :]
    return causal & (segment_row[:, None] == segment_row[None, :])


def offset_table(buckets, bias_table):
    onehot = (buckets[:, None] == jnp.arange(bias_table.shape[0], dtype=jnp.int32)[None, :]).astype(
        jnp.float32
    )
    return (
        onehot,
        jnp.dot(onehot, bias_table.astype(jnp.float32), precision=lax.Precision.HIGHEST),
    )


def spread_diagonals(per_offset, row_count):
    head_count = per_offset.shape[1]
    pattern = jnp.concatenate(
        [
            jnp.flip(jnp.transpose(per_offset), axis=1),
            jnp.zeros((head_count, row_count), jnp.float32),
        ],
        axis=1,
    )
    width = 2 * row_count - 1
    tiled = jnp.tile(pattern, (1, row_count))[:, : row_count * width]
    return tiled.reshape(head_count, row_count, width)[:, :, row_count - 1 :]


def sum_diagonals(d_scores, row_count):
    head_count = d_scores.shape[0]
    width = 2 * row_count - 1
    placed = jnp.concatenate(
        [jnp.zeros((head_count, row_count, row_count - 1), jnp.float32), d_scores], axis=2
    )
    flat = placed.reshape(head_count, row_count * width)
    flat = jnp.concatenate([flat, jnp.zeros((head_count, row_count), jnp.float32)], axis=1)
    folded = jnp.sum(flat.reshape(head_count, row_count, 2 * row_count), axis=1)
    return jnp.transpose(jnp.flip(folded[:, :row_count], axis=1))


def scores_of(query, key_rows, head_count, pos_bias, allowed):
    query_h = query.reshape(query.shape[0], head_count, -1)
    key_h = key_rows.reshape(key_rows.shape[0], head_count, -1)
    scores = jnp.einsum("qhd,khd->hqk", query_h, key_h, preferred_element_type=jnp.float32)
    if pos_bias is not None:
        scores = scores + pos_bias
    if allowed is not None:
        scores = jnp.where(allowed[None], scores, masked_value)
    return scores


def attend(query, key_rows, values, head_count, pos_bias, allowed):
    scores = scores_of(query, key_rows, head_count, pos_bias, allowed)
    row_top = jnp.max(scores, axis=-1, keepdims=True)
    exp_scores = jnp.exp(scores - row_top)
    exp_total = jnp.sum(exp_scores, axis=-1, keepdims=True)
    weights = (exp_scores / exp_total).astype(jnp.bfloat16)
    value_h = values.reshape(values.shape[0], head_count, -1)
    mixed = jnp.einsum("hqk,khd->qhd", weights, value_h, preferred_element_type=jnp.float32)
    return (mixed.reshape(query.shape[0], -1).astype(jnp.bfloat16), row_top + jnp.log(exp_total))


def attend_back(query, key_rows, values, mixed, d_mixed, lse_rows, head_count, pos_bias, allowed):
    scores = scores_of(query, key_rows, head_count, pos_bias, allowed)
    prob_rows = jnp.exp(scores - lse_rows)
    row_count = query.shape[0]
    query_h = query.reshape(row_count, head_count, -1)
    key_h = key_rows.reshape(key_rows.shape[0], head_count, -1)
    value_h = values.reshape(values.shape[0], head_count, -1)
    dmix_h = d_mixed.reshape(row_count, head_count, -1)
    mix_h = mixed.reshape(row_count, head_count, -1)
    d_probs = jnp.einsum("qhd,khd->hqk", dmix_h, value_h, preferred_element_type=jnp.float32)
    delta_rows = jnp.transpose(
        jnp.sum(dmix_h.astype(jnp.float32) * mix_h.astype(jnp.float32), axis=-1)
    )[:, :, None]
    d_scores = prob_rows * (d_probs - delta_rows)
    d_weights = d_scores.astype(jnp.bfloat16)
    d_query = jnp.einsum("hqk,khd->qhd", d_weights, key_h, preferred_element_type=jnp.float32)
    d_keys = jnp.einsum("hqk,qhd->khd", d_weights, query_h, preferred_element_type=jnp.float32)
    d_values = jnp.einsum(
        "hqk,qhd->khd", prob_rows.astype(jnp.bfloat16), dmix_h, preferred_element_type=jnp.float32
    )
    return (
        d_query.reshape(row_count, -1).astype(jnp.bfloat16),
        d_keys.reshape(key_rows.shape[0], -1).astype(jnp.bfloat16),
        d_values.reshape(key_rows.shape[0], -1).astype(jnp.bfloat16),
        d_scores,
    )


def norm_back(values, gain_vec, cotangent):
    unused, pull_back = jax.vjp(rms_norm, values, gain_vec)
    return pull_back(cotangent)


def branch_sum(partial_rows):
    return lax.psum(partial_rows, "tensor")


def input_sum(partial_rows):
    return lax.psum(partial_rows, "tensor")


def on_device(
    layer_input,
    encoder_states,
    output_grad,
    segments,
    buckets,
    bias_table,
    gain_self,
    self_query,
    self_key,
    self_value,
    self_out,
    gain_cross,
    cross_query,
    cross_key,
    cross_value,
    cross_out,
    gain_ff,
    ff_gate,
    ff_up,
    ff_down,
):
    heads_local = bias_table.shape[1]
    row_count = layer_input.shape[0]
    stream_in = layer_input.astype(jnp.float32)
    allowed = allowed_pairs(segments[0], row_count)
    onehot, per_offset = offset_table(buckets, bias_table)
    pos_bias = spread_diagonals(per_offset, row_count)
    normed_self = rms_norm(stream_in, gain_self).astype(jnp.bfloat16)
    self_q = product(normed_self, self_query).astype(jnp.bfloat16)
    self_k = product(normed_self, self_key).astype(jnp.bfloat16)
    self_v = product(normed_self, self_value).astype(jnp.bfloat16)
    mix_self, lse_self = attend(self_q, self_k, self_v, heads_local, pos_bias, allowed)
    resid_one = stream_in + branch_sum(product(mix_self, self_out))
    normed_cross = rms_norm(resid_one, gain_cross).astype(jnp.bfloat16)
    cross_q = product(normed_cross, cross_query).astype(jnp.bfloat16)
    cross_k = product(encoder_states, cross_key).astype(jnp.bfloat16)
    cross_v = product(encoder_states, cross_value).astype(jnp.bfloat16)
    mix_cross, lse_cross = attend(cross_q, cross_k, cross_v, heads_local, None, None)
    resid_two = resid_one + branch_sum(product(mix_cross, cross_out))
    normed_ff = rms_norm(resid_two, gain_ff).astype(jnp.bfloat16)
    gate_pre = product(normed_ff, ff_gate)
    up_pre = product(normed_ff, ff_up)
    activ, gelu_pull = jax.vjp(gelu_tanh, gate_pre)
    hidden = (activ * up_pre).astype(jnp.bfloat16)
    ff_share = lax.psum_scatter(product(hidden, ff_down), "tensor", scatter_dimension=1, tiled=True)
    col_width = ff_share.shape[1]
    resid_cols = lax.dynamic_slice_in_dim(
        resid_two, lax.axis_index("tensor") * col_width, col_width, 1
    )
    layer_output = (resid_cols + ff_share).astype(jnp.bfloat16)
    grad_out = output_grad.astype(jnp.float32)
    d_ff_down = product_left(hidden, output_grad)
    d_hidden = product_right(output_grad, ff_down)
    d_gate_pre = gelu_pull(d_hidden * up_pre)[0].astype(jnp.bfloat16)
    d_up_pre = (d_hidden * activ).astype(jnp.bfloat16)
    d_ff_gate = product_left(normed_ff, d_gate_pre)
    d_ff_up = product_left(normed_ff, d_up_pre)
    d_normed_ff = input_sum(product_right(d_gate_pre, ff_gate) + product_right(d_up_pre, ff_up))
    d_resid, d_gain_ff = norm_back(resid_two, gain_ff, d_normed_ff)
    grad_two = grad_out + d_resid
    grad_two_b = grad_two.astype(jnp.bfloat16)
    d_cross_out = product_left(mix_cross, grad_two_b)
    d_mix_cross = product_right(grad_two_b, cross_out).astype(jnp.bfloat16)
    d_cross_q, d_cross_k, d_cross_v, unused = attend_back(
        cross_q, cross_k, cross_v, mix_cross, d_mix_cross, lse_cross, heads_local, None, None
    )
    d_cross_query = product_left(normed_cross, d_cross_q)
    d_cross_key = product_left(encoder_states, d_cross_k)
    d_cross_value = product_left(encoder_states, d_cross_v)
    d_normed_cross = lax.psum(product_right(d_cross_q, cross_query), "tensor")
    d_encoder_states = lax.psum_scatter(
        product_right(d_cross_k, cross_key) + product_right(d_cross_v, cross_value),
        "tensor",
        scatter_dimension=1,
        tiled=True,
    )
    d_resid, d_gain_cross = norm_back(resid_one, gain_cross, d_normed_cross)
    grad_one = grad_two + d_resid
    grad_one_b = grad_one.astype(jnp.bfloat16)
    d_self_out = product_left(mix_self, grad_one_b)
    d_mix_self = product_right(grad_one_b, self_out).astype(jnp.bfloat16)
    d_self_q, d_self_k, d_self_v, ds_self = attend_back(
        self_q, self_k, self_v, mix_self, d_mix_self, lse_self, heads_local, pos_bias, allowed
    )
    by_offset = sum_diagonals(ds_self, row_count)
    d_bias_table = lax.psum(jnp.dot(onehot.T, by_offset, precision=lax.Precision.HIGHEST), "dp")
    d_self_query = product_left(normed_self, d_self_q)
    d_self_key = product_left(normed_self, d_self_k)
    d_self_value = product_left(normed_self, d_self_v)
    d_normed_self = input_sum(
        product_right(d_self_q, self_query)
        + product_right(d_self_k, self_key)
        + product_right(d_self_v, self_value)
    )
    d_resid, d_gain_self = norm_back(stream_in, gain_self, d_normed_self)
    d_layer_input = grad_one + d_resid
    summed = (
        lax.psum_scatter(d_gain_self, "dp", scatter_dimension=0, tiled=True),
        lax.psum_scatter(d_self_query, "dp", scatter_dimension=0, tiled=True),
        lax.psum_scatter(d_self_key, "dp", scatter_dimension=0, tiled=True),
        lax.psum_scatter(d_self_value, "dp", scatter_dimension=0, tiled=True),
        lax.psum_scatter(d_self_out, "dp", scatter_dimension=1, tiled=True),
        lax.psum_scatter(d_gain_cross, "dp", scatter_dimension=0, tiled=True),
        lax.psum_scatter(d_cross_query, "dp", scatter_dimension=0, tiled=True),
        lax.psum_scatter(d_cross_key, "dp", scatter_dimension=0, tiled=True),
        lax.psum_scatter(d_cross_value, "dp", scatter_dimension=0, tiled=True),
        lax.psum_scatter(d_cross_out, "dp", scatter_dimension=1, tiled=True),
        lax.psum_scatter(d_gain_ff, "dp", scatter_dimension=0, tiled=True),
        lax.psum_scatter(d_ff_gate, "dp", scatter_dimension=0, tiled=True),
        lax.psum_scatter(d_ff_up, "dp", scatter_dimension=0, tiled=True),
        lax.psum_scatter(d_ff_down, "dp", scatter_dimension=1, tiled=True),
    )
    return (layer_output, d_layer_input, d_encoder_states, d_bias_table) + tuple(summed)


def solution(mesh):
    in_specs = (
        P("dp", None),
        P("dp", None),
        P("dp", None),
        P("dp", None),
        P(),
        P(None, "tensor"),
        P(),
        P(None, "tensor"),
        P(None, "tensor"),
        P(None, "tensor"),
        P("tensor", None),
        P(),
        P(None, "tensor"),
        P(None, "tensor"),
        P(None, "tensor"),
        P("tensor", None),
        P(),
        P(None, "tensor"),
        P(None, "tensor"),
        P("tensor", None),
    )
    out_specs = (
        P("dp", "tensor"),
        P("dp", None),
        P("dp", "tensor"),
        P(None, "tensor"),
        P("dp"),
        P("dp", "tensor"),
        P("dp", "tensor"),
        P("dp", "tensor"),
        P("tensor", "dp"),
        P("dp"),
        P("dp", "tensor"),
        P("dp", "tensor"),
        P("dp", "tensor"),
        P("tensor", "dp"),
        P("dp"),
        P("dp", "tensor"),
        P("dp", "tensor"),
        P("tensor", "dp"),
    )
    return jax.shard_map(
        on_device, mesh=mesh, in_specs=in_specs, out_specs=out_specs, check_vma=False
    )
```

profile of v0, /device:TPU:0, one launch (start us, length us, event | category | flops | bytes accessed | tf_op | source)
XLA Modules:
  0.0 1027.0 jit_solution(11915159089499301788)
XLA Ops:
  9.7 1.5 fusion.28
  11.2 2.1 convolution_convert_fusion.14
  16.6 1.7 slice.12
  18.3 3.3 reshape.230
  22.8 1.4 copy.105
  29.6 35.9 %all-reduce.13.cloned.1.call-done = f32[256,768]{1,0:T(8,128)} async-done(((f32[256,768]{1,0:T(8,128)}), f32[256,768]{1,0:T(8,128)}) %all-reduce.13.cloned.1.call-update) | async-done | bytes 786448 | tf_op jit(solution)/shard_map/psum | solution.py:134
  65.5 1.3 multiply_reduce_fusion.5
  70.6 35.1 %all-reduce.15.cloned.1.call-done = f32[256,768]{1,0:T(8,128)} async-done(((f32[256,768]{1,0:T(8,128)}), f32[256,768]{1,0:T(8,128)}) %all-reduce.15.cloned.1.call-update) | async-done | bytes 786448 | tf_op jit(solution)/shard_map/psum | solution.py:134
  107.8 1.6 fusion.56
  109.9 1.4 multiply_convert_fusion.2
  114.7 34.4 %all-reduce.17.cloned.1.call-done = f32[256,768]{1,0:T(8,128)} async-done(((f32[256,768]{1,0:T(8,128)}), f32[256,768]{1,0:T(8,128)}) %all-reduce.17.cloned.1.call-update) | async-done | bytes 786448 | tf_op jit(solution)/shard_map/psum | solution.py:138
  149.1 2.0 multiply_reduce_fusion
  156.7 33.7 %all-reduce.19.cloned.1.call-done = f32[256,768]{1,0:T(8,128)} async-done(((f32[256,768]{1,0:T(8,128)}), f32[256,768]{1,0:T(8,128)}) %all-reduce.19.cloned.1.call-update) | async-done | bytes 786448 | tf_op jit(solution)/shard_map/psum | solution.py:211
  190.4 2.0 multiply_reduce_fusion.1
  194.4 1.5 fusion
  198.8 2.4 convolution_bitcast_fusion.1
  201.3 2.3 convolution_bitcast_fusion
  203.6 2.4 convolution_bitcast_fusion.2
  208.1 2.1 convolution_bitcast_fusion.4
  210.2 2.2 copy.99
  212.5 1.5 convolution_convert_fusion
  214.6 2.1 convolution_bitcast_fusion.3
  216.7 2.2 copy.101
  219.0 2.2 fusion.41
  221.3 1.4 fusion.60
  228.2 2.6 fusion.63
  230.9 2.6 fusion.62
  233.6 1.6 fusion.61
  237.6 1.5 concatenate.10.clone
  239.1 3.4 reshape.236
  242.4 1.9 concatenate.11
  245.9 2.1 fusion.7
  248.0 37.8 %all-reduce.6 = (f32[32,3]{0,1:T(4,128)}, f32[768]{0:T(1024)}, f32[768]{0:T(1024)}, f32[768]{0:T(1024)}) all-reduce(f32[32,3]{0,1:T(4,128)} %fusion.35, f32[768]{0:T(1024)} %get-tuple-element.76, f32[768]{0:T(1024)S(1)} %copy-done.78, f32[768]{0:T(1024)S(1)} %copy-done.77), channel_id=1, replica_groups=mesh['dp'=8,'tensor'=4] {'dp'}, use_global_device_ids=true, to_apply=%region_20.21 | all-reduce | flops 2400 | bytes 19200 | tf_op jit(solution)/shard_map/psum | solution.py:227
  291.4 9.2 reduce-scatter.48.cloned.1.call-done
  300.5 1.6 copy.104
  302.2 23.1 %reduce-scatter.40.cloned.1.call-done = f32[192,256]{1,0:T(8,128)} async-done(((f32[768,256]{1,0:T(8,128)}), f32[192,256]{1,0:T(8,128)}) %reduce-scatter.40.cloned.1.call-update) | async-done | bytes 196624
  327.3 64.5 %reduce-scatter.42.cloned.1.call-done = f32[96,192]{1,0:T(8,128)} async-done(((f32[768,192]{1,0:T(8,128)}), f32[96,192]{1,0:T(8,128)}) %reduce-scatter.42.cloned.1.call-update) | async-done | bytes 73744
  391.8 1.6 copy.98
  393.4 64.5 %reduce-scatter.44.cloned.1.call-done = f32[96,192]{1,0:T(8,128)} async-done(((f32[768,192]{1,0:T(8,128)}), f32[96,192]{1,0:T(8,128)}) %reduce-scatter.44.cloned.1.call-update) | async-done | bytes 73744
  458.0 66.0 %reduce-scatter.46.cloned.1.call-done = f32[96,192]{1,0:T(8,128)} async-done(((f32[768,192]{1,0:T(8,128)}), f32[96,192]{1,0:T(8,128)}) %reduce-scatter.46.cloned.1.call-update) | async-done | bytes 73744
  524.0 66.3 %reduce-scatter.32.cloned.1.call-done = f32[96,192]{1,0:T(8,128)} async-done(((f32[768,192]{1,0:T(8,128)}), f32[96,192]{1,0:T(8,128)}) %reduce-scatter.32.cloned.1.call-update) | async-done | bytes 73744 | tf_op jit(solution)/shard_map/reduce_scatter | solution.py:245
  590.2 25.2 %reduce-scatter.24.cloned.1.call-done = f32[256,192]{0,1:T(8,128)} async-done(((f32[256,768]{0,1:T(8,128)}), f32[256,192]{0,1:T(8,128)}) %reduce-scatter.24.cloned.1.call-update) | async-done | bytes 196624 | tf_op jit(solution)/shard_map/reduce_scatter | solution.py:212
  615.4 67.1 %reduce-scatter.26.cloned.1.call-done = f32[96,192]{1,0:T(8,128)} async-done(((f32[768,192]{1,0:T(8,128)}), f32[96,192]{1,0:T(8,128)}) %reduce-scatter.26.cloned.1.call-update) | async-done | bytes 73744 | tf_op jit(solution)/shard_map/reduce_scatter | solution.py:240
  682.6 66.0 %reduce-scatter.30.cloned.1.call-done = f32[96,192]{1,0:T(8,128)} async-done(((f32[768,192]{1,0:T(8,128)}), f32[96,192]{1,0:T(8,128)}) %reduce-scatter.30.cloned.1.call-update) | async-done | bytes 73744 | tf_op jit(solution)/shard_map/reduce_scatter | solution.py:242
  748.6 66.0 %reduce-scatter.28.cloned.1.call-done = f32[96,192]{1,0:T(8,128)} async-done(((f32[768,192]{1,0:T(8,128)}), f32[96,192]{1,0:T(8,128)}) %reduce-scatter.28.cloned.1.call-update) | async-done | bytes 73744 | tf_op jit(solution)/shard_map/reduce_scatter | solution.py:241
  814.6 68.7 %reduce-scatter.38.cloned.1.call-done = f32[512,96]{0,1:T(8,128)} async-done(((f32[512,768]{0,1:T(8,128)}), f32[512,96]{0,1:T(8,128)}) %reduce-scatter.38.cloned.1.call-update) | async-done | bytes 196624 | tf_op jit(solution)/shard_map/reduce_scatter | solution.py:252
  883.3 68.5 %reduce-scatter.36.cloned.1.call-done = f32[96,512]{1,0:T(8,128)} async-done(((f32[768,512]{1,0:T(8,128)}), f32[96,512]{1,0:T(8,128)}) %reduce-scatter.36.cloned.1.call-update) | async-done | bytes 196624 | tf_op jit(solution)/shard_map/reduce_scatter | solution.py:251
  951.7 68.5 %reduce-scatter.34.cloned.1.call-done = f32[96,512]{1,0:T(8,128)} async-done(((f32[768,512]{1,0:T(8,128)}), f32[96,512]{1,0:T(8,128)}) %reduce-scatter.34.cloned.1.call-update) | async-done | bytes 196624 | tf_op jit(solution)/shard_map/reduce_scatter | solution.py:250
  (283 shorter events, 50.8 us)
Async XLA Ops:
  7.2 102.7 %copy-start = (bf16[512,768]{1,0:T(8,128)(2,1)S(1)}, bf16[512,768]{1,0:T(8,128)(2,1)}, u32[]{:S(2)}) copy-start(bf16[512,768]{1,0:T(8,128)(2,1)} %param.39) | copy-start | bytes 2359300
  7.2 6.1 copy-start.1
  7.2 6.1 copy-start.63
  7.2 6.1 copy-start.58
  7.2 7.1 copy-start.60
  7.3 58.3 %all-reduce.13.cloned.1.call-start = ((), (), s32[]{:S(2)}) async-start(), calls=%async_computation.13 | async-start | bytes 1572864 | tf_op jit(solution)/shard_map/psum | solution.py:134
  8.6 5.8 copy-start.85
  8.6 6.8 copy-start.72
  24.7 169.2 %copy-start.2 = (f32[3,256,256]{1,2,0:T(8,128)}, f32[3,256,256]{1,2,0:T(8,128)S(1)}, u32[]{:S(2)}) copy-start(f32[3,256,256]{1,2,0:T(8,128)S(1)} %get-tuple-element.90) | copy-start | bytes 2359300
  25.8 3.9 copy-start.36
  25.8 2.9 copy-start.23
  27.7 78.1 %all-reduce.15.cloned.1.call-start = ((), (), s32[]{:S(2)}) async-start(), calls=%async_computation.14 | async-start | bytes 1572864 | tf_op jit(solution)/shard_map/psum | solution.py:134
  28.7 38.3 %copy-start.27 = (bf16[768,192]{0,1:T(8,128)(2,1)S(1)}, bf16[768,192]{0,1:T(8,128)(2,1)}, u32[]{:S(2)}) copy-start(bf16[768,192]{0,1:T(8,128)(2,1)} %param.32) | copy-start | bytes 884740
  28.7 38.3 %copy-start.66 = (f32[768]{0:T(1024)S(1)}, f32[768]{0:T(1024)}, u32[]{:S(2)}) copy-start(f32[768]{0:T(1024)} %param.31) | copy-start | bytes 9220
  70.6 37.1 %copy-start.67 = (f32[768]{0:T(1024)S(1)}, f32[768]{0:T(1024)}, u32[]{:S(2)}) copy-start(f32[768]{0:T(1024)} %param.36) | copy-start | bytes 9220
  70.6 78.5 %all-reduce.17.cloned.1.call-start = ((), (), s32[]{:S(2)}) async-start(), calls=%async_computation.15 | async-start | bytes 1572864 | tf_op jit(solution)/shard_map/psum | solution.py:138
  107.1 2.4 copy-start.13
  107.1 2.4 copy-start.81
  113.9 76.5 %all-reduce.19.cloned.1.call-start = ((), (), s32[]{:S(2)}) async-start(), calls=%async_computation.16 | async-start | bytes 1572864 | tf_op jit(solution)/shard_map/psum | solution.py:211
  153.1 2.3 copy-start.69
  155.2 90.7 %all-reduce.21.cloned.1.call-start = ((), (), s32[]{:S(2)}) async-start(), calls=%async_computation.17 | async-start | bytes 1572864 | tf_op jit(solution)/shard_map/psum | solution.py:138
  156.7 35.7 %copy-start.84 = (f32[256]{0:T(256)S(1)}, f32[256]{0:T(256)}, u32[]{:S(2)}) copy-start(f32[256]{0:T(256)} %copy-done.83) | copy-start | bytes 3076
  190.4 2.1 copy-start.16
  190.4 2.1 copy-start.75
  193.5 2.5 copy-start.3
  193.8 2.2 copy-start.54
  194.1 3.3 copy-start.47
  194.1 2.1 copy-start.52
  198.7 101.8 %reduce-scatter.48.cloned.1.call-start = ((), (), s32[]{:S(2)}) async-start(), calls=%async_computation.30 | async-start | bytes 884736
  201.2 124.1 %reduce-scatter.40.cloned.1.call-start = ((), (), s32[]{:S(2)}) async-start(), calls=%async_computation.26 | async-start | bytes 983040
  203.6 188.2 %reduce-scatter.42.cloned.1.call-start = ((), (), s32[]{:S(2)}) async-start(), calls=%async_computation.27 | async-start | bytes 884736
  206.1 251.9 %reduce-scatter.44.cloned.1.call-start = ((), (), s32[]{:S(2)}) async-start(), calls=%async_computation.28 | async-start | bytes 884736
  212.4 311.5 %reduce-scatter.46.cloned.1.call-start = ((), (), s32[]{:S(2)}) async-start(), calls=%async_computation.29 | async-start | bytes 884736
  214.6 4.4 copy-start.76
  218.9 371.3 %reduce-scatter.32.cloned.1.call-start = ((), (), s32[]{:S(2)}) async-start(), calls=%async_computation.22 | async-start | bytes 884736 | tf_op jit(solution)/shard_map/reduce_scatter | solution.py:245
  221.2 394.2 %reduce-scatter.24.cloned.1.call-start = ((), (), s32[]{:S(2)}) async-start(), calls=%async_computation.18 | async-start | bytes 983040 | tf_op jit(solution)/shard_map/reduce_scatter | solution.py:212
  224.0 458.6 %reduce-scatter.26.cloned.1.call-start = ((), (), s32[]{:S(2)}) async-start(), calls=%async_computation.19 | async-start | bytes 884736 | tf_op jit(solution)/shard_map/reduce_scatter | solution.py:240
  225.4 523.2 %reduce-scatter.30.cloned.1.call-start = ((), (), s32[]{:S(2)}) async-start(), calls=%async_computation.21 | async-start | bytes 884736 | tf_op jit(solution)/shard_map/reduce_scatter | solution.py:242
  226.8 587.8 %reduce-scatter.28.cloned.1.call-start = ((), (), s32[]{:S(2)}) async-start(), calls=%async_computation.20 | async-start | bytes 884736 | tf_op jit(solution)/shard_map/reduce_scatter | solution.py:241
  228.2 2.7 copy-start.10
  228.2 655.1 %reduce-scatter.38.cloned.1.call-start = ((), (), s32[]{:S(2)}) async-start(), calls=%async_computation.25 | async-start | bytes 1769472 | tf_op jit(solution)/shard_map/reduce_scatter | solution.py:252
  230.8 2.7 copy-start.32
  230.9 720.9 %reduce-scatter.36.cloned.1.call-start = ((), (), s32[]{:S(2)}) async-start(), calls=%async_computation.24 | async-start | bytes 1769472 | tf_op jit(solution)/shard_map/reduce_scatter | solution.py:251
  233.5 786.7 %reduce-scatter.34.cloned.1.call-start = ((), (), s32[]{:S(2)}) async-start(), calls=%async_computation.23 | async-start | bytes 1769472 | tf_op jit(solution)/shard_map/reduce_scatter | solution.py:250
  244.4 3.6 copy-start.77
  244.4 3.6 copy-start.78
  244.4 45.8 %copy-start.4 = (f32[256,768]{1,0:T(8,128)S(1)}, f32[256,768]{1,0:T(8,128)}, u32[]{:S(2)}) copy-start(f32[256,768]{1,0:T(8,128)} %copy-done.3) | copy-start | bytes 2359300
  245.9 44.4 %copy-start.14 = (f32[256,768]{1,0:T(8,128)S(1)}, f32[256,768]{1,0:T(8,128)}, u32[]{:S(2)}) copy-start(f32[256,768]{1,0:T(8,128)} %all-reduce.21.cloned.1.call-done) | copy-start | bytes 2359300
  (60 other events, 74.8 us)
Sparse Core Ops, SparseCore 0:
  27.8 37.7 all-reduce.12
  70.7 35.0 all-reduce.14
  114.0 35.0 all-reduce.16
  155.3 35.0 all-reduce.18
  198.9 34.7 all-reduce.20
  236.8 63.6 reduce-scatter.47
  303.1 22.1 reduce-scatter.39
  328.6 63.1 reduce-scatter.41
  395.7 62.2 reduce-scatter.43
  461.7 62.2 reduce-scatter.45
  527.9 62.3 reduce-scatter.31
  593.2 22.2 reduce-scatter.23
  619.3 63.2 reduce-scatter.25
  686.3 62.2 reduce-scatter.29
  752.3 62.2 reduce-scatter.27
  818.4 64.7 reduce-scatter.37
  887.1 64.5 reduce-scatter.35
  955.6 64.5 reduce-scatter.33
where the time goes:
time: 1030 us
  waiting for transfers between devices  863 us (84%)
  matrix products  52.5 us (5%)
  local copies, waits for them, and re-layouts  39.8 us (4%)
  blocking collectives  37.8 us (4%)
  other arithmetic  16.9 us (2%)
  between operations  16 us (2%)
    unnamed x23, waiting for transfers between devices  228 us
    psum x2, waiting for transfers between devices, branch_sum(): return lax.psum(partial_rows, 'tensor')  71 us
    reduce_scatter x1, waiting for transfers between devices, on_device(): lax.psum_scatter(d_ff_down, 'dp', scatter_dimension=1, tiled=True)  68.7 us
    reduce_scatter x1, waiting for transfers between devices, on_device(): lax.psum_scatter(d_ff_gate, 'dp', scatter_dimension=0, tiled=True)  68.5 us
    reduce_scatter x1, waiting for transfers between devices, on_device(): lax.psum_scatter(d_ff_up, 'dp', scatter_dimension=0, tiled=True)  68.5 us
    reduce_scatter x1, waiting for transfers between devices, on_device(): lax.psum_scatter(d_self_query, 'dp', scatter_dimension=0, tiled=True)  67.1 us
    reduce_scatter x1, waiting for transfers between devices, on_device(): lax.psum_scatter(d_cross_query, 'dp', scatter_dimension=0, tiled=True)  66.3 us
    reduce_scatter x1, waiting for transfers between devices, on_device(): lax.psum_scatter(d_self_key, 'dp', scatter_dimension=0, tiled=True)  66 us
  transfers between devices with their start and end apart: 18, of which 17 were waited for; matrix products, arithmetic and copies ran while one was open for 6% of the time, Pallas kernels for 0%

commit v1 on v0

--- a/solution.py
+++ b/solution.py
@@ -130,12 +130,78 @@
     return pull_back(cotangent)
 
 
-def branch_sum(partial_rows):
-    return lax.psum(partial_rows, "tensor")
-
-
-def input_sum(partial_rows):
-    return lax.psum(partial_rows, "tensor")
+def swap_pairs(count, stride):
+    return [(i, i ^ stride) for i in range(count)]
+
+
+def power_of_two(count):
+    return count > 1 and count & (count - 1) == 0
+
+
+def pick_half(values, bit, axis):
+    half = values.shape[axis] // 2
+    return lax.dynamic_slice_in_dim(values, bit * half, half, axis)
+
+
+def tensor_sum(partial_rows):
+    count = lax.axis_size("tensor")
+    if not power_of_two(count):
+        return lax.psum(partial_rows, "tensor")
+    bit = lax.axis_index("tensor") & 1
+    total = pick_half(partial_rows, bit, 0) + lax.ppermute(
+        pick_half(partial_rows, 1 - bit, 0), "tensor", swap_pairs(count, 1)
+    )
+    stride = 2
+    while stride < count:
+        total = total + lax.ppermute(total, "tensor", swap_pairs(count, stride))
+        stride *= 2
+    other = lax.ppermute(total, "tensor", swap_pairs(count, 1))
+    first = jnp.where(bit == 0, total, other)
+    second = jnp.where(bit == 0, other, total)
+    return jnp.concatenate([first, second], axis=0)
+
+
+def scatter_blocks(blocks, axis_name, bits):
+    count = lax.axis_size(axis_name)
+    index = lax.axis_index(axis_name)
+    remaining = list(range(count.bit_length() - 1))
+    shape = blocks.shape[1:]
+    for bit in bits:
+        place = remaining.index(bit)
+        low = 2**place
+        high = 2 ** (len(remaining) - 1 - place)
+        mine = (index >> bit) & 1
+        view = blocks.reshape((high, 2, low) + shape)
+        keep = lax.dynamic_index_in_dim(view, mine, 1, keepdims=False)
+        send = lax.dynamic_index_in_dim(view, 1 - mine, 1, keepdims=False)
+        received = lax.ppermute(send, axis_name, swap_pairs(count, 2**bit))
+        blocks = (keep + received).reshape((high * low,) + shape)
+        remaining.remove(bit)
+    return blocks[0]
+
+
+def scatter_sum(blocks, axis_name, low_first):
+    count = lax.axis_size(axis_name)
+    if not power_of_two(count):
+        return lax.psum_scatter(blocks, axis_name, scatter_dimension=0, tiled=False)
+    bits = list(range(count.bit_length() - 1))
+    if not low_first:
+        bits = bits[1:] + bits[:1]
+    return scatter_blocks(blocks, axis_name, bits)
+
+
+def row_scatter(grad_rows, low_first=True):
+    count = lax.axis_size("dp")
+    return scatter_sum(
+        grad_rows.reshape(count, grad_rows.shape[0] // count, grad_rows.shape[1]), "dp", low_first
+    )
+
+
+def column_scatter(partial_rows):
+    count = lax.axis_size("tensor")
+    width = partial_rows.shape[1] // count
+    blocks = jnp.stack([partial_rows[:, i * width : (i + 1) * width] for i in range(count)])
+    return scatter_sum(blocks, "tensor", True)
 
 
 def on_device(
@@ -171,87 +237,115 @@
     self_k = product(normed_self, self_key).astype(jnp.bfloat16)
     self_v = product(normed_self, self_value).astype(jnp.bfloat16)
     mix_self, lse_self = attend(self_q, self_k, self_v, heads_local, pos_bias, allowed)
-    resid_one = stream_in + branch_sum(product(mix_self, self_out))
+    resid_one = stream_in + tensor_sum(product(mix_self, self_out))
     normed_cross = rms_norm(resid_one, gain_cross).astype(jnp.bfloat16)
     cross_q = product(normed_cross, cross_query).astype(jnp.bfloat16)
     cross_k = product(encoder_states, cross_key).astype(jnp.bfloat16)
     cross_v = product(encoder_states, cross_value).astype(jnp.bfloat16)
     mix_cross, lse_cross = attend(cross_q, cross_k, cross_v, heads_local, None, None)
-    resid_two = resid_one + branch_sum(product(mix_cross, cross_out))
+    resid_two = resid_one + tensor_sum(product(mix_cross, cross_out))
     normed_ff = rms_norm(resid_two, gain_ff).astype(jnp.bfloat16)
     gate_pre = product(normed_ff, ff_gate)
     up_pre = product(normed_ff, ff_up)
     activ, gelu_pull = jax.vjp(gelu_tanh, gate_pre)
     hidden = (activ * up_pre).astype(jnp.bfloat16)
-    ff_share = lax.psum_scatter(product(hidden, ff_down), "tensor", scatter_dimension=1, tiled=True)
+    grad_out = output_grad.astype(jnp.float32)
+    d_hidden = product_right(output_grad, ff_down)
+    d_gate_pre = gelu_pull(d_hidden * up_pre)[0].astype(jnp.bfloat16)
+    d_up_pre = (d_hidden * activ).astype(jnp.bfloat16)
+    d_normed_ff = tensor_sum(product_right(d_gate_pre, ff_gate) + product_right(d_up_pre, ff_up))
+    ff_share = column_scatter(product(hidden, ff_down))
     col_width = ff_share.shape[1]
     resid_cols = lax.dynamic_slice_in_dim(
         resid_two, lax.axis_index("tensor") * col_width, col_width, 1
     )
     layer_output = (resid_cols + ff_share).astype(jnp.bfloat16)
-    grad_out = output_grad.astype(jnp.float32)
-    d_ff_down = product_left(hidden, output_grad)
-    d_hidden = product_right(output_grad, ff_down)
-    d_gate_pre = gelu_pull(d_hidden * up_pre)[0].astype(jnp.bfloat16)
-    d_up_pre = (d_hidden * activ).astype(jnp.bfloat16)
-    d_ff_gate = product_left(normed_ff, d_gate_pre)
-    d_ff_up = product_left(normed_ff, d_up_pre)
-    d_normed_ff = input_sum(product_right(d_gate_pre, ff_gate) + product_right(d_up_pre, ff_up))
+    down_rows = row_scatter(product_left(output_grad, hidden), False)
+    gate_rows = row_scatter(product_left(normed_ff, d_gate_pre))
+    up_rows = row_scatter(product_left(normed_ff, d_up_pre))
     d_resid, d_gain_ff = norm_back(resid_two, gain_ff, d_normed_ff)
     grad_two = grad_out + d_resid
     grad_two_b = grad_two.astype(jnp.bfloat16)
-    d_cross_out = product_left(mix_cross, grad_two_b)
     d_mix_cross = product_right(grad_two_b, cross_out).astype(jnp.bfloat16)
     d_cross_q, d_cross_k, d_cross_v, unused = attend_back(
         cross_q, cross_k, cross_v, mix_cross, d_mix_cross, lse_cross, heads_local, None, None
     )
-    d_cross_query = product_left(normed_cross, d_cross_q)
-    d_cross_key = product_left(encoder_states, d_cross_k)
-    d_cross_value = product_left(encoder_states, d_cross_v)
-    d_normed_cross = lax.psum(product_right(d_cross_q, cross_query), "tensor")
-    d_encoder_states = lax.psum_scatter(
-        product_right(d_cross_k, cross_key) + product_right(d_cross_v, cross_value),
-        "tensor",
-        scatter_dimension=1,
-        tiled=True,
+    d_normed_cross = tensor_sum(product_right(d_cross_q, cross_query))
+    cross_rows = row_scatter(
+        jnp.concatenate(
+            [
+                product_left(normed_cross, d_cross_q),
+                product_left(encoder_states, d_cross_k),
+                product_left(encoder_states, d_cross_v),
+                product_left(grad_two_b, mix_cross),
+            ],
+            axis=1,
+        )
+    )
+    d_encoder_states = column_scatter(
+        product_right(d_cross_k, cross_key) + product_right(d_cross_v, cross_value)
     )
     d_resid, d_gain_cross = norm_back(resid_one, gain_cross, d_normed_cross)
     grad_one = grad_two + d_resid
     grad_one_b = grad_one.astype(jnp.bfloat16)
-    d_self_out = product_left(mix_self, grad_one_b)
     d_mix_self = product_right(grad_one_b, self_out).astype(jnp.bfloat16)
     d_self_q, d_self_k, d_self_v, ds_self = attend_back(
         self_q, self_k, self_v, mix_self, d_mix_self, lse_self, heads_local, pos_bias, allowed
     )
-    by_offset = sum_diagonals(ds_self, row_count)
-    d_bias_table = lax.psum(jnp.dot(onehot.T, by_offset, precision=lax.Precision.HIGHEST), "dp")
-    d_self_query = product_left(normed_self, d_self_q)
-    d_self_key = product_left(normed_self, d_self_k)
-    d_self_value = product_left(normed_self, d_self_v)
-    d_normed_self = input_sum(
+    d_normed_self = tensor_sum(
         product_right(d_self_q, self_query)
         + product_right(d_self_k, self_key)
         + product_right(d_self_v, self_value)
     )
+    self_rows = row_scatter(
+        jnp.concatenate(
+            [
+                product_left(normed_self, d_self_q),
+                product_left(normed_self, d_self_k),
+                product_left(normed_self, d_self_v),
+                product_left(grad_one_b, mix_self),
+            ],
+            axis=1,
+        )
+    )
+    by_offset = sum_diagonals(ds_self, row_count)
+    d_bias = jnp.dot(onehot.T, by_offset, precision=lax.Precision.HIGHEST)
     d_resid, d_gain_self = norm_back(stream_in, gain_self, d_normed_self)
     d_layer_input = grad_one + d_resid
-    summed = (
-        lax.psum_scatter(d_gain_self, "dp", scatter_dimension=0, tiled=True),
-        lax.psum_scatter(d_self_query, "dp", scatter_dimension=0, tiled=True),
-        lax.psum_scatter(d_self_key, "dp", scatter_dimension=0, tiled=True),
-        lax.psum_scatter(d_self_value, "dp", scatter_dimension=0, tiled=True),
-        lax.psum_scatter(d_self_out, "dp", scatter_dimension=1, tiled=True),
-        lax.psum_scatter(d_gain_cross, "dp", scatter_dimension=0, tiled=True),
-        lax.psum_scatter(d_cross_query, "dp", scatter_dimension=0, tiled=True),
-        lax.psum_scatter(d_cross_key, "dp", scatter_dimension=0, tiled=True),
-        lax.psum_scatter(d_cross_value, "dp", scatter_dimension=0, tiled=True),
-        lax.psum_scatter(d_cross_out, "dp", scatter_dimension=1, tiled=True),
-        lax.psum_scatter(d_gain_ff, "dp", scatter_dimension=0, tiled=True),
-        lax.psum_scatter(d_ff_gate, "dp", scatter_dimension=0, tiled=True),
-        lax.psum_scatter(d_ff_up, "dp", scatter_dimension=0, tiled=True),
-        lax.psum_scatter(d_ff_down, "dp", scatter_dimension=1, tiled=True),
-    )
-    return (layer_output, d_layer_input, d_encoder_states, d_bias_table) + tuple(summed)
+    dp_count = lax.axis_size("dp")
+    small = jnp.concatenate(
+        [g.reshape(dp_count, -1) for g in (d_gain_self, d_gain_cross, d_gain_ff)]
+        + [jnp.broadcast_to(d_bias.reshape(1, -1), (dp_count, d_bias.size))],
+        axis=1,
+    )
+    small = scatter_sum(small, "dp", True)
+    share = gain_self.shape[0] // dp_count
+    d_bias_table = small[3 * share :].reshape(d_bias.shape)
+    width = self_query.shape[1]
+
+    def quarter(rows, i):
+        return rows[:, i * width : (i + 1) * width]
+
+    return (
+        layer_output,
+        d_layer_input,
+        d_encoder_states,
+        d_bias_table,
+        small[:share],
+        quarter(self_rows, 0),
+        quarter(self_rows, 1),
+        quarter(self_rows, 2),
+        jnp.transpose(quarter(self_rows, 3)),
+        small[share : 2 * share],
+        quarter(cross_rows, 0),
+        quarter(cross_rows, 1),
+        quarter(cross_rows, 2),
+        jnp.transpose(quarter(cross_rows, 3)),
+        small[2 * share : 3 * share],
+        gate_rows,
+        up_rows,
+        jnp.transpose(down_rows),
+    )
 
 
 def solution(mesh):

time: 1030 us -> 258 us (0.25)
  waiting for transfers between devices: 863 us -> 89.5 us
  blocking collectives: 37.8 us -> 0 us
  starting transfers between devices: 0.93 us -> 36.2 us
  matrix products: 52.5 us -> 28.4 us
  other arithmetic: 16.9 us -> 39.9 us
  local copies, waits for them, and re-layouts: 39.8 us -> 60.6 us
  between operations: 16 us -> 2.09 us
    reduce_scatter x8 -> x0, waiting for transfers between devices: 496 us -> none  [the longest x1 68.7 us: on_device(): lax.psum_scatter(d_ff_down, 'dp', scatter_dimension=1, tiled=True)]
    unnamed x23 -> x0, waiting for transfers between devices: 228 us -> none
    psum x5 -> x0, waiting for transfers between devices: 139 us -> none  [the longest x2 71 us: branch_sum(): return lax.psum(partial_rows, 'tensor')]
    ppermute x0 -> x37, waiting for transfers between devices: none -> 89.5 us  [the longest x22 60 us: scatter_blocks(): received = lax.ppermute(send, axis_name, swap_pairs(count, 2 ** bit))]
    psum x1 -> x0, blocking collectives: 37.8 us -> none  [on_device(): lax.psum(jnp.dot(onehot.T, by_offset, precision=lax.Precision.HIGHEST), '...]
    ppermute x0 -> x37, starting transfers between devices: none -> 36.2 us  [the longest x22 26.1 us: scatter_blocks(): received = lax.ppermute(send, axis_name, swap_pairs(count, 2 ** bit))]
    add x0 -> x25, other arithmetic: none -> 16.4 us  [the longest x15 10 us: scatter_blocks(): blocks = (keep + received).reshape((high * low,) + shape)]
    squeeze x0 -> x21, local copies, waits for them, and re-layouts: none -> 13.3 us  [scatter_blocks(): send = lax.dynamic_index_in_dim(view, 1 - mine, 1, keepdims=False)]
  transfers between devices with their start and end apart: 18 -> 37, of which waited for: 17 -> 17; matrix products, arithmetic and copies ran while one was open for 6% -> 35% of each run, Pallas kernels for 0% -> 0%
where the time goes in v1:
time: 258 us; the launch traced here: 257 us
  waiting for transfers between devices  89.5 us (35%)
  local copies, waits for them, and re-layouts  60.6 us (23%)
  other arithmetic  39.9 us (15%)
  starting transfers between devices  36.2 us (14%)
  matrix products  28.4 us (11%)
    ppermute x22, waiting for transfers between devices, scatter_blocks(): received = lax.ppermute(send, axis_name, swap_pairs(count, 2 ** bit))  60 us
    ppermute x5, waiting for transfers between devices, tensor_sum(): total = total + lax.ppermute(total, 'tensor', swap_pairs(count, stride))  26.7 us
    ppermute x22, starting transfers between devices, scatter_blocks(): received = lax.ppermute(send, axis_name, swap_pairs(count, 2 ** bit))  26.1 us
    squeeze x21, local copies, waits for them, and re-layouts, scatter_blocks(): send = lax.dynamic_index_in_dim(view, 1 - mine, 1, keepdims=False)  13.3 us
    unnamed x184, local copies, waits for them, and re-layouts  13.1 us
    dot_general x11, matrix products, product(): return jnp.dot(left, right, preferred_element_type=jnp.float32)  10.1 us
    add x15, other arithmetic, scatter_blocks(): blocks = (keep + received).reshape((high * low,) + shape)  10 us
    ppermute x5, starting transfers between devices, tensor_sum(): total = total + lax.ppermute(total, 'tensor', swap_pairs(count, stride))  8.37 us
  transfers between devices with their start and end apart: 37, of which 17 were waited for; matrix products, arithmetic and copies ran while one was open for 35% of the time, Pallas kernels for 0%

profile of v1, /device:TPU:0, one launch (start us, length us, event | category | flops | bytes accessed | tf_op | source)
XLA Modules:
  0.0 256.6 jit_solution(9569418571205535717)
XLA Ops:
  1.9 2.1 convolution_convert_fusion.14
  4.1 2.1 convolution_convert_fusion.13
  7.9 1.7 slice.105
  9.5 3.3 %reshape.301 = f32[3,256,511]{2,1,0:T(8,128)S(1)} reshape(f32[3,130816]{1,0:T(4,128)} %slice.105) | data formatting | bytes 3139584 | tf_op jit(solution)/shard_map/reshape | solution.py:63
  20.4 2.9 %collective-permute-start.1 = (f32[128,768]{1,0:T(8,128)S(1)}, f32[128,768]{1,0:T(8,128)S(1)}, u32[]{:S(2)}, u32[]{:S(2)}) collective-permute-start(f32[128,768]{1,0:T(8,128)S(1)} %dynamic-slice_add_fusion.5), channel_id=1, source_target_pairs={{0,2},{1,3},{2,0},{3,1},{4,6},{5,7},{6,4},{7,5},{8,10},{9,11},{10,... | collective-permute-start | bytes 1179656 | tf_op jit(solution)/shard_map/ppermute | solution.py:156
  23.3 9.4 %collective-permute-done.1 = f32[128,768]{1,0:T(8,128)S(1)} collective-permute-done((f32[128,768]{1,0:T(8,128)S(1)}, f32[128,768]{1,0:T(8,128)S(1)}, u32[]{:S(2)}, u32[]{:S(2)}) %collective-permute-start.1) | collective-permute-done | bytes 393248 | tf_op jit(solution)/shard_map/ppermute | solution.py:156
  41.8 1.8 collective-permute-start.4
  43.6 9.7 %collective-permute-done.4 = f32[128,768]{1,0:T(8,128)S(1)} collective-permute-done((f32[128,768]{1,0:T(8,128)S(1)}, f32[128,768]{1,0:T(8,128)S(1)}, u32[]{:S(2)}, u32[]{:S(2)}) %collective-permute-start.4) | collective-permute-done | bytes 393248 | tf_op jit(solution)/shard_map/ppermute | solution.py:156
  59.8 1.6 convolution_bitcast_fusion
  62.7 3.1 %copy.110 = f32[768,512]{1,0:T(8,128)} copy(f32[768,512]{0,1:T(8,128)} %convolution_bitcast_fusion) | data formatting | bytes 3145728 | tf_op jit(solution)/shard_map/dot_general | solution.py:25
  65.7 2.2 dynamic-slice_bitcast_fusion.2
  67.9 1.8 collective-permute-start.34
  72.2 1.5 collective-permute-start.31
  77.8 1.5 collective-permute-start.7
  80.7 6.3 %collective-permute-done.7 = f32[1,1,256,192]{3,2,1,0:T(8,128)S(1)} collective-permute-done((f32[1,1,256,192]{3,2,1,0:T(8,128)S(1)}, f32[1,1,256,192]{3,2,1,0:T(8,128)S(1)}, u32[]{:S(2)}, u32[]{:S(2)}) %collective-permute-start.7) | collective-permute-done | bytes 196640 | tf_op jit(solution)/shard_map/ppermute | solution.py:177
  89.8 3.0 %collective-permute-start.35 = (f32[1,2,96,512]{3,2,1,0:T(8,128)S(1)}, f32[1,2,96,512]{3,2,1,0:T(8,128)S(1)}, u32[]{:S(2)}, u32[]{:S(2)}) collective-permute-start(f32[1,2,96,512]{3,2,1,0:T(8,128)S(1)} %constant_dynamic-slice_fusion), channel_id=1, source_target_pairs={{0,16},{4,20},{8,24},{12,28},{16,0},{20,4},{24,8},{28,12},{1,17},{... | collective-permute-start | bytes 1179656 | tf_op jit(solution)/shard_map/ppermute | solution.py:177
  92.8 2.0 collective-permute-done.9
  98.1 11.0 %collective-permute-done.28 = f32[4,1,96,512]{3,2,0,1:T(8,128)} collective-permute-done((f32[4,1,96,512]{3,2,0,1:T(8,128)}, f32[4,1,96,512]{3,2,0,1:T(8,128)}, u32[]{:S(2)}, u32[]{:S(2)}) %collective-permute-start.28) | collective-permute-done | bytes 786464 | tf_op jit(solution)/shard_map/ppermute | solution.py:177
  116.4 1.5 collective-permute-start.36
  119.2 2.6 %collective-permute-start.33 = (f32[1,1,96,512]{3,2,1,0:T(8,128)}, f32[1,1,96,512]{3,2,1,0:T(8,128)}, u32[]{:S(2)}, u32[]{:S(2)}) collective-permute-start(f32[1,1,96,512]{3,2,1,0:T(8,128)} %constant_dynamic-slice_fusion.1), channel_id=1, source_target_pairs={{0,16},{4,20},{8,24},{12,28},{16,0},{20,4},{24,8},{28,12},{1,17},{... | collective-permute-start | bytes 589832 | tf_op jit(solution)/shard_map/ppermute | solution.py:177
  122.7 3.1 %collective-permute-done.29 = f32[2,1,96,512]{3,2,1,0:T(8,128)S(1)} collective-permute-done((f32[2,1,96,512]{3,2,1,0:T(8,128)S(1)}, f32[2,1,96,512]{3,2,1,0:T(8,128)S(1)}, u32[]{:S(2)}, u32[]{:S(2)}) %collective-permute-start.29) | collective-permute-done | bytes 393248 | tf_op jit(solution)/shard_map/ppermute | solution.py:177
  127.7 1.6 pad_maximum_fusion.1
  129.3 3.1 %copy.109 = f32[768,768]{1,0:T(8,128)} copy(f32[768,768]{0,1:T(8,128)} %pad_maximum_fusion.1) | data formatting | bytes 4718592 | tf_op jit(solution)/shard_map/concatenate | solution.py:275
  132.4 2.5 dynamic-slice_bitcast_fusion
  134.9 1.7 collective-permute-start.25
  140.3 2.3 constant_dynamic-slice_fusion.13
  142.6 2.0 copy.105
  144.6 2.0 copy.104
  147.1 1.7 add_bitcast_fusion.2
  148.8 1.8 add_bitcast_fusion.3
  151.6 1.6 collective-permute-start.12
  153.9 1.7 add_bitcast_fusion.4
  155.6 11.4 %collective-permute-done.18 = f32[1,1,256,192]{2,3,1,0:T(8,128)S(1)} collective-permute-done((f32[1,1,256,192]{2,3,1,0:T(8,128)S(1)}, f32[1,1,256,192]{2,3,1,0:T(8,128)S(1)}, u32[]{:S(2)}, u32[]{:S(2)}) %collective-permute-start.18) | collective-permute-done | bytes 196640 | tf_op jit(solution)/shard_map/ppermute | solution.py:177
  170.2 2.3 collective-permute-start.26
  183.3 3.0 %pad_maximum_fusion = f32[768,768]{0,1:T(8,128)} fusion(f32[768,192]{0,1:T(8,128)} %fusion.32, f32[768,192]{0,1:T(8,128)S(1)} %copy-done.26, f32[768,192]{0,1:T(8,128)} %fusion.57, f32[768,192]{0,1:T(8,128)} %fusion.55), kind=kLoop, calls=%fused_computation | loop fusion | flops 1769472 | bytes 4718592 | tf_op jit(solution)/shard_map/concatenate | solution.py:301
  186.3 3.1 %copy.108 = f32[768,768]{1,0:T(8,128)} copy(f32[768,768]{0,1:T(8,128)} %pad_maximum_fusion) | data formatting | bytes 4718592 | tf_op jit(solution)/shard_map/concatenate | solution.py:301
  189.4 2.4 dynamic-slice_bitcast_fusion.1
  192.7 3.3 %reshape.309 = f32[3,130816]{1,0:T(4,128)} reshape(f32[3,256,511]{2,1,0:T(8,128)S(1)} %concatenate.49.clone) | data formatting | bytes 3139584 | tf_op jit(solution)/shard_map/reshape | solution.py:72
  196.1 2.0 concatenate.50
  199.3 1.5 collective-permute-start.15
  204.8 5.5 %collective-permute-done.15 = f32[128,768]{1,0:T(8,128)S(1)} collective-permute-done((f32[128,768]{1,0:T(8,128)S(1)}, f32[128,768]{1,0:T(8,128)S(1)}, u32[]{:S(2)}, u32[]{:S(2)}) %collective-permute-start.15) | collective-permute-done | bytes 393248 | tf_op jit(solution)/shard_map/ppermute | solution.py:156
  210.5 6.9 %collective-permute-done.27 = f32[1,1,96,768]{3,2,0,1:T(8,128)S(1)} collective-permute-done((f32[1,1,96,768]{3,2,0,1:T(8,128)S(1)}, f32[1,1,96,768]{3,2,0,1:T(8,128)S(1)}, u32[]{:S(2)}, u32[]{:S(2)}) %collective-permute-start.27) | collective-permute-done | bytes 294944 | tf_op jit(solution)/shard_map/ppermute | solution.py:177
  220.3 1.8 bitcast_add_fusion.1
  226.5 2.4 collective-permute-done.19
  229.0 2.0 collective-permute-start.20
  232.1 5.9 %collective-permute-done.20 = f32[2,1,384]{2,1,0:T(1,128)S(1)} collective-permute-done((f32[2,1,384]{2,1,0:T(1,128)S(1)}, f32[2,1,384]{2,1,0:T(1,128)S(1)}, u32[]{:S(2)}, u32[]{:S(2)}) %collective-permute-start.20) | collective-permute-done | bytes 3104 | tf_op jit(solution)/shard_map/ppermute | solution.py:177
  240.2 2.1 collective-permute-start.24
  243.9 11.2 %collective-permute-done.24 = f32[1,1,96,768]{3,2,0,1:T(8,128)S(1)} collective-permute-done((f32[1,1,96,768]{3,2,0,1:T(8,128)S(1)}, f32[1,1,96,768]{3,2,0,1:T(8,128)S(1)}, u32[]{:S(2)}, u32[]{:S(2)}) %collective-permute-start.24) | collective-permute-done | bytes 294944 | tf_op jit(solution)/shard_map/ppermute | solution.py:177
  (377 shorter events, 91.6 us)
Async XLA Ops:
  0.7 57.6 %copy-start = (bf16[512,768]{1,0:T(8,128)(2,1)S(1)}, bf16[512,768]{1,0:T(8,128)(2,1)}, u32[]{:S(2)}) copy-start(bf16[512,768]{1,0:T(8,128)(2,1)} %param.39) | copy-start | bytes 2359300
  0.7 5.5 %copy-start.86 = (s32[256]{0:T(256)S(1)}, s32[256]{0:T(256)}, u32[]{:S(2)}) copy-start(s32[256]{0:T(256)} %param.24) | copy-start | bytes 3076
  0.7 5.5 %copy-start.85 = (bf16[32,3]{0,1:T(4,128)(2,1)S(1)}, bf16[32,3]{0,1:T(4,128)(2,1)}, u32[]{:S(2)}) copy-start(bf16[32,3]{0,1:T(4,128)(2,1)} %param.25) | copy-start | bytes 580
  17.3 16.6 %copy-start.14 = (bf16[256,768]{1,0:T(8,128)(2,1)S(1)}, bf16[256,768]{1,0:T(8,128)(2,1)}, u32[]{:S(2)}) copy-start(bf16[256,768]{1,0:T(8,128)(2,1)} %param.21) | copy-start | bytes 1179652
  17.3 2.0 collective-permute-start
  20.4 12.3 %collective-permute-start.1 = (f32[128,768]{1,0:T(8,128)S(1)}, f32[128,768]{1,0:T(8,128)S(1)}, u32[]{:S(2)}, u32[]{:S(2)}) collective-permute-start(f32[128,768]{1,0:T(8,128)S(1)} %dynamic-slice_add_fusion.5), channel_id=1, source_target_pairs={{0,2},{1,3},{2,0},{3,1},{4,6},{5,7},{6,4},{7,5},{8,10},{9,11},{10,... | collective-permute-start | bytes 1179656 | tf_op jit(solution)/shard_map/ppermute | solution.py:156
  33.8 2.7 %collective-permute-start.2 = (f32[128,768]{1,0:T(8,128)S(1)}, f32[128,768]{1,0:T(8,128)S(1)}, u32[]{:S(2)}, u32[]{:S(2)}) collective-permute-start(f32[128,768]{1,0:T(8,128)S(1)} %add.296), channel_id=1, source_target_pairs={{0,1},{1,0},{2,3},{3,2},{4,5},{5,4},{6,7},{7,6},{8,9},{9,8},{10,11... | collective-permute-start | bytes 1179656 | tf_op jit(solution)/shard_map/ppermute | solution.py:158
  39.8 1.9 collective-permute-start.3
  41.8 11.5 %collective-permute-start.4 = (f32[128,768]{1,0:T(8,128)S(1)}, f32[128,768]{1,0:T(8,128)S(1)}, u32[]{:S(2)}, u32[]{:S(2)}) collective-permute-start(f32[128,768]{1,0:T(8,128)S(1)} %dynamic-slice_add_fusion.4), channel_id=1, source_target_pairs={{0,2},{1,3},{2,0},{3,1},{4,6},{5,7},{6,4},{7,5},{8,10},{9,11},{10,... | collective-permute-start | bytes 1179656 | tf_op jit(solution)/shard_map/ppermute | solution.py:156
  53.3 2.7 %collective-permute-start.5 = (f32[128,768]{1,0:T(8,128)S(1)}, f32[128,768]{1,0:T(8,128)S(1)}, u32[]{:S(2)}, u32[]{:S(2)}) collective-permute-start(f32[128,768]{1,0:T(8,128)S(1)} %add.300), channel_id=1, source_target_pairs={{0,1},{1,0},{2,3},{3,2},{4,5},{5,4},{6,7},{7,6},{8,9},{9,8},{10,11... | collective-permute-start | bytes 1179656 | tf_op jit(solution)/shard_map/ppermute | solution.py:158
  67.9 20.4 %collective-permute-start.34 = (f32[2,2,96,512]{3,2,1,0:T(8,128)}, f32[2,2,96,512]{3,2,1,0:T(8,128)}, u32[]{:S(2)}, u32[]{:S(2)}) collective-permute-start(f32[2,2,96,512]{3,2,1,0:T(8,128)} %dynamic-slice_bitcast_fusion.2), channel_id=1, source_target_pairs={{0,8},{4,12},{8,0},{12,4},{16,24},{20,28},{24,16},{28,20},{1,9},{5... | collective-permute-start | bytes 2359304 | tf_op jit(solution)/shard_map/ppermute | solution.py:177
  72.2 23.9 %collective-permute-start.31 = (f32[4,1,96,512]{3,2,0,1:T(8,128)}, f32[4,1,96,512]{3,2,0,1:T(8,128)}, u32[]{:S(2)}, u32[]{:S(2)}) collective-permute-start(f32[4,1,96,512]{3,2,0,1:T(8,128)} %dynamic-slice_bitcast_fusion.3), channel_id=1, source_target_pairs={{0,4},{4,0},{8,12},{12,8},{16,20},{20,16},{24,28},{28,24},{1,5},{5... | collective-permute-start | bytes 2359304 | tf_op jit(solution)/shard_map/ppermute | solution.py:177
  74.6 4.7 %collective-permute-start.8 = (f32[128,768]{1,0:T(8,128)S(1)}, f32[128,768]{1,0:T(8,128)S(1)}, u32[]{:S(2)}, u32[]{:S(2)}) collective-permute-start(f32[128,768]{1,0:T(8,128)S(1)} %constant_dynamic-slice_fusion.16), channel_id=1, source_target_pairs={{0,1},{1,0},{2,3},{3,2},{4,5},{5,4},{6,7},{7,6},{8,9},{9,8},{10,11... | collective-permute-start | bytes 1179656 | tf_op jit(solution)/shard_map/ppermute | solution.py:151
  75.6 2.0 collective-permute-start.6
  77.1 31.9 %collective-permute-start.28 = (f32[4,1,96,512]{3,2,0,1:T(8,128)}, f32[4,1,96,512]{3,2,0,1:T(8,128)}, u32[]{:S(2)}, u32[]{:S(2)}) collective-permute-start(f32[4,1,96,512]{3,2,0,1:T(8,128)} %dynamic-slice_bitcast_fusion.4), channel_id=1, source_target_pairs={{0,4},{4,0},{8,12},{12,8},{16,20},{20,16},{24,28},{28,24},{1,5},{5... | collective-permute-start | bytes 2359304 | tf_op jit(solution)/shard_map/ppermute | solution.py:177
  77.8 9.2 %collective-permute-start.7 = (f32[1,1,256,192]{3,2,1,0:T(8,128)S(1)}, f32[1,1,256,192]{3,2,1,0:T(8,128)S(1)}, u32[]{:S(2)}, u32[]{:S(2)}) collective-permute-start(f32[1,1,256,192]{3,2,1,0:T(8,128)S(1)} %constant_dynamic-slice_fusion.17), channel_id=1, source_target_pairs={{0,2},{1,3},{2,0},{3,1},{4,6},{5,7},{6,4},{7,5},{8,10},{9,11},{10,... | collective-permute-start | bytes 589832 | tf_op jit(solution)/shard_map/ppermute | solution.py:177
  80.1 14.7 %collective-permute-start.9 = (f32[128,768]{1,0:T(8,128)}, f32[128,768]{1,0:T(8,128)}, u32[]{:S(2)}, u32[]{:S(2)}) collective-permute-start(f32[128,768]{1,0:T(8,128)} %dynamic-slice_add_fusion.3), channel_id=1, source_target_pairs={{0,2},{1,3},{2,0},{3,1},{4,6},{5,7},{6,4},{7,5},{8,10},{9,11},{10,... | collective-permute-start | bytes 1179656 | tf_op jit(solution)/shard_map/ppermute | solution.py:156
  89.8 6.4 %copy-start.11 = (f32[768,512]{1,0:T(8,128)S(1)}, f32[768,512]{1,0:T(8,128)}, u32[]{:S(2)}) copy-start(f32[768,512]{1,0:T(8,128)} %copy-done.10) | copy-start | bytes 4718596
  89.8 25.7 %collective-permute-start.35 = (f32[1,2,96,512]{3,2,1,0:T(8,128)S(1)}, f32[1,2,96,512]{3,2,1,0:T(8,128)S(1)}, u32[]{:S(2)}, u32[]{:S(2)}) collective-permute-start(f32[1,2,96,512]{3,2,1,0:T(8,128)S(1)} %constant_dynamic-slice_fusion), channel_id=1, source_target_pairs={{0,16},{4,20},{8,24},{12,28},{16,0},{20,4},{24,8},{28,12},{1,17},{... | collective-permute-start | bytes 1179656 | tf_op jit(solution)/shard_map/ppermute | solution.py:177
  96.0 13.1 %copy-start.13 = (f32[768,512]{1,0:T(8,128)S(1)}, f32[768,512]{1,0:T(8,128)}, u32[]{:S(2)}) copy-start(f32[768,512]{1,0:T(8,128)} %copy-done.12) | copy-start | bytes 4718596
  96.0 14.8 %collective-permute-start.10 = (f32[128,768]{1,0:T(8,128)S(1)}, f32[128,768]{1,0:T(8,128)S(1)}, u32[]{:S(2)}, u32[]{:S(2)}) collective-permute-start(f32[128,768]{1,0:T(8,128)S(1)} %add.315), channel_id=1, source_target_pairs={{0,1},{1,0},{2,3},{3,2},{4,5},{5,4},{6,7},{7,6},{8,9},{9,8},{10,11... | collective-permute-start | bytes 1179656 | tf_op jit(solution)/shard_map/ppermute | solution.py:158
  97.5 20.8 %collective-permute-start.32 = (f32[2,1,96,512]{3,2,1,0:T(8,128)S(1)}, f32[2,1,96,512]{3,2,1,0:T(8,128)S(1)}, u32[]{:S(2)}, u32[]{:S(2)}) collective-permute-start(f32[2,1,96,512]{3,2,1,0:T(8,128)S(1)} %dynamic-slice_bitcast_fusion.8), channel_id=1, source_target_pairs={{0,8},{4,12},{8,0},{12,4},{16,24},{20,28},{24,16},{28,20},{1,9},{5... | collective-permute-start | bytes 1179656 | tf_op jit(solution)/shard_map/ppermute | solution.py:177
  110.4 15.3 %collective-permute-start.29 = (f32[2,1,96,512]{3,2,1,0:T(8,128)S(1)}, f32[2,1,96,512]{3,2,1,0:T(8,128)S(1)}, u32[]{:S(2)}, u32[]{:S(2)}) collective-permute-start(f32[2,1,96,512]{3,2,1,0:T(8,128)S(1)} %dynamic-slice_bitcast_fusion.9), channel_id=1, source_target_pairs={{0,8},{4,12},{8,0},{12,4},{16,24},{20,28},{24,16},{28,20},{1,9},{5... | collective-permute-start | bytes 1179656 | tf_op jit(solution)/shard_map/ppermute | solution.py:177
  116.4 30.2 %collective-permute-start.36 = (f32[1,1,96,512]{3,2,1,0:T(8,128)}, f32[1,1,96,512]{3,2,1,0:T(8,128)}, u32[]{:S(2)}, u32[]{:S(2)}) collective-permute-start(f32[1,1,96,512]{3,2,1,0:T(8,128)} %constant_dynamic-slice_fusion.18), channel_id=1, source_target_pairs={{0,4},{4,0},{8,12},{12,8},{16,20},{20,16},{24,28},{28,24},{1,5},{5... | collective-permute-start | bytes 589832 | tf_op jit(solution)/shard_map/ppermute | solution.py:177
  119.2 29.7 %collective-permute-start.33 = (f32[1,1,96,512]{3,2,1,0:T(8,128)}, f32[1,1,96,512]{3,2,1,0:T(8,128)}, u32[]{:S(2)}, u32[]{:S(2)}) collective-permute-start(f32[1,1,96,512]{3,2,1,0:T(8,128)} %constant_dynamic-slice_fusion.1), channel_id=1, source_target_pairs={{0,16},{4,20},{8,24},{12,28},{16,0},{20,4},{24,8},{28,12},{1,17},{... | collective-permute-start | bytes 589832 | tf_op jit(solution)/shard_map/ppermute | solution.py:177
  122.3 5.1 %copy-start.53 = (bf16[3,64,256]{2,1,0:T(8,128)(2,1)}, bf16[3,64,256]{2,1,0:T(8,128)(2,1)S(1)}, u32[]{:S(2)}) copy-start(bf16[3,64,256]{2,1,0:T(8,128)(2,1)S(1)} %convolution_convert_fusion) | copy-start | bytes 294916
  126.6 27.3 %collective-permute-start.30 = (f32[1,1,96,512]{3,2,1,0:T(8,128)}, f32[1,1,96,512]{3,2,1,0:T(8,128)}, u32[]{:S(2)}, u32[]{:S(2)}) collective-permute-start(f32[1,1,96,512]{3,2,1,0:T(8,128)} %constant_dynamic-slice_fusion.2), channel_id=1, source_target_pairs={{0,16},{4,20},{8,24},{12,28},{16,0},{20,4},{24,8},{28,12},{1,17},{... | collective-permute-start | bytes 589832 | tf_op jit(solution)/shard_map/ppermute | solution.py:177
  134.9 33.0 %collective-permute-start.25 = (f32[4,1,96,768]{3,2,0,1:T(8,128)}, f32[4,1,96,768]{3,2,0,1:T(8,128)}, u32[]{:S(2)}, u32[]{:S(2)}) collective-permute-start(f32[4,1,96,768]{3,2,0,1:T(8,128)} %dynamic-slice_bitcast_fusion), channel_id=1, source_target_pairs={{0,4},{4,0},{8,12},{12,8},{16,20},{20,16},{24,28},{28,24},{1,5},{5... | collective-permute-start | bytes 3538952 | tf_op jit(solution)/shard_map/ppermute | solution.py:177
  137.4 13.2 %collective-permute-start.11 = (f32[128,768]{1,0:T(8,128)}, f32[128,768]{1,0:T(8,128)}, u32[]{:S(2)}, u32[]{:S(2)}) collective-permute-start(f32[128,768]{1,0:T(8,128)} %constant_dynamic-slice_fusion.15), channel_id=1, source_target_pairs={{0,1},{1,0},{2,3},{3,2},{4,5},{5,4},{6,7},{7,6},{8,9},{9,8},{10,11... | collective-permute-start | bytes 1179656 | tf_op jit(solution)/shard_map/ppermute | solution.py:151
  146.6 6.6 %copy-start.27 = (f32[2,1,1,256,192]{3,4,0,2,1:T(8,128)S(1)}, f32[2,1,1,256,192]{3,4,0,2,1:T(8,128)}, u32[]{:S(2)}) copy-start(f32[2,1,1,256,192]{3,4,0,2,1:T(8,128)} %copy.104) | copy-start | bytes 1179652
  146.6 6.6 %collective-permute-start.17 = (f32[2,1,256,192]{2,3,1,0:T(8,128)}, f32[2,1,256,192]{2,3,1,0:T(8,128)S(1)}, u32[]{:S(2)}, u32[]{:S(2)}) collective-permute-start(f32[2,1,256,192]{2,3,1,0:T(8,128)} %bitcast.290), channel_id=1, source_target_pairs={{0,1},{1,0},{2,3},{3,2},{4,5},{5,4},{6,7},{7,6},{8,9},{9,8},{10,11... | collective-permute-start | bytes 1179656 | tf_op jit(solution)/shard_map/ppermute | solution.py:177
  151.6 16.1 %collective-permute-start.12 = (f32[128,768]{1,0:T(8,128)S(1)}, f32[128,768]{1,0:T(8,128)S(1)}, u32[]{:S(2)}, u32[]{:S(2)}) collective-permute-start(f32[128,768]{1,0:T(8,128)S(1)} %dynamic-slice_add_fusion.2), channel_id=1, source_target_pairs={{0,2},{1,3},{2,0},{3,1},{4,6},{5,7},{6,4},{7,5},{8,10},{9,11},{10,... | collective-permute-start | bytes 1179656 | tf_op jit(solution)/shard_map/ppermute | solution.py:156
  153.3 14.6 %copy-start.9 = (f32[768,768]{1,0:T(8,128)S(1)}, f32[768,768]{1,0:T(8,128)}, u32[]{:S(2)}) copy-start(f32[768,768]{1,0:T(8,128)} %copy.109) | copy-start | bytes 7077892
  153.3 13.7 %collective-permute-start.18 = (f32[1,1,256,192]{2,3,1,0:T(8,128)S(1)}, f32[1,1,256,192]{2,3,1,0:T(8,128)S(1)}, u32[]{:S(2)}, u32[]{:S(2)}) collective-permute-start(f32[1,1,256,192]{2,3,1,0:T(8,128)S(1)} %constant_dynamic-slice_fusion.11), channel_id=1, source_target_pairs={{0,2},{1,3},{2,0},{3,1},{4,6},{5,7},{6,4},{7,5},{8,10},{9,11},{10,... | collective-permute-start | bytes 589832 | tf_op jit(solution)/shard_map/ppermute | solution.py:177
  167.8 4.7 %collective-permute-start.13 = (f32[128,768]{1,0:T(8,128)S(1)}, f32[128,768]{1,0:T(8,128)S(1)}, u32[]{:S(2)}, u32[]{:S(2)}) collective-permute-start(f32[128,768]{1,0:T(8,128)S(1)} %add.319), channel_id=1, source_target_pairs={{0,1},{1,0},{2,3},{3,2},{4,5},{5,4},{6,7},{7,6},{8,9},{9,8},{10,11... | collective-permute-start | bytes 1179656 | tf_op jit(solution)/shard_map/ppermute | solution.py:158
  170.2 30.6 %collective-permute-start.26 = (f32[2,1,96,768]{3,2,0,1:T(8,128)}, f32[2,1,96,768]{3,2,0,1:T(8,128)}, u32[]{:S(2)}, u32[]{:S(2)}) collective-permute-start(f32[2,1,96,768]{3,2,0,1:T(8,128)} %dynamic-slice_bitcast_fusion.5), channel_id=1, source_target_pairs={{0,8},{4,12},{8,0},{12,4},{16,24},{20,28},{24,16},{28,20},{1,9},{5... | collective-permute-start | bytes 1769480 | tf_op jit(solution)/shard_map/ppermute | solution.py:177
  181.6 16.5 %collective-permute-start.14 = (f32[128,768]{1,0:T(8,128)}, f32[128,768]{1,0:T(8,128)}, u32[]{:S(2)}, u32[]{:S(2)}) collective-permute-start(f32[128,768]{1,0:T(8,128)} %constant_dynamic-slice_fusion.14), channel_id=1, source_target_pairs={{0,1},{1,0},{2,3},{3,2},{4,5},{5,4},{6,7},{7,6},{8,9},{9,8},{10,11... | collective-permute-start | bytes 1179656 | tf_op jit(solution)/shard_map/ppermute | solution.py:151
  191.8 28.5 %collective-permute-start.22 = (f32[4,1,96,768]{3,2,0,1:T(8,128)}, f32[4,1,96,768]{3,2,0,1:T(8,128)}, u32[]{:S(2)}, u32[]{:S(2)}) collective-permute-start(f32[4,1,96,768]{3,2,0,1:T(8,128)} %dynamic-slice_bitcast_fusion.1), channel_id=1, source_target_pairs={{0,4},{4,0},{8,12},{12,8},{16,20},{20,16},{24,28},{28,24},{1,5},{5... | collective-permute-start | bytes 3538952 | tf_op jit(solution)/shard_map/ppermute | solution.py:177
  199.3 11.1 %collective-permute-start.15 = (f32[128,768]{1,0:T(8,128)S(1)}, f32[128,768]{1,0:T(8,128)S(1)}, u32[]{:S(2)}, u32[]{:S(2)}) collective-permute-start(f32[128,768]{1,0:T(8,128)S(1)} %dynamic-slice_add_fusion.1), channel_id=1, source_target_pairs={{0,2},{1,3},{2,0},{3,1},{4,6},{5,7},{6,4},{7,5},{8,10},{9,11},{10,... | collective-permute-start | bytes 1179656 | tf_op jit(solution)/shard_map/ppermute | solution.py:156
  202.0 15.4 %collective-permute-start.27 = (f32[1,1,96,768]{3,2,0,1:T(8,128)S(1)}, f32[1,1,96,768]{3,2,0,1:T(8,128)S(1)}, u32[]{:S(2)}, u32[]{:S(2)}) collective-permute-start(f32[1,1,96,768]{3,2,0,1:T(8,128)S(1)} %constant_dynamic-slice_fusion.3), channel_id=1, source_target_pairs={{0,16},{4,20},{8,24},{12,28},{16,0},{20,4},{24,8},{28,12},{1,17},{... | collective-permute-start | bytes 884744 | tf_op jit(solution)/shard_map/ppermute | solution.py:177
  210.4 12.5 %collective-permute-start.16 = (f32[128,768]{1,0:T(8,128)S(1)}, f32[128,768]{1,0:T(8,128)}, u32[]{:S(2)}, u32[]{:S(2)}) collective-permute-start(f32[128,768]{1,0:T(8,128)S(1)} %add.325), channel_id=1, source_target_pairs={{0,1},{1,0},{2,3},{3,2},{4,5},{5,4},{6,7},{7,6},{8,9},{9,8},{10,11... | collective-permute-start | bytes 1179656 | tf_op jit(solution)/shard_map/ppermute | solution.py:158
  222.9 8.1 %copy-start.4 = (f32[256,768]{1,0:T(8,128)S(1)}, f32[256,768]{1,0:T(8,128)}, u32[]{:S(2)}) copy-start(f32[256,768]{1,0:T(8,128)} %copy-done.3) | copy-start | bytes 2359300
  222.9 16.1 %collective-permute-start.23 = (f32[2,1,96,768]{3,2,0,1:T(8,128)}, f32[2,1,96,768]{3,2,0,1:T(8,128)}, u32[]{:S(2)}, u32[]{:S(2)}) collective-permute-start(f32[2,1,96,768]{3,2,0,1:T(8,128)} %dynamic-slice_bitcast_fusion.6), channel_id=1, source_target_pairs={{0,8},{4,12},{8,0},{12,4},{16,24},{20,28},{24,16},{28,20},{1,9},{5... | collective-permute-start | bytes 1769480 | tf_op jit(solution)/shard_map/ppermute | solution.py:177
  225.2 3.7 %collective-permute-start.19 = (f32[4,1,384]{2,1,0:T(1,128)S(1)}, f32[4,1,384]{2,1,0:T(1,128)S(1)}, u32[]{:S(2)}, u32[]{:S(2)}) collective-permute-start(f32[4,1,384]{2,1,0:T(1,128)S(1)} %fusion.46), channel_id=1, source_target_pairs={{0,4},{4,0},{8,12},{12,8},{16,20},{20,16},{24,28},{28,24},{1,5},{5... | collective-permute-start | bytes 18440 | tf_op jit(solution)/shard_map/ppermute | solution.py:177
  229.0 9.0 %collective-permute-start.20 = (f32[2,1,384]{2,1,0:T(1,128)S(1)}, f32[2,1,384]{2,1,0:T(1,128)S(1)}, u32[]{:S(2)}, u32[]{:S(2)}) collective-permute-start(f32[2,1,384]{2,1,0:T(1,128)S(1)} %fusion.49), channel_id=1, source_target_pairs={{0,8},{4,12},{8,0},{12,4},{16,24},{20,28},{24,16},{28,20},{1,9},{5... | collective-permute-start | bytes 9224 | tf_op jit(solution)/shard_map/ppermute | solution.py:177
  238.0 4.6 %collective-permute-start.21 = (f32[1,1,384]{2,1,0:T(1,128)S(1)}, f32[1,1,384]{2,1,0:T(1,128)S(1)}, u32[]{:S(2)}, u32[]{:S(2)}) collective-permute-start(f32[1,1,384]{2,1,0:T(1,128)S(1)} %constant_dynamic-slice_fusion.5), channel_id=1, source_target_pairs={{0,16},{4,20},{8,24},{12,28},{16,0},{20,4},{24,8},{28,12},{1,17},{... | collective-permute-start | bytes 4616 | tf_op jit(solution)/shard_map/ppermute | solution.py:177
  239.0 17.7 %copy-start.1 = (bf16[512,768]{1,0:T(8,128)(2,1)S(1)}, bf16[512,768]{1,0:T(8,128)(2,1)}, u32[]{:S(2)}) copy-start(bf16[512,768]{1,0:T(8,128)(2,1)} %param.39) | copy-start | bytes 2359300
  240.2 14.8 %collective-permute-start.24 = (f32[1,1,96,768]{3,2,0,1:T(8,128)S(1)}, f32[1,1,96,768]{3,2,0,1:T(8,128)S(1)}, u32[]{:S(2)}, u32[]{:S(2)}) collective-permute-start(f32[1,1,96,768]{3,2,0,1:T(8,128)S(1)} %constant_dynamic-slice_fusion.4), channel_id=1, source_target_pairs={{0,16},{4,20},{8,24},{12,28},{16,0},{20,4},{24,8},{28,12},{1,17},{... | collective-permute-start | bytes 884744 | tf_op jit(solution)/shard_map/ppermute | solution.py:177
  (77 other events, 151.8 us)

commit v2 on v0

v2 whole, which is shorter than its diff:
```python
import functools

import jax
import jax.numpy as jnp
from jax import lax
from jax.experimental import pallas as pl
from jax.experimental.pallas import tpu as pltpu
from jax.sharding import PartitionSpec as P

epsilon = 1e-06
masked_value = -1000000000.0
gelu_rate = 0.7978845608028654
gelu_cube = 0.044715
f32 = jnp.float32
bf16 = jnp.bfloat16


def product(left, right):
    return jnp.dot(left, right, preferred_element_type=f32)


def product_left(left, right):
    return lax.dot_general(left, right, (((0,), (0,)), ((), ())), preferred_element_type=f32)


def product_right(left, right):
    return lax.dot_general(left, right, (((1,), (1,)), ((), ())), preferred_element_type=f32)


def inverse_rms(values):
    return lax.rsqrt(jnp.mean(values * values, axis=-1, keepdims=True) + epsilon)


def norm_pull(values, gain_row, cotangent):
    scale = inverse_rms(values)
    weighted = cotangent * gain_row
    mean_part = jnp.mean(weighted * values, axis=-1, keepdims=True)
    d_values = scale * weighted - values * (scale * scale * scale * mean_part)
    d_gain = jnp.sum(cotangent * values * scale, axis=0, keepdims=True)
    return d_values, d_gain


def head_columns(values, head, width):
    return values[:, head * width : (head + 1) * width]


def split_halves(part_ref, send_ref, keep_ref, bit):
    half = keep_ref.shape[0]
    send_ref[...] = part_ref[pl.ds((1 - bit) * half, half), :]
    keep_ref[...] = part_ref[pl.ds(bit * half, half), :]


def join_halves(full_ref, own_ref, other_ref, bit):
    half = own_ref.shape[0]
    full_ref[pl.ds(bit * half, half), :] = own_ref[...]
    full_ref[pl.ds((1 - bit) * half, half), :] = other_ref[...]


def split_blocks(grad_ref, send_ref, keep_ref, bit):
    pairs, rows, unused = keep_ref.shape
    for pair in range(pairs):
        if rows % 8 == 0:
            start = 2 * pair * rows
            send_ref[pair] = grad_ref[pl.ds(pl.multiple_of(start + (1 - bit) * rows, 8), rows), :]
            keep_ref[pair] = grad_ref[pl.ds(pl.multiple_of(start + bit * rows, 8), rows), :]
        else:
            first = grad_ref[2 * pair * rows : (2 * pair + 1) * rows, :]
            second = grad_ref[(2 * pair + 1) * rows : (2 * pair + 2) * rows, :]
            send_ref[pair] = jnp.where(bit == 0, second, first)
            keep_ref[pair] = jnp.where(bit == 0, first, second)


def softmax_rows(scores):
    exp_scores = jnp.exp(scores - jnp.max(scores, axis=-1, keepdims=True))
    return exp_scores / jnp.sum(exp_scores, axis=-1, keepdims=True)


def self_forward(
    place, x_ref, gain, wq, wk, wv, wo, seg, back_buckets, table,
    normed_ref, qkv_ref, prob_ref, mix_ref, send_ref, keep_ref, part_ref,
):
    heads = table.shape[1]
    width = wq.shape[1]
    size = width // heads
    rows = x_ref.shape[0]
    x = x_ref[...].astype(f32)
    normed = (x * inverse_rms(x) * gain[...]).astype(bf16)
    normed_ref[...] = normed
    query = product(normed, wq[...]).astype(bf16)
    key_rows = product(normed, wk[...]).astype(bf16)
    values = product(normed, wv[...]).astype(bf16)
    qkv_ref[...] = jnp.concatenate([query, key_rows, values], axis=1)
    row_id = lax.broadcasted_iota(jnp.int32, (rows, rows), 0)
    col_id = lax.broadcasted_iota(jnp.int32, (rows, rows), 1)
    seg_row = seg[...]
    seg_col = jnp.sum(jnp.where(row_id == col_id, seg_row, 0), axis=1, keepdims=True)
    allowed = (row_id >= col_id) & (seg_col == seg_row)
    bucket_id = lax.broadcasted_iota(jnp.int32, (table.shape[0], rows), 0)
    hit = bucket_id == back_buckets[...]
    table_f = table[...].astype(f32)
    mixes = []
    for h in range(heads):
        pattern = jnp.sum(jnp.where(hit, table_f[:, h : h + 1], 0.0), axis=0, keepdims=True)
        bias = pltpu.roll(
            jnp.broadcast_to(pattern, (rows, rows)), 0, 1, stride=1, stride_axis=0
        )
        scores = product_right(head_columns(query, h, size), head_columns(key_rows, h, size))
        prob = softmax_rows(jnp.where(allowed, scores + bias, masked_value))
        prob_ref[h] = prob
        mixes.append(product(prob.astype(bf16), head_columns(values, h, size)))
    mix = jnp.concatenate(mixes, axis=1).astype(bf16)
    mix_ref[...] = mix
    part_ref[...] = product(mix, wo[...])
    split_halves(part_ref, send_ref, keep_ref, place[0])


def cross_forward(
    place, own, other, x_ref, gain, wq, wo, kv,
    resid_ref, normed_ref, query_ref, prob_ref, mix_ref, send_ref, keep_ref, part_ref, *, heads,
):
    width = wq.shape[1]
    size = width // heads
    join_halves(part_ref, own, other, place[0])
    resid = x_ref[...].astype(f32) + part_ref[...]
    resid_ref[...] = resid
    normed = (resid * inverse_rms(resid) * gain[...]).astype(bf16)
    normed_ref[...] = normed
    query = product(normed, wq[...]).astype(bf16)
    query_ref[...] = query
    mixes = []
    for h in range(heads):
        key_h = kv[:, h * size : (h + 1) * size]
        value_h = kv[:, width + h * size : width + (h + 1) * size]
        prob = softmax_rows(product_right(head_columns(query, h, size), key_h))
        prob_ref[h] = prob
        mixes.append(product(prob.astype(bf16), value_h))
    mix = jnp.concatenate(mixes, axis=1).astype(bf16)
    mix_ref[...] = mix
    part_ref[...] = product(mix, wo[...])
    split_halves(part_ref, send_ref, keep_ref, place[0])


def cross_key_value(enc, wk, wv, kv_ref):
    rows = enc[...]
    kv_ref[...] = jnp.concatenate(
        [product(rows, wk[...]).astype(bf16), product(rows, wv[...]).astype(bf16)], axis=1
    )


def ff_both(
    place, own, other, resid_one, gain, wg, wu, wd, out_grad,
    resid_ref, normed_ref, hidden_ref, d_pre_ref, send_ref, keep_ref, part_ref,
):
    join_halves(part_ref, own, other, place[0])
    resid = resid_one[...] + part_ref[...]
    resid_ref[...] = resid
    normed = (resid * inverse_rms(resid) * gain[...]).astype(bf16)
    normed_ref[...] = normed
    gate = product(normed, wg[...])
    up = product(normed, wu[...])
    d_hidden = product_right(out_grad[...], wd[...])
    square = gate * gate
    bend = jnp.tanh(gelu_rate * (gate + gelu_cube * (square * gate)))
    activ = 0.5 * gate * (1.0 + bend)
    slope = 0.5 * (1.0 + bend) + 0.5 * gate * (1.0 - bend * bend) * (
        gelu_rate * (1.0 + 3.0 * gelu_cube * square)
    )
    hidden_ref[...] = (activ * up).astype(bf16)
    d_gate = (d_hidden * up * slope).astype(bf16)
    d_up = (d_hidden * activ).astype(bf16)
    width = d_gate.shape[1]
    d_pre_ref[:, :width] = d_gate
    d_pre_ref[:, width:] = d_up
    part_ref[...] = product_right(d_gate, wg[...]) + product_right(d_up, wu[...])
    split_halves(part_ref, send_ref, keep_ref, place[0])


def column_pieces(part, send_ref, keep_ref, bit):
    pairs, unused, width = keep_ref.shape
    for pair in range(pairs):
        first = part[:, 2 * pair * width : (2 * pair + 1) * width]
        second = part[:, (2 * pair + 1) * width : (2 * pair + 2) * width]
        send_ref[pair] = jnp.where(bit == 0, second, first)
        keep_ref[pair] = jnp.where(bit == 0, first, second)


def ff_grads(
    place, normed, d_pre, hidden, out_grad, wd,
    send_ref, keep_ref, down_ref, out_send, out_keep, grad_ref,
):
    grad_ref[...] = product_left(normed[...], d_pre[...])
    split_blocks(grad_ref, send_ref, keep_ref, place[1])
    down = product_left(out_grad[...], hidden[...])
    blocks, rows, unused = down_ref.shape
    for block in range(blocks):
        down_ref[block] = down[block * rows : (block + 1) * rows, :]
    column_pieces(product(hidden[...], wd[...]), out_send, out_keep, place[0])


def cross_backward(
    place, own, other, resid_two, gain, out_grad, wo, wq, prob, query, kv, mix,
    grad_ref, grad_b_ref, d_gain_ref, d_mix_ref, d_score_ref, d_query_ref, send_ref, keep_ref,
    part_ref, *, heads,
):
    width = wq.shape[1]
    size = width // heads
    join_halves(part_ref, own, other, place[0])
    d_resid, d_gain = norm_pull(resid_two[...], gain[...], part_ref[...])
    d_gain_ref[...] = d_gain
    grad = out_grad[...].astype(f32) + d_resid
    grad_ref[...] = grad
    grad_b = grad.astype(bf16)
    grad_b_ref[...] = grad_b
    d_mix = product_right(grad_b, wo[...]).astype(bf16)
    d_mix_ref[...] = d_mix
    drift = d_mix.astype(f32) * mix[...].astype(f32)
    d_queries = []
    for h in range(heads):
        key_h = kv[:, h * size : (h + 1) * size]
        value_h = kv[:, width + h * size : width + (h + 1) * size]
        delta = jnp.sum(head_columns(drift, h, size), axis=1, keepdims=True)
        d_prob = product_right(head_columns(d_mix, h, size), value_h)
        d_score = (prob[h] * (d_prob - delta)).astype(bf16)
        d_score_ref[h] = d_score
        d_queries.append(product(d_score, key_h))
    d_query = jnp.concatenate(d_queries, axis=1).astype(bf16)
    d_query_ref[...] = d_query
    part_ref[...] = product_right(d_query, wq[...])
    split_halves(part_ref, send_ref, keep_ref, place[0])


def cross_grads(
    place, normed, enc, grad_b, mix, prob, query, d_mix, d_score, d_query, wk, wv,
    send_ref, keep_ref, enc_send, enc_keep, grad_ref, *, heads,
):
    width = wk.shape[1]
    size = width // heads
    d_keys = []
    d_values = []
    for h in range(heads):
        d_keys.append(product_left(d_score[h], query[:, h * size : (h + 1) * size]))
        d_values.append(product_left(prob[h].astype(bf16), d_mix[:, h * size : (h + 1) * size]))
    d_key = jnp.concatenate(d_keys, axis=1).astype(bf16)
    d_value = jnp.concatenate(d_values, axis=1).astype(bf16)
    column_pieces(
        product_right(d_key, wk[...]) + product_right(d_value, wv[...]),
        enc_send,
        enc_keep,
        place[0],
    )
    grad_ref[:, : 2 * width] = product_left(enc[...], jnp.concatenate([d_key, d_value], axis=1))
    grad_ref[:, 2 * width :] = jnp.concatenate(
        [product_left(normed[...], d_query[...]), product_left(grad_b[...], mix[...])], axis=1
    )
    split_blocks(grad_ref, send_ref, keep_ref, place[1])


def self_backward(
    place, own, other, resid_one, gain, grad_two, wo, wq, wk, wv, prob, qkv, mix,
    grad_ref, grad_b_ref, d_gain_ref, d_score_ref, d_qkv_ref, send_ref, keep_ref,
    part_ref, *, heads,
):
    width = wq.shape[1]
    size = width // heads
    join_halves(part_ref, own, other, place[0])
    d_resid, d_gain = norm_pull(resid_one[...], gain[...], part_ref[...])
    d_gain_ref[...] = d_gain
    grad = grad_two[...] + d_resid
    grad_ref[...] = grad
    grad_b = grad.astype(bf16)
    grad_b_ref[...] = grad_b
    d_mix = product_right(grad_b, wo[...]).astype(bf16)
    drift = d_mix.astype(f32) * mix[...].astype(f32)
    d_queries = []
    d_keys = []
    d_values = []
    for h in range(heads):
        query_h = qkv[:, h * size : (h + 1) * size]
        key_h = qkv[:, width + h * size : width + (h + 1) * size]
        value_h = qkv[:, 2 * width + h * size : 2 * width + (h + 1) * size]
        d_mix_h = head_columns(d_mix, h, size)
        delta = jnp.sum(head_columns(drift, h, size), axis=1, keepdims=True)
        prob_h = prob[h]
        d_score = prob_h * (product_right(d_mix_h, value_h) - delta)
        d_score_ref[h] = d_score
        d_score_b = d_score.astype(bf16)
        d_queries.append(product(d_score_b, key_h))
        d_keys.append(product_left(d_score_b, query_h))
        d_values.append(product_left(prob_h.astype(bf16), d_mix_h))
    d_query = jnp.concatenate(d_queries, axis=1).astype(bf16)
    d_key = jnp.concatenate(d_keys, axis=1).astype(bf16)
    d_value = jnp.concatenate(d_values, axis=1).astype(bf16)
    d_qkv_ref[...] = jnp.concatenate([d_query, d_key, d_value], axis=1)
    part_ref[...] = (
        product_right(d_query, wq[...])
        + product_right(d_key, wk[...])
        + product_right(d_value, wv[...])
    )
    split_halves(part_ref, send_ref, keep_ref, place[0])


def shift_left_by_row(values):
    rows, columns = values.shape
    row_id = lax.broadcasted_iota(jnp.int32, values.shape, 0)
    step = 1
    while step < rows:
        rolled = pltpu.roll(values, columns - step, 1)
        values = jnp.where(row_id & step != 0, rolled, values)
        step *= 2
    return values


def self_grads(
    place, normed, grad_b, mix, d_qkv, d_score, back_buckets,
    send_ref, keep_ref, d_bias_ref, grad_ref, *, heads,
):
    grad_ref[...] = jnp.concatenate(
        [product_left(normed[...], d_qkv[...]), product_left(grad_b[...], mix[...])], axis=1
    )
    split_blocks(grad_ref, send_ref, keep_ref, place[1])
    bucket_id = lax.broadcasted_iota(
        jnp.int32, (d_bias_ref.shape[0], back_buckets.shape[1]), 0
    )
    hit = bucket_id == back_buckets[...]
    for h in range(heads):
        by_offset = jnp.sum(shift_left_by_row(d_score[h]), axis=0, keepdims=True)
        d_bias_ref[:, h : h + 1] = jnp.sum(
            jnp.where(hit, by_offset, 0.0), axis=1, keepdims=True
        )


def input_grad(place, own, other, x_ref, gain, grad_one, d_input_ref, d_gain_ref, part_ref):
    join_halves(part_ref, own, other, place[0])
    d_resid, d_gain = norm_pull(x_ref[...].astype(f32), gain[...], part_ref[...])
    d_gain_ref[...] = d_gain
    d_input_ref[...] = grad_one[...] + d_resid


def kernel_call(body, outs, scratch, *operands, **static):
    if static:
        body = functools.partial(body, **static)
    specs = [
        pl.BlockSpec(memory_space=pltpu.SMEM if operand.ndim == 1 else pltpu.VMEM)
        for operand in operands
    ]
    return pl.pallas_call(
        body,
        out_shape=[jax.ShapeDtypeStruct(shape, dtype) for shape, dtype in outs],
        in_specs=specs,
        out_specs=[pl.BlockSpec(memory_space=pltpu.VMEM) for unused in outs],
        scratch_shapes=[pltpu.VMEM(shape, f32) for shape in scratch],
    )(*operands)


def swap_pairs(count, stride):
    return [(i, i ^ stride) for i in range(count)]


def swap_halves(send, keep):
    count = lax.axis_size("tensor")
    total = keep + lax.ppermute(send, "tensor", swap_pairs(count, 1))
    stride = 2
    while stride < count:
        total = total + lax.ppermute(total, "tensor", swap_pairs(count, stride))
        stride *= 2
    return total, lax.ppermute(total, "tensor", swap_pairs(count, 1))


def halve_blocks(blocks, axis_name, bits, remaining):
    count = lax.axis_size(axis_name)
    index = lax.axis_index(axis_name)
    remaining = list(remaining)
    shape = blocks.shape[1:]
    for bit in bits:
        low = 2 ** remaining.index(bit)
        high = 2 ** (len(remaining) - 1 - remaining.index(bit))
        mine = (index >> bit) & 1
        view = blocks.reshape((high, 2, low) + shape)
        keep = lax.dynamic_index_in_dim(view, mine, 1, keepdims=False)
        send = lax.dynamic_index_in_dim(view, 1 - mine, 1, keepdims=False)
        received = lax.ppermute(send, axis_name, swap_pairs(count, 2**bit))
        blocks = (keep + received).reshape((high * low,) + shape)
        remaining.remove(bit)
    return blocks[0]


def bit_list(axis_name):
    return list(range(lax.axis_size(axis_name).bit_length() - 1))


def finish_blocks(send, keep, axis_name):
    bits = bit_list(axis_name)
    count = lax.axis_size(axis_name)
    blocks = keep + lax.ppermute(send, axis_name, swap_pairs(count, 1))
    return halve_blocks(blocks, axis_name, bits[1:], bits[1:])


def on_device(
    layer_input,
    encoder_states,
    output_grad,
    segments,
    buckets,
    bias_table,
    gain_self,
    self_query,
    self_key,
    self_value,
    self_out,
    gain_cross,
    cross_query,
    cross_key,
    cross_value,
    cross_out,
    gain_ff,
    ff_gate,
    ff_up,
    ff_down,
):
    rows, model = layer_input.shape
    heads = bias_table.shape[1]
    width = self_query.shape[1]
    hidden_width = ff_gate.shape[1]
    dp_count = lax.axis_size("dp")
    share = model // dp_count
    tensor_count = lax.axis_size("tensor")
    place = jnp.stack([lax.axis_index("tensor") & 1, lax.axis_index("dp") & 1]).astype(jnp.int32)
    back_buckets = jnp.roll(jnp.flip(buckets), 1).reshape(1, rows)
    gain_a = gain_self.reshape(1, model)
    gain_b = gain_cross.reshape(1, model)
    gain_c = gain_ff.reshape(1, model)
    full = (rows, model)
    half = ((rows // 2, model), f32)
    probs = (heads, rows, rows)
    pieces = ((tensor_count // 2, rows, model // tensor_count), f32)

    normed_self, qkv, prob_self, mix_self, send, keep = kernel_call(
        self_forward,
        [(full, bf16), ((rows, 3 * width), bf16), (probs, f32), ((rows, width), bf16), half, half],
        [full],
        place, layer_input, gain_a, self_query, self_key, self_value, self_out,
        segments, back_buckets, bias_table,
    )
    own, other = swap_halves(send, keep)
    (kv,) = kernel_call(
        cross_key_value,
        [((rows, 2 * width), bf16)],
        [],
        encoder_states, cross_key, cross_value,
    )
    resid_one, normed_cross, query, prob_cross, mix_cross, send, keep = kernel_call(
        cross_forward,
        [(full, f32), (full, bf16), ((rows, width), bf16), (probs, f32), ((rows, width), bf16),
         half, half],
        [full],
        place, own, other, layer_input, gain_b, cross_query, cross_out, kv,
        heads=heads,
    )
    own, other = swap_halves(send, keep)
    resid_two, normed_ff, hidden, d_pre, send, keep = kernel_call(
        ff_both,
        [(full, f32), (full, bf16), ((rows, hidden_width), bf16), ((rows, 2 * hidden_width), bf16),
         half, half],
        [full],
        place, own, other, resid_one, gain_c, ff_gate, ff_up, ff_down, output_grad,
    )
    own, other = swap_halves(send, keep)
    split = (dp_count // 2, share)
    pre_send, pre_keep, down_blocks, out_send, out_keep = kernel_call(
        ff_grads,
        [(split + (2 * hidden_width,), f32), (split + (2 * hidden_width,), f32),
         ((dp_count, share, hidden_width), f32), pieces, pieces],
        [(model, 2 * hidden_width)],
        place, normed_ff, d_pre, hidden, output_grad, ff_down,
    )
    (grad_two, grad_two_b, d_gain_ff, d_mix, d_score, d_query, send, keep) = kernel_call(
        cross_backward,
        [(full, f32), (full, bf16), ((1, model), f32), ((rows, width), bf16), (probs, bf16),
         ((rows, width), bf16), half, half],
        [full],
        place, own, other, resid_two, gain_c, output_grad, cross_out, cross_query,
        prob_cross, query, kv, mix_cross,
        heads=heads,
    )
    own, other = swap_halves(send, keep)
    cross_send, cross_keep, enc_send, enc_keep = kernel_call(
        cross_grads,
        [(split + (4 * width,), f32), (split + (4 * width,), f32), pieces, pieces],
        [(model, 4 * width)],
        place, normed_cross, encoder_states, grad_two_b, mix_cross, prob_cross, query, d_mix,
        d_score, d_query, cross_key, cross_value,
        heads=heads,
    )
    grad_one, grad_one_b, d_gain_cross, d_score_self, d_qkv, send, keep = kernel_call(
        self_backward,
        [(full, f32), (full, bf16), ((1, model), f32), (probs, f32), ((rows, 3 * width), bf16),
         half, half],
        [full],
        place, own, other, resid_one, gain_b, grad_two, self_out, self_query, self_key,
        self_value, prob_self, qkv, mix_self,
        heads=heads,
    )
    own, other = swap_halves(send, keep)
    self_send, self_keep, d_bias = kernel_call(
        self_grads,
        [(split + (4 * width,), f32), (split + (4 * width,), f32), (bias_table.shape, f32)],
        [(model, 4 * width)],
        place, normed_self, grad_one_b, mix_self, d_qkv, d_score_self, back_buckets,
        heads=heads,
    )
    d_layer_input, d_gain_self = kernel_call(
        input_grad,
        [(full, f32), ((1, model), f32)],
        [full],
        place, own, other, layer_input, gain_a, grad_one,
    )

    out_share = finish_blocks(out_send, out_keep, "tensor")
    col_width = out_share.shape[1]
    resid_cols = lax.dynamic_slice_in_dim(
        resid_two, lax.axis_index("tensor") * col_width, col_width, 1
    )
    layer_output = (resid_cols + out_share).astype(bf16)
    d_encoder_states = finish_blocks(enc_send, enc_keep, "tensor")
    dp_bits = bit_list("dp")
    down_rows = halve_blocks(down_blocks, "dp", dp_bits[1:] + dp_bits[:1], dp_bits)
    pre_rows = finish_blocks(pre_send, pre_keep, "dp")
    cross_rows = finish_blocks(cross_send, cross_keep, "dp")
    self_rows = finish_blocks(self_send, self_keep, "dp")
    small = jnp.concatenate(
        [g.reshape(dp_count, share) for g in (d_gain_self, d_gain_cross, d_gain_ff)]
        + [jnp.broadcast_to(d_bias.reshape(1, d_bias.size), (dp_count, d_bias.size))],
        axis=1,
    )
    small = halve_blocks(small, "dp", dp_bits, dp_bits)
    return (
        layer_output,
        d_layer_input,
        d_encoder_states,
        small[3 * share :].reshape(d_bias.shape),
        small[:share],
        self_rows[:, :width],
        self_rows[:, width : 2 * width],
        self_rows[:, 2 * width : 3 * width],
        jnp.transpose(self_rows[:, 3 * width :]),
        small[share : 2 * share],
        cross_rows[:, 2 * width : 3 * width],
        cross_rows[:, :width],
        cross_rows[:, width : 2 * width],
        jnp.transpose(cross_rows[:, 3 * width :]),
        small[2 * share : 3 * share],
        pre_rows[:, :hidden_width],
        pre_rows[:, hidden_width:],
        jnp.transpose(down_rows),
    )


def solution(mesh):
    in_specs = (
        P("dp", None),
        P("dp", None),
        P("dp", None),
        P("dp", None),
        P(),
        P(None, "tensor"),
        P(),
        P(None, "tensor"),
        P(None, "tensor"),
        P(None, "tensor"),
        P("tensor", None),
        P(),
        P(None, "tensor"),
        P(None, "tensor"),
        P(None, "tensor"),
        P("tensor", None),
        P(),
        P(None, "tensor"),
        P(None, "tensor"),
        P("tensor", None),
    )
    out_specs = (
        P("dp", "tensor"),
        P("dp", None),
        P("dp", "tensor"),
        P(None, "tensor"),
        P("dp"),
        P("dp", "tensor"),
        P("dp", "tensor"),
        P("dp", "tensor"),
        P("tensor", "dp"),
        P("dp"),
        P("dp", "tensor"),
        P("dp", "tensor"),
        P("dp", "tensor"),
        P("tensor", "dp"),
        P("dp"),
        P("dp", "tensor"),
        P("dp", "tensor"),
        P("tensor", "dp"),
    )
    return jax.shard_map(
        on_device, mesh=mesh, in_specs=in_specs, out_specs=out_specs, check_vma=False
    )
```

time: 1030 us -> 234 us (0.23)
  waiting for transfers between devices: 863 us -> 94.5 us
  matrix products: 52.5 us -> 0 us
  Pallas kernels: 0 us -> 43.9 us
  blocking collectives: 37.8 us -> 0 us
  starting transfers between devices: 0.93 us -> 36.9 us
  between operations: 16 us -> 1.17 us
    reduce_scatter x8 -> x0, waiting for transfers between devices: 496 us -> none  [the longest x1 68.7 us: on_device(): lax.psum_scatter(d_ff_down, 'dp', scatter_dimension=1, tiled=True)]
    unnamed x23 -> x0, waiting for transfers between devices: 228 us -> none
    psum x5 -> x0, waiting for transfers between devices: 139 us -> none  [the longest x2 71 us: branch_sum(): return lax.psum(partial_rows, 'tensor')]
    ppermute x0 -> x34, waiting for transfers between devices: none -> 94.5 us  [the longest x14 57.8 us: halve_blocks(): received = lax.ppermute(send, axis_name, swap_pairs(count, 2 ** bit))]
    dot_general x44 -> x0, matrix products: 45.4 us -> none  [the longest x9 16.9 us: product_left(): lax.dot_general(left, right, (((0,), (0,)), ((), ())), preferred_element_...]
    pallas_call x0 -> x10, Pallas kernels: none -> 43.9 us  [kernel_call(): pl.pallas_call(body, out_shape=[jax.ShapeDtypeStruct(shape, dtype) for sh...]
    psum x1 -> x0, blocking collectives: 37.8 us -> none  [on_device(): lax.psum(jnp.dot(onehot.T, by_offset, precision=lax.Precision.HIGHEST), '...]
    ppermute x0 -> x34, starting transfers between devices: none -> 36.9 us  [the longest x14 22.3 us: halve_blocks(): received = lax.ppermute(send, axis_name, swap_pairs(count, 2 ** bit))]
  transfers between devices with their start and end apart: 18 -> 34, of which waited for: 17 -> 17; matrix products, arithmetic and copies ran while one was open for 6% -> 15% of each run, Pallas kernels for 0% -> 12%
where the time goes in v2:
time: 234 us; the launch traced here: 233 us
  waiting for transfers between devices  94.5 us (40%)
  Pallas kernels  43.9 us (19%)
  starting transfers between devices  36.9 us (16%)
  local copies, waits for them, and re-layouts  33.4 us (14%)
  other arithmetic  23.5 us (10%)
    ppermute x14, waiting for transfers between devices, halve_blocks(): received = lax.ppermute(send, axis_name, swap_pairs(count, 2 ** bit))  57.8 us
    pallas_call x10, Pallas kernels, kernel_call(): pl.pallas_call(body, out_shape=[jax.ShapeDtypeStruct(shape, dtype) for sh...  43.9 us
    ppermute x5, waiting for transfers between devices, swap_halves(): total = total + lax.ppermute(total, 'tensor', swap_pairs(count, stride))  30.9 us
    ppermute x14, starting transfers between devices, halve_blocks(): received = lax.ppermute(send, axis_name, swap_pairs(count, 2 ** bit))  22.3 us
    unnamed x70, local copies, waits for them, and re-layouts  17.5 us
    ppermute x5, starting transfers between devices, swap_halves(): total = total + lax.ppermute(total, 'tensor', swap_pairs(count, stride))  8.49 us
    add x5, other arithmetic, finish_blocks(): blocks = keep + lax.ppermute(send, axis_name, swap_pairs(count, 1))  7.08 us
    squeeze x12, local copies, waits for them, and re-layouts, halve_blocks(): send = lax.dynamic_index_in_dim(view, 1 - mine, 1, keepdims=False)  5.6 us
  transfers between devices with their start and end apart: 34, of which 17 were waited for; matrix products, arithmetic and copies ran while one was open for 15% of the time, Pallas kernels for 12%

profile of v2, /device:TPU:0, one launch (start us, length us, event | category | flops | bytes accessed | tf_op | source)
XLA Modules:
  0.0 233.4 jit_solution(14090526858479880266)
XLA Ops:
  5.5 1.9 copy.90.wq
  7.3 1.9 copy.91.wk
  12.0 4.4 %shard_map.331 = (bf16[256,768]{1,0:T(8,128)(2,1)}, bf16[256,576]{1,0:T(8,128)(2,1)}, f32[3,256,256]{2,1,0:T(8,128)}, bf16[256,192]{1,0:T(8,128)(2,1)}, f32[128,768]{1,0:T(8,128)}, /*index=5*/f32[128,768]{1,0:T(8,128)}) custom-call(s32[2]{0:T(128)} %pad_add_fusion.1.place, bf16[256,768]{1,0:T(8,128)(2,1)} %x_ref.5, f32[1,768]{1,0:T(1,128)} %reshape.120.gain, ...), custom_call_target="tpu_custom_call" | custom-call | tf_op jit(solution)/shard_map/pallas_call | solution.py:346
  16.9 1.6 collective-permute-done
  19.6 2.9 %collective-permute-start.1 = (f32[128,768]{1,0:T(8,128)S(1)}, f32[128,768]{1,0:T(8,128)S(1)}, u32[]{:S(2)}, u32[]{:S(2)}) collective-permute-start(f32[128,768]{1,0:T(8,128)S(1)} %add.152), channel_id=1, source_target_pairs={{0,2},{1,3},{2,0},{3,1},{4,6},{5,7},{6,4},{7,5},{8,10},{9,11},{10,... | collective-permute-start | bytes 1179656 | tf_op jit(solution)/shard_map/ppermute | solution.py:364
  22.5 9.4 %collective-permute-done.1 = f32[128,768]{1,0:T(8,128)S(1)} collective-permute-done((f32[128,768]{1,0:T(8,128)S(1)}, f32[128,768]{1,0:T(8,128)S(1)}, u32[]{:S(2)}, u32[]{:S(2)}) %collective-permute-start.1) | collective-permute-done | bytes 393248 | tf_op jit(solution)/shard_map/ppermute | solution.py:364
  35.5 2.3 %shard_map.332.kv = bf16[256,384]{1,0:T(8,128)(2,1)} custom-call(bf16[256,768]{1,0:T(8,128)(2,1)} %enc.3, bf16[768,192]{1,0:T(8,128)(2,1)} %copy.94.wk, bf16[768,192]{1,0:T(8,128)(2,1)} %copy.95.wv), custom_call_target="tpu_custom_call" | custom-call | tf_op jit(solution)/shard_map/pallas_call | solution.py:346
  38.6 4.3 %shard_map.333 = (f32[256,768]{1,0:T(8,128)}, bf16[256,768]{1,0:T(8,128)(2,1)}, bf16[256,192]{1,0:T(8,128)(2,1)}, f32[3,256,256]{2,1,0:T(8,128)}, bf16[256,192]{...) custom-call(s32[2]{0:T(128)} %pad_add_fusion.1.place, f32[128,768]{1,0:T(8,128)} %copy-done.3, ...), custom_call_target="tpu_custom_call" | custom-call | tf_op jit(solution)/shard_map/pallas_call | solution.py:346
  43.3 1.6 collective-permute-done.3
  46.0 1.8 collective-permute-start.4
  47.8 9.7 %collective-permute-done.4 = f32[128,768]{1,0:T(8,128)S(1)} collective-permute-done((f32[128,768]{1,0:T(8,128)S(1)}, f32[128,768]{1,0:T(8,128)S(1)}, u32[]{:S(2)}, u32[]{:S(2)}) %collective-permute-start.4) | collective-permute-done | bytes 393248 | tf_op jit(solution)/shard_map/ppermute | solution.py:364
  60.0 4.8 %shard_map.334 = (f32[256,768]{1,0:T(8,128)}, bf16[256,768]{1,0:T(8,128)(2,1)}, bf16[256,512]{1,0:T(8,128)(2,1)}, bf16[256,1024]{1,0:T(8,128)(2,1)}, f32[128,768]{1,0:T(8,128)}, /*index=5*/f32[128,768]{1,0:T(8,128)}) custom-call(s32[2]{0:T(128)} %pad_add_fusion.1.place, f32[128,768]{1,0:T(8,128)} %copy-done.2, f32[128,768]{1,0:T(8,128)} %copy-done.13, ...), custom_call_target="tpu_custom_call" | custom-call | tf_op jit(solution)/shard_map/pallas_call | solution.py:346
  64.9 4.9 %shard_map.335 = (f32[4,96,1024]{2,1,0:T(8,128)}, f32[4,96,1024]{2,1,0:T(8,128)}, f32[8,96,512]{2,1,0:T(8,128)}, f32[2,256,192]{2,1,0:T(8,128)}, f32[2,256,192]{2,1,0:T(8,128)}) custom-call(s32[2]{0:T(128)} %pad_add_fusion.1.place, bf16[256,768]{1,0:T(8,128)(2,1)} %get-tuple-element.72.normed, bf16[256,1024]{1,0:T(8,128)(2,1)} %get-tuple-element.73.d_pre, ...), custom_call_target="tpu_custom_call" | custom-call | tf_op jit(solution)/shard_map/pallas_call | solution.py:346
  69.8 2.1 dynamic-slice_bitcast_fusion
  71.9 1.8 collective-permute-start.31
  73.8 1.5 collective-permute-start.28
  75.3 1.6 collective-permute-start.9
  76.9 9.3 %collective-permute-done.9 = f32[128,768]{1,0:T(8,128)S(1)} collective-permute-done((f32[128,768]{1,0:T(8,128)S(1)}, f32[128,768]{1,0:T(8,128)S(1)}, u32[]{:S(2)}, u32[]{:S(2)}) %collective-permute-start.9) | collective-permute-done | bytes 393248 | tf_op jit(solution)/shard_map/ppermute | solution.py:364
  86.4 5.7 %collective-permute-done.31 = f32[2,2,96,512]{3,2,1,0:T(8,128)S(1)} collective-permute-done((f32[2,2,96,512]{3,2,1,0:T(8,128)}, f32[2,2,96,512]{3,2,1,0:T(8,128)S(1)}, u32[]{:S(2)}, u32[]{:S(2)}) %collective-permute-start.31) | collective-permute-done | bytes 786464 | tf_op jit(solution)/shard_map/ppermute | solution.py:381
  92.3 2.8 %collective-permute-start.32 = (f32[1,2,96,512]{3,2,1,0:T(8,128)S(1)}, f32[1,2,96,512]{3,2,1,0:T(8,128)S(1)}, u32[]{:S(2)}, u32[]{:S(2)}) collective-permute-start(f32[1,2,96,512]{3,2,1,0:T(8,128)S(1)} %constant_dynamic-slice_fusion.1), channel_id=1, source_target_pairs={{0,16},{4,20},{8,24},{12,28},{16,0},{20,4},{24,8},{28,12},{1,17},{... | collective-permute-start | bytes 1179656 | tf_op jit(solution)/shard_map/ppermute | solution.py:381
  95.8 4.3 %shard_map.336 = (f32[256,768]{1,0:T(8,128)}, bf16[256,768]{1,0:T(8,128)(2,1)}, f32[1,768]{1,0:T(1,128)}, bf16[256,192]{1,0:T(8,128)(2,1)}, bf16[3,256,256]{2,1,...) custom-call(s32[2]{0:T(128)} %pad_add_fusion.1.place, f32[128,768]{1,0:T(8,128)} %copy-done.1, ...), custom_call_target="tpu_custom_call" | custom-call | tf_op jit(solution)/shard_map/pallas_call | solution.py:346
  101.3 5.5 %shard_map.339 = (f32[4,96,768]{2,1,0:T(8,128)}, f32[4,96,768]{2,1,0:T(8,128)}, f32[2,256,192]{2,1,0:T(8,128)}, f32[2,256,192]{2,1,0:T(8,128)}) custom-call(s32[2]{0:T(128)} %pad_add_fusion.1.place, bf16[256,768]{1,0:T(8,128)(2,1)} %get-tuple-element.92.normed, bf16[256,768]{1,0:T(8,128)(2,1)} %enc.3, bf16[256,768]{1,0:T(8,128)(2,1)} %get-tuple-element.93.grad_b, ...), custom_call_target="tpu_custom_call" | custom-call | tf_op jit(solution)/shard_map/pallas_call | solution.py:346
  106.8 1.6 collective-permute-start.25
  108.4 1.7 collective-permute-start.7
  110.2 2.2 collective-permute-done.32
  114.3 1.6 collective-permute-start.12
  115.9 1.7 add.185
  119.9 1.5 collective-permute-start.33
  123.5 2.5 %collective-permute-done.12 = f32[128,768]{1,0:T(8,128)} collective-permute-done((f32[128,768]{1,0:T(8,128)S(1)}, f32[128,768]{1,0:T(8,128)}, u32[]{:S(2)}, u32[]{:S(2)}) %collective-permute-start.12) | collective-permute-done | bytes 393248 | tf_op jit(solution)/shard_map/ppermute | solution.py:364
  127.1 12.9 %collective-permute-done.33 = f32[1,1,96,512]{3,2,1,0:T(8,128)} collective-permute-done((f32[1,1,96,512]{3,2,1,0:T(8,128)}, f32[1,1,96,512]{3,2,1,0:T(8,128)}, u32[]{:S(2)}, u32[]{:S(2)}) %collective-permute-start.33) | collective-permute-done | bytes 196640 | tf_op jit(solution)/shard_map/ppermute | solution.py:381
  140.0 1.6 add_bitcast_fusion.3
  145.9 1.8 add.182
  150.6 5.2 %shard_map.337 = (f32[256,768]{1,0:T(8,128)}, bf16[256,768]{1,0:T(8,128)(2,1)}, f32[1,768]{1,0:T(1,128)}, f32[3,256,256]{2,1,0:T(8,128)}, bf16[256,576]{1,0:T(8,...) custom-call(s32[2]{0:T(128)} %pad_add_fusion.1.place, f32[128,768]{1,0:T(8,128)} %copy-done.6, f32[128,768]{1,0:T(8,128)} %copy-done.19, ...), custom_call_target="tpu_custom_call" | custom-call | tf_op jit(solution)/shard_map/pallas_call | solution.py:346
  157.8 1.7 collective-permute-start.30
  159.5 5.4 %shard_map.340 = (f32[4,96,768]{2,1,0:T(8,128)}, f32[4,96,768]{2,1,0:T(8,128)}, f32[32,3]{1,0:T(8,128)}) custom-call(s32[2]{0:T(128)} %pad_add_fusion.1.place, bf16[256,768]{1,0:T(8,128)(2,1)} %get-tuple-element.102.normed, bf16[256,768]{1,0:T(8,128)(2,1)} %get-tuple-element.103.grad_b, bf16[256,192]{1,0:T(8,128)(2,1)} %get-tuple-element.87.mix, ...), custom_call_target="tpu_custom_call" | custom-call | tf_op jit(solution)/shard_map/pallas_call | solution.py:346
  164.9 1.5 collective-permute-start.22
  166.4 1.6 fusion.1
  173.3 12.5 %collective-permute-done.30 = f32[1,1,96,1024]{3,2,1,0:T(8,128)} collective-permute-done((f32[1,1,96,1024]{3,2,1,0:T(8,128)}, f32[1,1,96,1024]{3,2,1,0:T(8,128)}, u32[]{:S(2)}, u32[]{:S(2)}) %collective-permute-start.30) | collective-permute-done | bytes 393248 | tf_op jit(solution)/shard_map/ppermute | solution.py:381
  187.8 3.8 %collective-permute-done.27 = f32[1,1,96,768]{3,2,1,0:T(8,128)S(1)} collective-permute-done((f32[1,1,96,768]{3,2,1,0:T(8,128)S(1)}, f32[1,1,96,768]{3,2,1,0:T(8,128)S(1)}, u32[]{:S(2)}, u32[]{:S(2)}) %collective-permute-start.27) | collective-permute-done | bytes 294944 | tf_op jit(solution)/shard_map/ppermute | solution.py:381
  191.6 1.6 collective-permute-done.22
  196.4 2.8 %shard_map.338 = (f32[256,768]{1,0:T(8,128)}, f32[1,768]{1,0:T(1,128)}) custom-call(s32[2]{0:T(128)} %pad_add_fusion.1.place, f32[128,768]{1,0:T(8,128)} %copy-done.5, f32[128,768]{1,0:T(8,128)} %copy-done.18, bf16[256,768]{1,0:T(8,128)(2,1)} %x_ref.5, f32[1,768]{1,0:T(1,128)} %reshape.120.gain, f32[256,768]{1,0:T(8,128)} %get-tuple-element.90.grad_one), custom_call_target="tpu_custom_call" | custom-call | tf_op jit(solution)/shard_map/pallas_call | solution.py:346
  200.1 1.6 collective-permute-start.19
  201.7 1.6 collective-permute-start.23
  203.8 1.6 collective-permute-start.20
  207.0 9.2 %collective-permute-done.20 = f32[2,1,384]{2,1,0:T(1,128)S(1)} collective-permute-done((f32[2,1,384]{2,1,0:T(1,128)S(1)}, f32[2,1,384]{2,1,0:T(1,128)S(1)}, u32[]{:S(2)}, u32[]{:S(2)}) %collective-permute-start.20) | collective-permute-done | bytes 3104 | tf_op jit(solution)/shard_map/ppermute | solution.py:381
  217.6 1.7 collective-permute-start.24
  219.4 6.7 %collective-permute-done.21 = f32[1,1,384]{2,1,0:T(1,128)S(1)} collective-permute-done((f32[1,1,384]{2,1,0:T(1,128)S(1)}, f32[1,1,384]{2,1,0:T(1,128)S(1)}, u32[]{:S(2)}, u32[]{:S(2)}) %collective-permute-start.21) | collective-permute-done | bytes 1568 | tf_op jit(solution)/shard_map/ppermute | solution.py:381
  227.4 4.4 %collective-permute-done.24 = f32[1,1,96,768]{3,2,1,0:T(8,128)S(1)} collective-permute-done((f32[1,1,96,768]{3,2,1,0:T(8,128)S(1)}, f32[1,1,96,768]{3,2,1,0:T(8,128)S(1)}, u32[]{:S(2)}, u32[]{:S(2)}) %collective-permute-start.24) | collective-permute-done | bytes 294944 | tf_op jit(solution)/shard_map/ppermute | solution.py:381
  (167 shorter events, 54.1 us)
Async XLA Ops:
  0.7 8.6 %copy-start.20 = (bf16[768,192]{0,1:T(8,128)(2,1)S(1)}, bf16[768,192]{0,1:T(8,128)(2,1)}, u32[]{:S(2)}) copy-start(bf16[768,192]{0,1:T(8,128)(2,1)} %param.29) | copy-start | bytes 884740
  16.4 2.1 collective-permute-start
  18.5 13.6 %copy-start.24 = (f32[768]{0:T(1024)S(1)}, f32[768]{0:T(1024)}, u32[]{:S(2)}) copy-start(f32[768]{0:T(1024)} %param.31) | copy-start | bytes 9220
  18.5 14.2 %copy-start.21 = (bf16[768,192]{0,1:T(8,128)(2,1)S(1)}, bf16[768,192]{0,1:T(8,128)(2,1)}, u32[]{:S(2)}) copy-start(bf16[768,192]{0,1:T(8,128)(2,1)} %param.32) | copy-start | bytes 884740
  19.6 14.1 %copy-start.22 = (bf16[768,192]{0,1:T(8,128)(2,1)S(1)}, bf16[768,192]{0,1:T(8,128)(2,1)}, u32[]{:S(2)}) copy-start(bf16[768,192]{0,1:T(8,128)(2,1)} %param.33) | copy-start | bytes 884740
  19.6 15.0 %copy-start.23 = (bf16[768,192]{0,1:T(8,128)(2,1)S(1)}, bf16[768,192]{0,1:T(8,128)(2,1)}, u32[]{:S(2)}) copy-start(bf16[768,192]{0,1:T(8,128)(2,1)} %param.34) | copy-start | bytes 884740
  19.6 12.3 %collective-permute-start.1 = (f32[128,768]{1,0:T(8,128)S(1)}, f32[128,768]{1,0:T(8,128)S(1)}, u32[]{:S(2)}, u32[]{:S(2)}) collective-permute-start(f32[128,768]{1,0:T(8,128)S(1)} %add.152), channel_id=1, source_target_pairs={{0,2},{1,3},{2,0},{3,1},{4,6},{5,7},{6,4},{7,5},{8,10},{9,11},{10,... | collective-permute-start | bytes 1179656 | tf_op jit(solution)/shard_map/ppermute | solution.py:364
  32.0 5.8 %collective-permute-start.2 = (f32[128,768]{1,0:T(8,128)S(1)}, f32[128,768]{1,0:T(8,128)S(1)}, u32[]{:S(2)}, u32[]{:S(2)}) collective-permute-start(f32[128,768]{1,0:T(8,128)S(1)} %add.153.own), channel_id=1, source_target_pairs={{0,1},{1,0},{2,3},{3,2},{4,5},{5,4},{6,7},{7,6},{8,9},{9,8},{10,11... | collective-permute-start | bytes 1179656 | tf_op jit(solution)/shard_map/ppermute | solution.py:366
  42.9 2.0 collective-permute-start.3
  44.9 12.7 %copy-start.25 = (f32[768]{0:T(1024)S(1)}, f32[768]{0:T(1024)}, u32[]{:S(2)}) copy-start(f32[768]{0:T(1024)} %param.36) | copy-start | bytes 9220
  46.0 11.5 %collective-permute-start.4 = (f32[128,768]{1,0:T(8,128)S(1)}, f32[128,768]{1,0:T(8,128)S(1)}, u32[]{:S(2)}, u32[]{:S(2)}) collective-permute-start(f32[128,768]{1,0:T(8,128)S(1)} %add.154), channel_id=1, source_target_pairs={{0,2},{1,3},{2,0},{3,1},{4,6},{5,7},{6,4},{7,5},{8,10},{9,11},{10,... | collective-permute-start | bytes 1179656 | tf_op jit(solution)/shard_map/ppermute | solution.py:364
  57.5 1.8 collective-permute-start.5
  64.8 10.5 %collective-permute-start.8 = (f32[128,768]{1,0:T(8,128)}, f32[128,768]{1,0:T(8,128)S(1)}, u32[]{:S(2)}, u32[]{:S(2)}) collective-permute-start(f32[128,768]{1,0:T(8,128)} %get-tuple-element.78), channel_id=1, source_target_pairs={{0,1},{1,0},{2,3},{3,2},{4,5},{5,4},{6,7},{7,6},{8,9},{9,8},{10,11... | collective-permute-start | bytes 1179656 | tf_op jit(solution)/shard_map/ppermute | solution.py:361
  71.9 20.1 %collective-permute-start.31 = (f32[2,2,96,512]{3,2,1,0:T(8,128)}, f32[2,2,96,512]{3,2,1,0:T(8,128)S(1)}, u32[]{:S(2)}, u32[]{:S(2)}) collective-permute-start(f32[2,2,96,512]{3,2,1,0:T(8,128)} %dynamic-slice_bitcast_fusion), channel_id=1, source_target_pairs={{0,8},{4,12},{8,0},{12,4},{16,24},{20,28},{24,16},{28,20},{1,9},{5... | collective-permute-start | bytes 2359304 | tf_op jit(solution)/shard_map/ppermute | solution.py:381
  73.8 42.1 %collective-permute-start.28 = (f32[4,96,1024]{2,1,0:T(8,128)}, f32[4,96,1024]{2,1,0:T(8,128)}, u32[]{:S(2)}, u32[]{:S(2)}) collective-permute-start(f32[4,96,1024]{2,1,0:T(8,128)} %get-tuple-element.112), channel_id=1, source_target_pairs={{0,4},{4,0},{8,12},{12,8},{16,20},{20,16},{24,28},{28,24},{1,5},{5... | collective-permute-start | bytes 4718600 | tf_op jit(solution)/shard_map/ppermute | solution.py:394
  75.3 16.8 %copy-start = (f32[8,96,512]{2,1,0:T(8,128)S(1)}, f32[8,96,512]{2,1,0:T(8,128)}, u32[]{:S(2)}) copy-start(f32[8,96,512]{2,1,0:T(8,128)} %get-tuple-element.113) | copy-start | bytes 4718596
  75.3 10.9 %collective-permute-start.9 = (f32[128,768]{1,0:T(8,128)S(1)}, f32[128,768]{1,0:T(8,128)S(1)}, u32[]{:S(2)}, u32[]{:S(2)}) collective-permute-start(f32[128,768]{1,0:T(8,128)S(1)} %add.162), channel_id=1, source_target_pairs={{0,2},{1,3},{2,0},{3,1},{4,6},{5,7},{6,4},{7,5},{8,10},{9,11},{10,... | collective-permute-start | bytes 1179656 | tf_op jit(solution)/shard_map/ppermute | solution.py:364
  76.9 23.3 %collective-permute-start.6 = (f32[2,256,192]{2,1,0:T(8,128)}, f32[2,256,192]{2,1,0:T(8,128)}, u32[]{:S(2)}, u32[]{:S(2)}) collective-permute-start(f32[2,256,192]{2,1,0:T(8,128)} %get-tuple-element.76), channel_id=1, source_target_pairs={{0,1},{1,0},{2,3},{3,2},{4,5},{5,4},{6,7},{7,6},{8,9},{9,8},{10,11... | collective-permute-start | bytes 1179656 | tf_op jit(solution)/shard_map/ppermute | solution.py:394
  86.3 8.8 %collective-permute-start.10 = (f32[128,768]{1,0:T(8,128)S(1)}, f32[128,768]{1,0:T(8,128)S(1)}, u32[]{:S(2)}, u32[]{:S(2)}) collective-permute-start(f32[128,768]{1,0:T(8,128)S(1)} %add.163.own), channel_id=1, source_target_pairs={{0,1},{1,0},{2,3},{3,2},{4,5},{5,4},{6,7},{7,6},{8,9},{9,8},{10,11... | collective-permute-start | bytes 1179656 | tf_op jit(solution)/shard_map/ppermute | solution.py:366
  92.3 20.1 %collective-permute-start.32 = (f32[1,2,96,512]{3,2,1,0:T(8,128)S(1)}, f32[1,2,96,512]{3,2,1,0:T(8,128)S(1)}, u32[]{:S(2)}, u32[]{:S(2)}) collective-permute-start(f32[1,2,96,512]{3,2,1,0:T(8,128)S(1)} %constant_dynamic-slice_fusion.1), channel_id=1, source_target_pairs={{0,16},{4,20},{8,24},{12,28},{16,0},{20,4},{24,8},{28,12},{1,17},{... | collective-permute-start | bytes 1179656 | tf_op jit(solution)/shard_map/ppermute | solution.py:381
  100.2 12.3 %collective-permute-start.11 = (f32[128,768]{1,0:T(8,128)}, f32[128,768]{1,0:T(8,128)S(1)}, u32[]{:S(2)}, u32[]{:S(2)}) collective-permute-start(f32[128,768]{1,0:T(8,128)} %get-tuple-element.83), channel_id=1, source_target_pairs={{0,1},{1,0},{2,3},{3,2},{4,5},{5,4},{6,7},{7,6},{8,9},{9,8},{10,11... | collective-permute-start | bytes 1179656 | tf_op jit(solution)/shard_map/ppermute | solution.py:361
  106.8 6.4 %copy-start.15 = (f32[128,768]{1,0:T(8,128)S(1)}, f32[128,768]{1,0:T(8,128)}, u32[]{:S(2)}) copy-start(f32[128,768]{1,0:T(8,128)} %get-tuple-element.82) | copy-start | bytes 1179652
  106.8 39.1 %collective-permute-start.25 = (f32[4,96,768]{2,1,0:T(8,128)}, f32[4,96,768]{2,1,0:T(8,128)}, u32[]{:S(2)}, u32[]{:S(2)}) collective-permute-start(f32[4,96,768]{2,1,0:T(8,128)} %get-tuple-element.110), channel_id=1, source_target_pairs={{0,4},{4,0},{8,12},{12,8},{16,20},{20,16},{24,28},{28,24},{1,5},{5... | collective-permute-start | bytes 3538952 | tf_op jit(solution)/shard_map/ppermute | solution.py:394
  108.4 11.5 %collective-permute-start.7 = (f32[1,1,256,192]{3,2,1,0:T(8,128)S(1)}, f32[1,1,256,192]{3,2,1,0:T(8,128)S(1)}, u32[]{:S(2)}, u32[]{:S(2)}) collective-permute-start(f32[1,1,256,192]{3,2,1,0:T(8,128)S(1)} %dynamic-slice_bitcast_fusion.4), channel_id=1, source_target_pairs={{0,2},{1,3},{2,0},{3,1},{4,6},{5,7},{6,4},{7,5},{8,10},{9,11},{10,... | collective-permute-start | bytes 589832 | tf_op jit(solution)/shard_map/ppermute | solution.py:381
  112.4 29.2 %collective-permute-start.17 = (f32[2,256,192]{2,1,0:T(8,128)}, f32[2,256,192]{2,1,0:T(8,128)}, u32[]{:S(2)}, u32[]{:S(2)}) collective-permute-start(f32[2,256,192]{2,1,0:T(8,128)} %get-tuple-element.98), channel_id=1, source_target_pairs={{0,1},{1,0},{2,3},{3,2},{4,5},{5,4},{6,7},{7,6},{8,9},{9,8},{10,11... | collective-permute-start | bytes 1179656 | tf_op jit(solution)/shard_map/ppermute | solution.py:394
  114.3 11.7 %collective-permute-start.12 = (f32[128,768]{1,0:T(8,128)S(1)}, f32[128,768]{1,0:T(8,128)}, u32[]{:S(2)}, u32[]{:S(2)}) collective-permute-start(f32[128,768]{1,0:T(8,128)S(1)} %add.164), channel_id=1, source_target_pairs={{0,2},{1,3},{2,0},{3,1},{4,6},{5,7},{6,4},{7,5},{8,10},{9,11},{10,... | collective-permute-start | bytes 1179656 | tf_op jit(solution)/shard_map/ppermute | solution.py:364
  118.6 37.3 %collective-permute-start.29 = (f32[2,1,96,1024]{3,2,1,0:T(8,128)}, f32[2,1,96,1024]{3,2,1,0:T(8,128)}, u32[]{:S(2)}, u32[]{:S(2)}) collective-permute-start(f32[2,1,96,1024]{3,2,1,0:T(8,128)} %dynamic-slice_bitcast_fusion.1), channel_id=1, source_target_pairs={{0,8},{4,12},{8,0},{12,4},{16,24},{20,28},{24,16},{28,20},{1,9},{5... | collective-permute-start | bytes 2359304 | tf_op jit(solution)/shard_map/ppermute | solution.py:381
  119.9 20.0 %collective-permute-start.33 = (f32[1,1,96,512]{3,2,1,0:T(8,128)}, f32[1,1,96,512]{3,2,1,0:T(8,128)}, u32[]{:S(2)}, u32[]{:S(2)}) collective-permute-start(f32[1,1,96,512]{3,2,1,0:T(8,128)} %constant_dynamic-slice_fusion), channel_id=1, source_target_pairs={{0,4},{4,0},{8,12},{12,8},{16,20},{20,16},{24,28},{28,24},{1,5},{5... | collective-permute-start | bytes 589832 | tf_op jit(solution)/shard_map/ppermute | solution.py:381
  122.6 19.0 %copy-start.11 = (f32[2,256,192]{2,1,0:T(8,128)S(1)}, f32[2,256,192]{2,1,0:T(8,128)}, u32[]{:S(2)}) copy-start(f32[2,256,192]{2,1,0:T(8,128)} %get-tuple-element.97) | copy-start | bytes 1179652
  127.0 15.8 %copy-start.6 = (f32[128,768]{1,0:T(8,128)}, f32[128,768]{1,0:T(8,128)S(1)}, u32[]{:S(2)}) copy-start(f32[128,768]{1,0:T(8,128)S(1)} %add.165.own) | copy-start | bytes 1179652
  127.0 22.8 %collective-permute-start.13 = (f32[128,768]{1,0:T(8,128)S(1)}, f32[128,768]{1,0:T(8,128)S(1)}, u32[]{:S(2)}, u32[]{:S(2)}) collective-permute-start(f32[128,768]{1,0:T(8,128)S(1)} %add.165.own), channel_id=1, source_target_pairs={{0,1},{1,0},{2,3},{3,2},{4,5},{5,4},{6,7},{7,6},{8,9},{9,8},{10,11... | collective-permute-start | bytes 1179656 | tf_op jit(solution)/shard_map/ppermute | solution.py:366
  144.4 22.0 %collective-permute-start.18 = (f32[1,1,256,192]{2,3,1,0:T(8,128)}, f32[1,1,256,192]{2,3,1,0:T(8,128)}, u32[]{:S(2)}, u32[]{:S(2)}) collective-permute-start(f32[1,1,256,192]{2,3,1,0:T(8,128)} %bitcast.7), channel_id=1, source_target_pairs={{0,2},{1,3},{2,0},{3,1},{4,6},{5,7},{6,4},{7,5},{8,10},{9,11},{10,... | collective-permute-start | bytes 589832 | tf_op jit(solution)/shard_map/ppermute | solution.py:381
  148.5 22.3 %collective-permute-start.26 = (f32[2,1,96,768]{3,2,1,0:T(8,128)}, f32[2,1,96,768]{3,2,1,0:T(8,128)}, u32[]{:S(2)}, u32[]{:S(2)}) collective-permute-start(f32[2,1,96,768]{3,2,1,0:T(8,128)} %dynamic-slice_bitcast_fusion.2), channel_id=1, source_target_pairs={{0,8},{4,12},{8,0},{12,4},{16,24},{20,28},{24,16},{28,20},{1,9},{5... | collective-permute-start | bytes 1769480 | tf_op jit(solution)/shard_map/ppermute | solution.py:381
  155.8 13.2 %collective-permute-start.14 = (f32[128,768]{1,0:T(8,128)}, f32[128,768]{1,0:T(8,128)}, u32[]{:S(2)}, u32[]{:S(2)}) collective-permute-start(f32[128,768]{1,0:T(8,128)} %get-tuple-element.89), channel_id=1, source_target_pairs={{0,1},{1,0},{2,3},{3,2},{4,5},{5,4},{6,7},{7,6},{8,9},{9,8},{10,11... | collective-permute-start | bytes 1179656 | tf_op jit(solution)/shard_map/ppermute | solution.py:361
  157.8 8.6 %copy-start.9 = (f32[1,256,192]{1,2,0:T(8,128)S(1)}, f32[1,256,192]{1,2,0:T(8,128)}, u32[]{:S(2)}) copy-start(f32[1,256,192]{1,2,0:T(8,128)} %copy.103) | copy-start | bytes 589828
  157.8 27.9 %collective-permute-start.30 = (f32[1,1,96,1024]{3,2,1,0:T(8,128)}, f32[1,1,96,1024]{3,2,1,0:T(8,128)}, u32[]{:S(2)}, u32[]{:S(2)}) collective-permute-start(f32[1,1,96,1024]{3,2,1,0:T(8,128)} %constant_dynamic-slice_fusion.2), channel_id=1, source_target_pairs={{0,16},{4,20},{8,24},{12,28},{16,0},{20,4},{24,8},{28,12},{1,17},{... | collective-permute-start | bytes 1179656 | tf_op jit(solution)/shard_map/ppermute | solution.py:381
  159.5 8.5 %copy-start.27 = (f32[1,768]{1,0:T(1,128)S(1)}, f32[1,768]{1,0:T(1,128)}, u32[]{:S(2)}) copy-start(f32[1,768]{1,0:T(1,128)} %get-tuple-element.100) | copy-start | bytes 9220
  164.9 28.3 %collective-permute-start.22 = (f32[4,96,768]{2,1,0:T(8,128)}, f32[4,96,768]{2,1,0:T(8,128)S(1)}, u32[]{:S(2)}, u32[]{:S(2)}) collective-permute-start(f32[4,96,768]{2,1,0:T(8,128)} %get-tuple-element.108), channel_id=1, source_target_pairs={{0,4},{4,0},{8,12},{12,8},{16,20},{20,16},{24,28},{28,24},{1,5},{5... | collective-permute-start | bytes 3538952 | tf_op jit(solution)/shard_map/ppermute | solution.py:394
  170.2 16.7 %collective-permute-start.15 = (f32[128,768]{1,0:T(8,128)S(1)}, f32[128,768]{1,0:T(8,128)S(1)}, u32[]{:S(2)}, u32[]{:S(2)}) collective-permute-start(f32[128,768]{1,0:T(8,128)S(1)} %add.166), channel_id=1, source_target_pairs={{0,2},{1,3},{2,0},{3,1},{4,6},{5,7},{6,4},{7,5},{8,10},{9,11},{10,... | collective-permute-start | bytes 1179656 | tf_op jit(solution)/shard_map/ppermute | solution.py:364
  172.0 19.6 %collective-permute-start.27 = (f32[1,1,96,768]{3,2,1,0:T(8,128)S(1)}, f32[1,1,96,768]{3,2,1,0:T(8,128)S(1)}, u32[]{:S(2)}, u32[]{:S(2)}) collective-permute-start(f32[1,1,96,768]{3,2,1,0:T(8,128)S(1)} %constant_dynamic-slice_fusion.3), channel_id=1, source_target_pairs={{0,16},{4,20},{8,24},{12,28},{16,0},{20,4},{24,8},{28,12},{1,17},{... | collective-permute-start | bytes 884744 | tf_op jit(solution)/shard_map/ppermute | solution.py:381
  186.8 7.4 %copy-start.7 = (f32[4,96,768]{2,1,0:T(8,128)S(1)}, f32[4,96,768]{2,1,0:T(8,128)}, u32[]{:S(2)}) copy-start(f32[4,96,768]{2,1,0:T(8,128)} %get-tuple-element.107) | copy-start | bytes 3538948
  186.9 8.7 %copy-start.5 = (f32[128,768]{1,0:T(8,128)}, f32[128,768]{1,0:T(8,128)S(1)}, u32[]{:S(2)}) copy-start(f32[128,768]{1,0:T(8,128)S(1)} %add.167.own) | copy-start | bytes 1179652
  186.9 8.7 %collective-permute-start.16 = (f32[128,768]{1,0:T(8,128)S(1)}, f32[128,768]{1,0:T(8,128)S(1)}, u32[]{:S(2)}, u32[]{:S(2)}) collective-permute-start(f32[128,768]{1,0:T(8,128)S(1)} %add.167.own), channel_id=1, source_target_pairs={{0,1},{1,0},{2,3},{3,2},{4,5},{5,4},{6,7},{7,6},{8,9},{9,8},{10,11... | collective-permute-start | bytes 1179656 | tf_op jit(solution)/shard_map/ppermute | solution.py:366
  200.1 3.7 %collective-permute-start.19 = (f32[4,1,384]{2,0,1:T(4,128)S(1)}, f32[4,1,384]{2,0,1:T(4,128)S(1)}, u32[]{:S(2)}, u32[]{:S(2)}) collective-permute-start(f32[4,1,384]{2,0,1:T(4,128)S(1)} %bitcast.84), channel_id=1, source_target_pairs={{0,4},{4,0},{8,12},{12,8},{16,20},{20,16},{24,28},{28,24},{1,5},{5... | collective-permute-start | bytes 18440 | tf_op jit(solution)/shard_map/ppermute | solution.py:381
  201.7 15.8 %collective-permute-start.23 = (f32[2,1,96,768]{3,2,1,0:T(8,128)S(1)}, f32[2,1,96,768]{3,2,1,0:T(8,128)S(1)}, u32[]{:S(2)}, u32[]{:S(2)}) collective-permute-start(f32[2,1,96,768]{3,2,1,0:T(8,128)S(1)} %dynamic-slice_bitcast_fusion.3), channel_id=1, source_target_pairs={{0,8},{4,12},{8,0},{12,4},{16,24},{20,28},{24,16},{28,20},{1,9},{5... | collective-permute-start | bytes 1769480 | tf_op jit(solution)/shard_map/ppermute | solution.py:381
  203.8 12.3 %collective-permute-start.20 = (f32[2,1,384]{2,1,0:T(1,128)S(1)}, f32[2,1,384]{2,1,0:T(1,128)S(1)}, u32[]{:S(2)}, u32[]{:S(2)}) collective-permute-start(f32[2,1,384]{2,1,0:T(1,128)S(1)} %fusion.4), channel_id=1, source_target_pairs={{0,8},{4,12},{8,0},{12,4},{16,24},{20,28},{24,16},{28,20},{1,9},{5... | collective-permute-start | bytes 9224 | tf_op jit(solution)/shard_map/ppermute | solution.py:381
  216.2 9.9 %collective-permute-start.21 = (f32[1,1,384]{2,1,0:T(1,128)S(1)}, f32[1,1,384]{2,1,0:T(1,128)S(1)}, u32[]{:S(2)}, u32[]{:S(2)}) collective-permute-start(f32[1,1,384]{2,1,0:T(1,128)S(1)} %constant_dynamic-slice_fusion.5), channel_id=1, source_target_pairs={{0,16},{4,20},{8,24},{12,28},{16,0},{20,4},{24,8},{28,12},{1,17},{... | collective-permute-start | bytes 4616 | tf_op jit(solution)/shard_map/ppermute | solution.py:381
  217.6 14.2 %collective-permute-start.24 = (f32[1,1,96,768]{3,2,1,0:T(8,128)S(1)}, f32[1,1,96,768]{3,2,1,0:T(8,128)S(1)}, u32[]{:S(2)}, u32[]{:S(2)}) collective-permute-start(f32[1,1,96,768]{3,2,1,0:T(8,128)S(1)} %constant_dynamic-slice_fusion.4), channel_id=1, source_target_pairs={{0,16},{4,20},{8,24},{12,28},{16,0},{20,4},{24,8},{28,12},{1,17},{... | collective-permute-start | bytes 884744 | tf_op jit(solution)/shard_map/ppermute | solution.py:381
  (14 other events, 38.3 us)

commit v3 on v2

v3 whole, which is shorter than its diff:
```python
import functools
import math

import jax
import jax.numpy as jnp
from jax import lax
from jax.experimental import pallas as pl
from jax.experimental.pallas import tpu as pltpu
from jax.sharding import PartitionSpec as P


epsilon = 1e-06
masked_value = -1000000000.0
gelu_rate = 0.7978845608028654
gelu_cube = 0.044715
f32 = jnp.float32
bf16 = jnp.bfloat16
spare_bytes = 12 * 2**20


def product(left, right):
    return jnp.dot(left, right, preferred_element_type=f32)


def product_left(left, right):
    return lax.dot_general(left, right, (((0,), (0,)), ((), ())), preferred_element_type=f32)


def product_right(left, right):
    return lax.dot_general(left, right, (((1,), (1,)), ((), ())), preferred_element_type=f32)


def inverse_rms(values):
    return lax.rsqrt(jnp.mean(values * values, axis=-1, keepdims=True) + epsilon)


def norm_pull(values, gain_row, cotangent):
    scale = inverse_rms(values)
    weighted = cotangent * gain_row
    mean_part = jnp.mean(weighted * values, axis=-1, keepdims=True)
    d_values = scale * weighted - values * (scale * scale * scale * mean_part)
    d_gain = jnp.sum(cotangent * values * scale, axis=0, keepdims=True)
    return d_values, d_gain


def core_bit():
    return lax.axis_index("tensor") & 1


def pair_bit():
    return lax.axis_index("dp") & 1


def as_row(ref):
    return ref[...].reshape(1, ref.shape[0])


def head_columns(values, head, width):
    return values[:, head * width : (head + 1) * width]


def split_halves(part_ref, send_ref, keep_ref, bit):
    half = keep_ref.shape[0]
    send_ref[...] = part_ref[pl.ds((1 - bit) * half, half), :]
    keep_ref[...] = part_ref[pl.ds(bit * half, half), :]


def join_halves(full_ref, own_ref, other_ref, bit):
    half = own_ref.shape[0]
    full_ref[pl.ds(bit * half, half), :] = own_ref[...]
    full_ref[pl.ds((1 - bit) * half, half), :] = other_ref[...]


def split_blocks(grad_ref, send_ref, keep_ref, bit):
    pairs, rows, _ = keep_ref.shape
    for pair in range(pairs):
        if rows % 8 == 0:
            start = 2 * pair * rows
            send_ref[pair] = grad_ref[pl.ds(pl.multiple_of(start + (1 - bit) * rows, 8), rows), :]
            keep_ref[pair] = grad_ref[pl.ds(pl.multiple_of(start + bit * rows, 8), rows), :]
        else:
            first = grad_ref[2 * pair * rows : (2 * pair + 1) * rows, :]
            second = grad_ref[(2 * pair + 1) * rows : (2 * pair + 2) * rows, :]
            send_ref[pair] = jnp.where(bit == 0, second, first)
            keep_ref[pair] = jnp.where(bit == 0, first, second)


def bucket_hits(buckets, count):
    size = buckets.shape[0]
    row = jnp.broadcast_to(as_row(buckets), (8, size)).astype(f32).astype(bf16)
    source = lax.broadcasted_iota(jnp.int32, (size, size), 0)
    target = lax.broadcasted_iota(jnp.int32, (size, size), 1)
    mirror = (source + target == size) | (source + target == 0)
    turned = product(row, mirror.astype(f32).astype(bf16))[:1]
    bucket_id = lax.broadcasted_iota(jnp.int32, (count, size), 0).astype(f32)
    return (bucket_id == turned).astype(f32)


def softmax_rows(scores):
    exp_scores = jnp.exp(scores - jnp.max(scores, axis=-1, keepdims=True))
    return exp_scores / jnp.sum(exp_scores, axis=-1, keepdims=True)


def self_forward(
    x_ref, gain, wq, wk, wv, wo, seg, buckets, table,
    normed_ref, qkv_ref, prob_ref, mix_ref, send_ref, keep_ref, part_ref,
):
    heads = table.shape[0]
    width = wq.shape[0]
    size = width // heads
    rows = x_ref.shape[0]
    x = x_ref[...].astype(f32)
    normed = (x * inverse_rms(x) * as_row(gain)).astype(bf16)
    normed_ref[...] = normed
    query = product_right(normed, wq[...]).astype(bf16)
    key_rows = product_right(normed, wk[...]).astype(bf16)
    values = product_right(normed, wv[...]).astype(bf16)
    qkv_ref[...] = jnp.concatenate([query, key_rows, values], axis=1)
    row_id = lax.broadcasted_iota(jnp.int32, (rows, rows), 0)
    col_id = lax.broadcasted_iota(jnp.int32, (rows, rows), 1)
    seg_row = seg[...]
    seg_col = jnp.sum(jnp.where(row_id == col_id, seg_row, 0), axis=1, keepdims=True)
    allowed = (row_id >= col_id) & (seg_col == seg_row)
    hit = bucket_hits(buckets, table.shape[1])
    table_f = table[...].astype(f32)
    by_offset = jnp.dot(table_f, hit, precision=lax.Precision.HIGHEST)
    mixes = []
    for h in range(heads):
        pattern = by_offset[h : h + 1]
        bias = pltpu.roll(
            jnp.broadcast_to(pattern, (rows, rows)), 0, 1, stride=1, stride_axis=0
        )
        scores = product_right(head_columns(query, h, size), head_columns(key_rows, h, size))
        prob = softmax_rows(jnp.where(allowed, scores + bias, masked_value))
        prob_ref[h] = prob
        mixes.append(product(prob.astype(bf16), head_columns(values, h, size)))
    mix = jnp.concatenate(mixes, axis=1).astype(bf16)
    mix_ref[...] = mix
    part_ref[...] = product(mix, wo[...])
    split_halves(part_ref, send_ref, keep_ref, core_bit())


def cross_forward(
    own, other, x_ref, gain, wq, wo, kv,
    resid_ref, normed_ref, query_ref, prob_ref, mix_ref, send_ref, keep_ref, part_ref, *, heads,
):
    width = wq.shape[0]
    size = width // heads
    join_halves(part_ref, own, other, core_bit())
    resid = x_ref[...].astype(f32) + part_ref[...]
    resid_ref[...] = resid
    normed = (resid * inverse_rms(resid) * as_row(gain)).astype(bf16)
    normed_ref[...] = normed
    query = product_right(normed, wq[...]).astype(bf16)
    query_ref[...] = query
    mixes = []
    for h in range(heads):
        key_h = kv[:, h * size : (h + 1) * size]
        value_h = kv[:, width + h * size : width + (h + 1) * size]
        prob = softmax_rows(product_right(head_columns(query, h, size), key_h))
        prob_ref[h] = prob
        mixes.append(product(prob.astype(bf16), value_h))
    mix = jnp.concatenate(mixes, axis=1).astype(bf16)
    mix_ref[...] = mix
    part_ref[...] = product(mix, wo[...])
    split_halves(part_ref, send_ref, keep_ref, core_bit())


def cross_key_value(enc, wk, wv, kv_ref):
    rows = enc[...]
    kv_ref[...] = jnp.concatenate(
        [product_right(rows, wk[...]).astype(bf16), product_right(rows, wv[...]).astype(bf16)],
        axis=1,
    )


def ff_both(
    own, other, resid_one, gain, wg, wu, wd, out_grad,
    resid_ref, normed_ref, hidden_ref, d_pre_ref, send_ref, keep_ref, part_ref,
):
    join_halves(part_ref, own, other, core_bit())
    resid = resid_one[...] + part_ref[...]
    resid_ref[...] = resid
    normed = (resid * inverse_rms(resid) * as_row(gain)).astype(bf16)
    normed_ref[...] = normed
    gate = product(normed, wg[...])
    up = product(normed, wu[...])
    d_hidden = product_right(out_grad[...], wd[...])
    square = gate * gate
    bend = jnp.tanh(gelu_rate * (gate + gelu_cube * (square * gate)))
    activ = 0.5 * gate * (1.0 + bend)
    slope = 0.5 * (1.0 + bend) + 0.5 * gate * (1.0 - bend * bend) * (
        gelu_rate * (1.0 + 3.0 * gelu_cube * square)
    )
    hidden_ref[...] = (activ * up).astype(bf16)
    d_gate = (d_hidden * up * slope).astype(bf16)
    d_up = (d_hidden * activ).astype(bf16)
    width = d_gate.shape[1]
    d_pre_ref[:, :width] = d_gate
    d_pre_ref[:, width:] = d_up
    part_ref[...] = product_right(d_gate, wg[...]) + product_right(d_up, wu[...])
    split_halves(part_ref, send_ref, keep_ref, core_bit())


def ff_pre_grads(
    normed, d_pre, gate_send, gate_keep, up_send, up_keep, grad_ref,
):
    width = grad_ref.shape[1]
    grad_ref[...] = product_left(normed[...], d_pre[:, :width])
    split_blocks(grad_ref, gate_send, gate_keep, pair_bit())
    grad_ref[...] = product_left(normed[...], d_pre[:, width:])
    split_blocks(grad_ref, up_send, up_keep, pair_bit())


def ff_down_grad(out_grad, hidden, down_ref):
    down = product_left(out_grad[...], hidden[...])
    blocks, rows, _ = down_ref.shape
    for block in range(blocks):
        down_ref[block] = down[block * rows : (block + 1) * rows, :]


def ff_output(hidden, wd, resid, out_send, out_keep, part_ref, resid_ref):
    part_ref[...] = lax.dot_general(
        wd[...], hidden[...], (((0,), (1,)), ((), ())), preferred_element_type=f32
    )
    split_blocks(part_ref, out_send, out_keep, core_bit())
    resid_ref[...] = jnp.transpose(resid[...])
    index = lax.axis_index("tensor")
    rows = out_keep.shape[1]
    out_keep[index >> 1] += resid_ref[pl.ds(pl.multiple_of(index * rows, 8), rows), :]


def cross_backward(
    own, other, resid_two, gain, out_grad, wo, wq, prob, query, kv, mix,
    grad_ref, grad_b_ref, d_gain_ref, d_mix_ref, d_score_ref, d_query_ref, send_ref, keep_ref,
    part_ref, *, heads,
):
    width = wq.shape[0]
    size = width // heads
    join_halves(part_ref, own, other, core_bit())
    d_resid, d_gain = norm_pull(resid_two[...], as_row(gain), part_ref[...])
    d_gain_ref[...] = d_gain
    grad = out_grad[...].astype(f32) + d_resid
    grad_ref[...] = grad
    grad_b = grad.astype(bf16)
    grad_b_ref[...] = grad_b
    d_mix = product_right(grad_b, wo[...]).astype(bf16)
    d_mix_ref[...] = d_mix
    drift = d_mix.astype(f32) * mix[...].astype(f32)
    d_queries = []
    for h in range(heads):
        key_h = kv[:, h * size : (h + 1) * size]
        value_h = kv[:, width + h * size : width + (h + 1) * size]
        delta = jnp.sum(head_columns(drift, h, size), axis=1, keepdims=True)
        d_prob = product_right(head_columns(d_mix, h, size), value_h)
        d_score = (prob[h] * (d_prob - delta)).astype(bf16)
        d_score_ref[h] = d_score
        d_queries.append(product(d_score, key_h))
    d_query = jnp.concatenate(d_queries, axis=1).astype(bf16)
    d_query_ref[...] = d_query
    part_ref[...] = product(d_query, wq[...])
    split_halves(part_ref, send_ref, keep_ref, core_bit())


def cross_grads(
    normed, enc, grad_b, mix, prob, query, d_mix, d_score, d_query, wk, wv,
    send_ref, keep_ref, enc_send, enc_keep, grad_ref, part_ref, *, heads,
):
    width = wk.shape[0]
    size = width // heads
    d_keys = []
    d_values = []
    for h in range(heads):
        d_keys.append(product_left(d_score[h], query[:, h * size : (h + 1) * size]))
        d_values.append(product_left(prob[h].astype(bf16), d_mix[:, h * size : (h + 1) * size]))
    d_key = jnp.concatenate(d_keys, axis=1).astype(bf16)
    d_value = jnp.concatenate(d_values, axis=1).astype(bf16)
    part_ref[...] = lax.dot_general(
        wk[...], d_key, (((0,), (1,)), ((), ())), preferred_element_type=f32
    ) + lax.dot_general(wv[...], d_value, (((0,), (1,)), ((), ())), preferred_element_type=f32)
    split_blocks(part_ref, enc_send, enc_keep, core_bit())
    grad_ref[:, : 2 * width] = product_left(enc[...], jnp.concatenate([d_key, d_value], axis=1))
    grad_ref[:, 2 * width :] = jnp.concatenate(
        [product_left(normed[...], d_query[...]), product_left(grad_b[...], mix[...])], axis=1
    )
    split_blocks(grad_ref, send_ref, keep_ref, pair_bit())


def self_backward(
    own, other, resid_one, gain, grad_two, wo, wq, wk, wv, prob, qkv, mix,
    grad_ref, grad_b_ref, d_gain_ref, d_score_ref, d_qkv_ref, send_ref, keep_ref,
    part_ref, *, heads,
):
    width = wq.shape[0]
    size = width // heads
    join_halves(part_ref, own, other, core_bit())
    d_resid, d_gain = norm_pull(resid_one[...], as_row(gain), part_ref[...])
    d_gain_ref[...] = d_gain
    grad = grad_two[...] + d_resid
    grad_ref[...] = grad
    grad_b = grad.astype(bf16)
    grad_b_ref[...] = grad_b
    d_mix = product_right(grad_b, wo[...]).astype(bf16)
    drift = d_mix.astype(f32) * mix[...].astype(f32)
    d_queries = []
    d_keys = []
    d_values = []
    for h in range(heads):
        query_h = qkv[:, h * size : (h + 1) * size]
        key_h = qkv[:, width + h * size : width + (h + 1) * size]
        value_h = qkv[:, 2 * width + h * size : 2 * width + (h + 1) * size]
        d_mix_h = head_columns(d_mix, h, size)
        delta = jnp.sum(head_columns(drift, h, size), axis=1, keepdims=True)
        prob_h = prob[h]
        d_score = prob_h * (product_right(d_mix_h, value_h) - delta)
        d_score_ref[h] = d_score
        d_score_b = d_score.astype(bf16)
        d_queries.append(product(d_score_b, key_h))
        d_keys.append(product_left(d_score_b, query_h))
        d_values.append(product_left(prob_h.astype(bf16), d_mix_h))
    d_query = jnp.concatenate(d_queries, axis=1).astype(bf16)
    d_key = jnp.concatenate(d_keys, axis=1).astype(bf16)
    d_value = jnp.concatenate(d_values, axis=1).astype(bf16)
    d_qkv_ref[...] = jnp.concatenate([d_query, d_key, d_value], axis=1)
    part_ref[...] = (
        product(d_query, wq[...]) + product(d_key, wk[...]) + product(d_value, wv[...])
    )
    split_halves(part_ref, send_ref, keep_ref, core_bit())


def shift_left_by_row(values):
    rows, columns = values.shape
    row_id = lax.broadcasted_iota(jnp.int32, values.shape, 0)
    step = 1
    while step < rows:
        rolled = pltpu.roll(values, columns - step, 1)
        values = jnp.where(row_id & step != 0, rolled, values)
        step *= 2
    return values


def self_grads(
    normed, grad_b, mix, d_qkv, d_score, buckets,
    send_ref, keep_ref, rest_ref, d_bias_ref, grad_ref, *, heads,
):
    width = mix.shape[1]
    grad_ref[...] = product_left(normed[...], d_qkv[:, : 2 * width])
    split_blocks(grad_ref, send_ref, keep_ref, pair_bit())
    rest = jnp.concatenate(
        [
            product_left(normed[...], d_qkv[:, 2 * width :]),
            product_left(grad_b[...], mix[...]),
        ],
        axis=1,
    )
    blocks, rows, _ = rest_ref.shape
    for block in range(blocks):
        rest_ref[block] = rest[block * rows : (block + 1) * rows, :]
    hit = bucket_hits(buckets, d_bias_ref.shape[1])
    by_offset = jnp.concatenate(
        [
            jnp.sum(shift_left_by_row(d_score[h]), axis=0, keepdims=True)
            for h in range(heads)
        ],
        axis=0,
    )
    d_bias_ref[...] = lax.dot_general(
        by_offset, hit, (((1,), (1,)), ((), ())), precision=lax.Precision.HIGHEST
    )


def input_grad(
    own, other, x_ref, gain, grad_one, d_gain_cross, d_gain_ff, d_bias,
    d_input_ref, small_ref, part_ref,
):
    join_halves(part_ref, own, other, core_bit())
    d_resid, d_gain = norm_pull(x_ref[...].astype(f32), as_row(gain), part_ref[...])
    d_input_ref[...] = grad_one[...] + d_resid
    blocks = small_ref.shape[0]
    share = d_gain.shape[1] // blocks
    for place, row in enumerate((d_gain, d_gain_cross[...], d_gain_ff[...])):
        for block in range(blocks):
            small_ref[block : block + 1, place * share : (place + 1) * share] = row[
                :, block * share : (block + 1) * share
            ]
    heads, count = d_bias.shape
    for h in range(heads):
        small_ref[:, 3 * share + h * count : 3 * share + (h + 1) * count] = jnp.broadcast_to(
            d_bias[h : h + 1, :], (blocks, count)
        )


def split_columns(keep, received, *out_refs):
    total = keep[...] + received[...]
    start = 0
    for out_ref in out_refs:
        out_ref[...] = total[:, start : start + out_ref.shape[1]]
        start += out_ref.shape[1]


def kernel_call(body, outs, scratch, *operands, **static):
    if static:
        body = functools.partial(body, **static)

    def size_of(shape, dtype):
        lanes = -(-shape[-1] // 128) * 128
        return math.prod(shape[:-1]) * lanes * jnp.dtype(dtype).itemsize

    used = sum(size_of(shape, dtype) for shape, dtype in outs)
    used += sum(size_of(operand.shape, operand.dtype) for operand in operands)
    used += sum(size_of(shape, f32) for shape in scratch)
    vmem = pl.BlockSpec(memory_space=pltpu.VMEM)
    return pl.pallas_call(
        body,
        out_shape=[jax.ShapeDtypeStruct(shape, dtype) for shape, dtype in outs],
        in_specs=[vmem for unused in operands],
        out_specs=[vmem for unused in outs],
        scratch_shapes=[pltpu.VMEM(shape, f32) for shape in scratch],
        compiler_params=pltpu.CompilerParams(vmem_limit_bytes=used + spare_bytes),
    )(*operands)


def after(value, *anchors):
    return lax.optimization_barrier((value,) + anchors)[0]


def swap(value, axis_name, stride):
    count = lax.axis_size(axis_name)
    return lax.ppermute(value, axis_name, [(i, i ^ stride) for i in range(count)])


def swap_halves(send, keep, filler=None, before=()):
    count = lax.axis_size("tensor")
    received = swap(send, "tensor", 1)
    if before:
        received = after(received, *before)
    total = keep + received
    extra = None
    stride = 2
    while stride < count:
        received = swap(total, "tensor", stride)
        if filler is not None:
            extra, anchors = filler(total)
            received = after(received, *anchors)
            filler = None
        total = total + received
        stride *= 2
    return total, swap(total, "tensor", 1), extra


class BlockSum:
    def __init__(self, axis_name, bits, blocks=None, send=None, keep=None):
        self.axis_name = axis_name
        self.bits = list(bits)
        self.left = sorted(bits)
        if blocks is not None:
            (keep,), (send,) = self.choose(blocks)
        self.launch(send, keep)

    def choose(self, *parts):
        bit = self.bits[0]
        place = self.left.index(bit)
        low = 2**place
        high = 2 ** (len(self.left) - 1 - place)
        mine = (lax.axis_index(self.axis_name) >> bit) & 1

        def pick(part, which):
            shape = part.shape[1:]
            view = part.reshape((high, 2, low) + shape)
            picked = lax.dynamic_index_in_dim(view, which, 1, keepdims=False)
            return picked.reshape((high * low,) + shape)

        return [pick(part, mine) for part in parts], [pick(part, 1 - mine) for part in parts]

    def launch(self, send, keep):
        self.keep = keep
        self.received = swap(send, self.axis_name, 2 ** self.bits[0])
        self.left.remove(self.bits.pop(0))

    def advance(self, *anchors):
        received = after(self.received, *anchors) if anchors else self.received
        kept, sent = self.choose(self.keep, received)
        self.launch(sent[0] + sent[1], kept[0] + kept[1])
        return self.keep

    def finish(self, *anchors):
        while self.bits:
            self.advance(*anchors)
            anchors = ()
        received = after(self.received, *anchors) if anchors else self.received
        return self.keep[0], received[0]


def bit_list(axis_name):
    return list(range(lax.axis_size(axis_name).bit_length() - 1))


def on_device(
    layer_input,
    encoder_states,
    output_grad,
    segments,
    buckets,
    bias_table,
    gain_self,
    self_query,
    self_key,
    self_value,
    self_out,
    gain_cross,
    cross_query,
    cross_key,
    cross_value,
    cross_out,
    gain_ff,
    ff_gate,
    ff_up,
    ff_down,
):
    rows, model = layer_input.shape
    heads = bias_table.shape[1]
    width = self_query.shape[1]
    hidden_width = ff_gate.shape[1]
    dp_count = lax.axis_size("dp")
    tensor_count = lax.axis_size("tensor")
    share = model // dp_count
    dp_bits = bit_list("dp")
    tensor_bits = bit_list("tensor")
    high_first = dp_bits[1:] + dp_bits[:1]
    table_rows = bias_table.T
    query_rows, key_rows, value_rows = self_query.T, self_key.T, self_value.T
    cross_query_rows, cross_key_rows, cross_value_rows = cross_query.T, cross_key.T, cross_value.T
    full = (rows, model)
    half = ((rows // 2, model), f32)
    probs = (heads, rows, rows)
    pieces = ((tensor_count // 2, model // tensor_count, rows), f32)
    split = (dp_count // 2, share)

    normed_self, qkv, prob_self, mix_self, send, keep = kernel_call(
        self_forward,
        [(full, bf16), ((rows, 3 * width), bf16), (probs, f32), ((rows, width), bf16), half, half],
        [full],
        layer_input, gain_self, query_rows, key_rows, value_rows, self_out,
        segments, buckets, table_rows,
    )

    def fill_self(anchor):
        (kv,) = kernel_call(
            cross_key_value,
            [((rows, 2 * width), bf16)],
            [],
            after(encoder_states, anchor), cross_key_rows, cross_value_rows,
        )
        return kv, (kv,)

    own, other, kv = swap_halves(send, keep, fill_self)
    resid_one, normed_cross, query, prob_cross, mix_cross, send, keep = kernel_call(
        cross_forward,
        [(full, f32), (full, bf16), ((rows, width), bf16), (probs, f32), ((rows, width), bf16),
         half, half],
        [full],
        own, other, layer_input, gain_cross, cross_query_rows, cross_out, kv,
        heads=heads,
    )
    own, other, _ = swap_halves(send, keep)
    resid_two, normed_ff, hidden, d_pre, send, keep = kernel_call(
        ff_both,
        [(full, f32), (full, bf16), ((rows, hidden_width), bf16), ((rows, 2 * hidden_width), bf16),
         half, half],
        [full],
        own, other, resid_one, gain_ff, ff_gate, ff_up, ff_down, output_grad,
    )
    piece = (split + (hidden_width,), f32)
    gate_send, gate_keep, up_send, up_keep = kernel_call(
        ff_pre_grads,
        [piece, piece, piece, piece],
        [(model, hidden_width)],
        normed_ff, d_pre,
    )
    gate_sum = BlockSum("dp", dp_bits, send=gate_send, keep=gate_keep)
    up_sum = BlockSum("dp", dp_bits, send=up_send, keep=up_keep)

    def fill_ff(anchor):
        (down_blocks,) = kernel_call(
            ff_down_grad,
            [((dp_count, share, hidden_width), f32)],
            [],
            after(output_grad, anchor), hidden,
        )
        down_sum = BlockSum("dp", high_first, blocks=down_blocks)
        out_send, out_keep = kernel_call(
            ff_output,
            [pieces, pieces],
            [(model, rows), (model, rows)],
            after(hidden, down_blocks), ff_down, resid_two,
        )
        out_sum = BlockSum("tensor", tensor_bits, send=out_send, keep=out_keep)
        return (down_sum, out_sum), (down_sum.keep, out_keep)

    own, other, (down_sum, out_sum) = swap_halves(send, keep, fill_ff, (gate_send,))
    grad_two, grad_two_b, d_gain_ff, d_mix, d_score, d_query, send, keep = kernel_call(
        cross_backward,
        [(full, f32), (full, bf16), ((1, model), f32), ((rows, width), bf16), (probs, bf16),
         ((rows, width), bf16), half, half],
        [full],
        own, other, resid_two, gain_ff, output_grad, cross_out, cross_query_rows,
        prob_cross, query, kv, mix_cross,
        heads=heads,
    )
    out_sum.advance(grad_two)

    def fill_cross(anchor):
        moved = [down_sum.advance(anchor), gate_sum.advance(anchor)]
        cross_send, cross_keep, enc_send, enc_keep = kernel_call(
            cross_grads,
            [(split + (4 * width,), f32), (split + (4 * width,), f32), pieces, pieces],
            [(model, 4 * width), (model, rows)],
            normed_cross, encoder_states, grad_two_b, mix_cross, prob_cross, query, d_mix,
            after(d_score, *moved), d_query, cross_key_rows, cross_value_rows,
            heads=heads,
        )
        cross_sum = BlockSum("dp", dp_bits, send=cross_send, keep=cross_keep)
        enc_sum = BlockSum("tensor", tensor_bits, send=enc_send, keep=enc_keep)
        return (cross_sum, enc_sum), (cross_keep,)

    own, other, (cross_sum, enc_sum) = swap_halves(send, keep, fill_cross)
    grad_one, grad_one_b, d_gain_cross, d_score_self, d_qkv, send, keep = kernel_call(
        self_backward,
        [(full, f32), (full, bf16), ((1, model), f32), (probs, f32), ((rows, 3 * width), bf16),
         half, half],
        [full],
        own, other, resid_one, gain_cross, grad_two, self_out, query_rows, key_rows,
        value_rows, prob_self, qkv, mix_self,
        heads=heads,
    )
    enc_sum.advance(grad_one)

    def fill_input(anchor):
        moved = [chain.advance(anchor) for chain in (down_sum, gate_sum, up_sum)]
        self_send, self_keep, rest_blocks, d_bias = kernel_call(
            self_grads,
            [(split + (2 * width,), f32), (split + (2 * width,), f32),
             ((dp_count, share, 2 * width), f32), (table_rows.shape, f32)],
            [(model, 2 * width)],
            after(normed_self, *moved), grad_one_b, mix_self, d_qkv, d_score_self, buckets,
            heads=heads,
        )
        self_sum = BlockSum("dp", dp_bits, send=self_send, keep=self_keep)
        rest_sum = BlockSum("dp", high_first, blocks=rest_blocks)
        return (self_sum, rest_sum, d_bias), (self_keep, rest_sum.keep)

    own, other, (self_sum, rest_sum, d_bias) = swap_halves(send, keep, fill_input)
    d_layer_input, small = kernel_call(
        input_grad,
        [(full, f32), ((dp_count, 3 * share + d_bias.size), f32)],
        [full],
        own, other, layer_input, gain_self, grad_one, d_gain_cross, d_gain_ff, d_bias,
    )
    small_sum = BlockSum("dp", dp_bits, blocks=small)

    def columns(chain, pieces, *anchors):
        kept, received = chain.finish(*anchors)
        return kernel_call(
            split_columns, [((share, width), f32) for _ in range(pieces)], [], kept, received
        )

    kept, received = out_sum.finish(d_layer_input)
    layer_output = (kept + received).astype(bf16).T
    kept, received = enc_sum.finish(d_layer_input)
    d_encoder_states = (kept + received).T
    kept, received = gate_sum.finish(d_layer_input)
    gate_rows = kept + received
    up_sum.advance(gate_rows)
    kept, received = down_sum.finish(gate_rows)
    down_rows = kept + received
    small_sum.advance(down_rows)
    cross_sum.advance(down_rows)
    kept, received = up_sum.finish(cross_sum.keep)
    up_rows = kept + received
    rest_sum.advance(up_rows)
    small_sum.advance(rest_sum.keep)
    self_sum.advance(rest_sum.keep)
    d_cross_key, d_cross_value, d_cross_query, d_cross_out = columns(cross_sum, 4, self_sum.keep)
    d_self_value, d_self_out = columns(rest_sum, 2, d_cross_out)
    kept, received = small_sum.finish(d_cross_out)
    small = kept + received
    d_self_query, d_self_key = columns(self_sum, 2, d_self_out)
    return (
        layer_output,
        d_layer_input,
        d_encoder_states,
        small[3 * share :].reshape(table_rows.shape).T,
        small[:share],
        d_self_query,
        d_self_key,
        d_self_value,
        d_self_out.T,
        small[share : 2 * share],
        d_cross_query,
        d_cross_key,
        d_cross_value,
        d_cross_out.T,
        small[2 * share : 3 * share],
        gate_rows,
        up_rows,
        down_rows.T,
    )


def solution(mesh):
    in_specs = (
        P("dp", None),
        P("dp", None),
        P("dp", None),
        P("dp", None),
        P(),
        P(None, "tensor"),
        P(),
        P(None, "tensor"),
        P(None, "tensor"),
        P(None, "tensor"),
        P("tensor", None),
        P(),
        P(None, "tensor"),
        P(None, "tensor"),
        P(None, "tensor"),
        P("tensor", None),
        P(),
        P(None, "tensor"),
        P(None, "tensor"),
        P("tensor", None),
    )
    out_specs = (
        P("dp", "tensor"),
        P("dp", None),
        P("dp", "tensor"),
        P(None, "tensor"),
        P("dp"),
        P("dp", "tensor"),
        P("dp", "tensor"),
        P("dp", "tensor"),
        P("tensor", "dp"),
        P("dp"),
        P("dp", "tensor"),
        P("dp", "tensor"),
        P("dp", "tensor"),
        P("tensor", "dp"),
        P("dp"),
        P("dp", "tensor"),
        P("dp", "tensor"),
        P("tensor", "dp"),
    )
    return jax.shard_map(
        on_device, mesh=mesh, in_specs=in_specs, out_specs=out_specs, check_vma=False
    )
```

time: 234 us -> 232 us (level)
  Pallas kernels: 43.9 us -> 24.1 us
  other arithmetic: 23.5 us -> 33.9 us
  waiting for transfers between devices: 94.5 us -> 101 us
  local copies, waits for them, and re-layouts: 33.4 us -> 29 us
  starting transfers between devices: 36.9 us -> 41 us
    pallas_call x10 -> x15, Pallas kernels: 43.9 us -> 24.1 us  [kernel_call(): pl.pallas_call(body, out_shape=[jax.ShapeDtypeStruct(shape, dtype) for sh...]
    add x23 -> x33, other arithmetic: 15.3 us -> 28.9 us  [the longest x20 23.6 us: advance(): self.launch(sent[0] + sent[1], kept[0] + kept[1])]
    ppermute x34 -> x40, waiting for transfers between devices: 94.5 us -> 101 us  [swap(): lax.ppermute(value, axis_name, [(i, i ^ stride) for i in range(count)])]
    unnamed x70 -> x170, local copies, waits for them, and re-layouts: 17.5 us -> 23.3 us
    squeeze x12 -> x0, local copies, waits for them, and re-layouts: 5.6 us -> none  [halve_blocks(): send = lax.dynamic_index_in_dim(view, 1 - mine, 1, keepdims=False)]
    ppermute x34 -> x40, starting transfers between devices: 36.9 us -> 41 us  [swap(): lax.ppermute(value, axis_name, [(i, i ^ stride) for i in range(count)])]
    transpose x1 -> x3, other arithmetic: 1.63 us -> 5.07 us  [the longest x1 1.73 us: on_device(): d_encoder_states = (kept + received).T]
    another operation x5 -> x0, other arithmetic: 3.32 us -> none  [the longest x4 2.74 us: halve_blocks(): return blocks[0]]
  transfers between devices with their start and end apart: 34 -> 40, of which waited for: 17 -> 25; matrix products, arithmetic and copies ran while one was open for 15% -> 18% of each run, Pallas kernels for 12% -> 7%
where the time goes in v3:
time: 232 us; the launch traced here: 230 us
  waiting for transfers between devices  101 us (44%)
  starting transfers between devices  41 us (18%)
  other arithmetic  33.9 us (15%)
  local copies, waits for them, and re-layouts  29 us (12%)
  Pallas kernels  24.1 us (10%)
    ppermute x40, waiting for transfers between devices, swap(): lax.ppermute(value, axis_name, [(i, i ^ stride) for i in range(count)])  101 us
    ppermute x40, starting transfers between devices, swap(): lax.ppermute(value, axis_name, [(i, i ^ stride) for i in range(count)])  41 us
    pallas_call x15, Pallas kernels, kernel_call(): pl.pallas_call(body, out_shape=[jax.ShapeDtypeStruct(shape, dtype) for sh...  24.1 us
    add x20, other arithmetic, advance(): self.launch(sent[0] + sent[1], kept[0] + kept[1])  23.6 us
    unnamed x170, local copies, waits for them, and re-layouts  23.3 us
  transfers between devices with their start and end apart: 40, of which 25 were waited for; matrix products, arithmetic and copies ran while one was open for 18% of the time, Pallas kernels for 7%

profile of v3, /device:TPU:0, one launch (start us, length us, event | category | flops | bytes accessed | tf_op | source)
XLA Modules:
  0.0 230.3 jit_solution(17666970377795596276)
XLA Ops:
  8.2 1.9 shard_map.331
  12.2 2.9 %collective-permute-start.1 = (f32[128,768]{1,0:T(8,128)S(1)}, f32[128,768]{1,0:T(8,128)S(1)}, u32[]{:S(2)}, u32[]{:S(2)}) collective-permute-start(f32[128,768]{1,0:T(8,128)S(1)} %add.350), channel_id=1, source_target_pairs={{0,2},{1,3},{2,0},{3,1},{4,6},{5,7},{6,4},{7,5},{8,10},{9,11},{10,... | collective-permute-start | bytes 1179656 | tf_op jit(solution)/shard_map/ppermute | solution.py:429
  15.6 8.9 %collective-permute-done.1 = f32[128,768]{1,0:T(8,128)S(1)} collective-permute-done((f32[128,768]{1,0:T(8,128)S(1)}, f32[128,768]{1,0:T(8,128)S(1)}, u32[]{:S(2)}, u32[]{:S(2)}) %collective-permute-start.1) | collective-permute-done | bytes 393248 | tf_op jit(solution)/shard_map/ppermute | solution.py:429
  24.6 1.7 collective-permute-done.2.other
  26.4 1.8 shard_map.333
  28.4 1.6 collective-permute-done.3
  30.1 1.8 collective-permute-start.4
  31.9 9.4 %collective-permute-done.4 = f32[128,768]{1,0:T(8,128)S(1)} collective-permute-done((f32[128,768]{1,0:T(8,128)S(1)}, f32[128,768]{1,0:T(8,128)S(1)}, u32[]{:S(2)}, u32[]{:S(2)}) %collective-permute-start.4) | collective-permute-done | bytes 393248 | tf_op jit(solution)/shard_map/ppermute | solution.py:429
  41.4 1.7 collective-permute-done.5.other
  43.2 1.9 shard_map.334
  46.9 1.8 collective-permute-start.8
  50.6 7.6 %collective-permute-done.8 = f32[128,768]{1,0:T(8,128)S(1)} collective-permute-done((f32[128,768]{1,0:T(8,128)S(1)}, f32[128,768]{1,0:T(8,128)S(1)}, u32[]{:S(2)}, u32[]{:S(2)}) %collective-permute-start.8) | collective-permute-done | bytes 393248 | tf_op jit(solution)/shard_map/ppermute | solution.py:429
  58.3 1.7 collective-permute-done.9.other
  60.0 2.3 shard_map.338
  66.9 1.8 collective-permute-start.18
  70.2 1.8 collective-permute-start.12
  74.6 3.0 %shard_map.339 = (f32[4,96,768]{2,1,0:T(8,128)}, f32[4,96,768]{2,1,0:T(8,128)S(1)}, f32[2,192,256]{2,1,0:T(8,128)S(1)}, f32[2,192,256]{2,1,0:T(8,128)S(1)}) custom-call(bf16[256,768]{1,0:T(8,128)(2,1)S(1)} %copy-done.56, bf16[256,768]{1,0:T(8,128)(2,1)S(1)} %copy-done.5, bf16[256,768]{1,0:T(8,128)(2,1)S(1)} %copy-done.58, bf16[256,192]{1,0:T(8,128)(2,1)S(1)} %copy-done.43, ...), custom_call_target="tpu_custom_call" | custom-call | tf_op jit(solution)/shard_map/pallas_call | solution.py:413
  82.1 1.8 collective-permute-start.28
  83.8 3.8 %collective-permute-done.18 = f32[4,96,512]{2,1,0:T(8,128)} collective-permute-done((f32[4,96,512]{2,1,0:T(8,128)}, f32[4,96,512]{2,1,0:T(8,128)}, u32[]{:S(2)}, u32[]{:S(2)}) %collective-permute-start.18) | collective-permute-done | bytes 786464 | tf_op jit(solution)/shard_map/ppermute | solution.py:429
  87.6 4.9 %collective-permute-done.16 = f32[4,96,512]{2,1,0:T(8,128)} collective-permute-done((f32[4,96,512]{2,1,0:T(8,128)}, f32[4,96,512]{2,1,0:T(8,128)}, u32[]{:S(2)}, u32[]{:S(2)}) %collective-permute-start.16) | collective-permute-done | bytes 786464 | tf_op jit(solution)/shard_map/ppermute | solution.py:429
  99.6 4.0 %shard_map.340 = (f32[256,768]{1,0:T(8,128)S(1)}, bf16[256,768]{1,0:T(8,128)(2,1)S(1)}, f32[1,768]{1,0:T(1,128)S(1)}, f32[3,256,256]{2,1,0:T(8,128)S(1)}, bf16[2...) custom-call(f32[128,768]{1,0:T(8,128)S(1)} %add.361.own, ...), custom_call_target="tpu_custom_call" | custom-call | tf_op jit(solution)/shard_map/pallas_call | solution.py:413
  103.7 2.1 fusion.2
  107.4 2.1 dynamic-slice_add_fusion.3
  109.6 2.6 %collective-permute-start.17 = (f32[2,96,512]{2,1,0:T(8,128)}, f32[2,96,512]{2,1,0:T(8,128)S(1)}, u32[]{:S(2)}, u32[]{:S(2)}) collective-permute-start(f32[2,96,512]{2,1,0:T(8,128)} %get-tuple-element.229), channel_id=1, source_target_pairs={{0,16},{4,20},{8,24},{12,28},{16,0},{20,4},{24,8},{28,12},{1,17},{... | collective-permute-start | bytes 1179656 | tf_op jit(solution)/shard_map/ppermute | solution.py:429
  113.9 1.6 dynamic-slice_add_fusion.7
  118.2 5.2 %collective-permute-done.19 = f32[2,96,512]{2,1,0:T(8,128)} collective-permute-done((f32[2,96,512]{2,1,0:T(8,128)}, f32[2,96,512]{2,1,0:T(8,128)}, u32[]{:S(2)}, u32[]{:S(2)}) %collective-permute-start.19) | collective-permute-done | bytes 393248 | tf_op jit(solution)/shard_map/ppermute | solution.py:429
  123.4 1.6 collective-permute-start.32
  125.0 5.2 %collective-permute-done.17 = f32[2,96,512]{2,1,0:T(8,128)S(1)} collective-permute-done((f32[2,96,512]{2,1,0:T(8,128)}, f32[2,96,512]{2,1,0:T(8,128)S(1)}, u32[]{:S(2)}, u32[]{:S(2)}) %collective-permute-start.17) | collective-permute-done | bytes 393248 | tf_op jit(solution)/shard_map/ppermute | solution.py:429
  132.1 2.6 %shard_map.341 = (f32[4,96,384]{2,1,0:T(8,128)S(1)}, f32[4,96,384]{2,1,0:T(8,128)S(1)}, f32[8,96,384]{2,1,0:T(8,128)S(1)}, f32[3,32]{1,0:T(4,128)S(1)}) custom-call(bf16[256,768]{1,0:T(8,128)(2,1)S(1)} %copy-done.45, bf16[256,768]{1,0:T(8,128)(2,1)S(1)} %copy-done.47, bf16[256,192]{1,0:T(8,128)(2,1)S(1)} %copy-done.39, bf16[256,576]{1,0:T(8,128)(2,1)S(1)} %copy-done.62, ...), custom_call_target="tpu_custom_call" | custom-call | tf_op jit(solution)/shard_map/pallas_call | solution.py:413
  134.9 1.9 dynamic-slice_add_fusion.6
  136.8 1.8 fusion.1
  138.7 3.0 %collective-permute-start.29 = (f32[2,96,512]{2,1,0:T(8,128)}, f32[2,96,512]{2,1,0:T(8,128)}, u32[]{:S(2)}, u32[]{:S(2)}) collective-permute-start(f32[2,96,512]{2,1,0:T(8,128)} %fusion.1), channel_id=1, source_target_pairs={{0,8},{4,12},{8,0},{12,4},{16,24},{20,28},{24,16},{28,20},{1,9},{5... | collective-permute-start | bytes 1179656 | tf_op jit(solution)/shard_map/ppermute | solution.py:429
  142.5 1.8 dynamic-slice_add_fusion.1
  146.3 2.6 %collective-permute-done.25 = f32[1,96,512]{2,1,0:T(8,128)S(1)} collective-permute-done((f32[1,96,512]{2,1,0:T(8,128)S(1)}, f32[1,96,512]{2,1,0:T(8,128)S(1)}, u32[]{:S(2)}, u32[]{:S(2)}) %collective-permute-start.25) | collective-permute-done | bytes 196640 | tf_op jit(solution)/shard_map/ppermute | solution.py:429
  153.1 2.2 collective-permute-done.29
  157.9 1.7 bitcast_add_fusion.6
  161.1 1.6 add_bitcast_fusion.4
  162.7 1.9 fusion
  165.5 1.7 add_bitcast_fusion.3
  167.2 1.7 fusion.9
  173.5 1.8 fusion.6
  177.1 9.9 %collective-permute-done.26 = f32[2,384]{1,0:T(2,128)S(1)} collective-permute-done((f32[2,384]{1,0:T(2,128)S(1)}, f32[2,384]{1,0:T(2,128)S(1)}, u32[]{:S(2)}, u32[]{:S(2)}) %collective-permute-start.26) | collective-permute-done | bytes 3104 | tf_op jit(solution)/shard_map/ppermute | solution.py:429
  188.5 2.7 %collective-permute-start.34 = (f32[1,96,768]{2,1,0:T(8,128)S(1)}, f32[1,96,768]{2,1,0:T(8,128)S(1)}, u32[]{:S(2)}, u32[]{:S(2)}) collective-permute-start(f32[1,96,768]{2,1,0:T(8,128)S(1)} %get-tuple-element.232), channel_id=1, source_target_pairs={{0,16},{4,20},{8,24},{12,28},{16,0},{20,4},{24,8},{28,12},{1,17},{... | collective-permute-start | bytes 884744 | tf_op jit(solution)/shard_map/ppermute | solution.py:429
  193.5 1.8 collective-permute-start.36
  195.3 19.1 %collective-permute-done.34 = f32[1,96,768]{2,1,0:T(8,128)S(1)} collective-permute-done((f32[1,96,768]{2,1,0:T(8,128)S(1)}, f32[1,96,768]{2,1,0:T(8,128)S(1)}, u32[]{:S(2)}, u32[]{:S(2)}) %collective-permute-start.34) | collective-permute-done | bytes 294944 | tf_op jit(solution)/shard_map/ppermute | solution.py:429
  215.2 1.6 collective-permute-start.38
  216.8 4.2 %collective-permute-done.38 = f32[1,96,384]{2,1,0:T(8,128)S(1)} collective-permute-done((f32[1,96,384]{2,1,0:T(8,128)S(1)}, f32[1,96,384]{2,1,0:T(8,128)S(1)}, u32[]{:S(2)}, u32[]{:S(2)}) %collective-permute-start.38) | collective-permute-done | bytes 147488 | tf_op jit(solution)/shard_map/ppermute | solution.py:429
  224.5 5.0 %collective-permute-done.39 = f32[1,96,384]{2,1,0:T(8,128)S(1)} collective-permute-done((f32[1,96,384]{2,1,0:T(8,128)S(1)}, f32[1,96,384]{2,1,0:T(8,128)S(1)}, u32[]{:S(2)}, u32[]{:S(2)}) %collective-permute-start.39) | collective-permute-done | bytes 147488 | tf_op jit(solution)/shard_map/ppermute | solution.py:429
  (260 shorter events, 69.4 us)
Async XLA Ops:
  10.2 1.9 collective-permute-start
  12.2 12.3 %collective-permute-start.1 = (f32[128,768]{1,0:T(8,128)S(1)}, f32[128,768]{1,0:T(8,128)S(1)}, u32[]{:S(2)}, u32[]{:S(2)}) collective-permute-start(f32[128,768]{1,0:T(8,128)S(1)} %add.350), channel_id=1, source_target_pairs={{0,2},{1,3},{2,0},{3,1},{4,6},{5,7},{6,4},{7,5},{8,10},{9,11},{10,... | collective-permute-start | bytes 1179656 | tf_op jit(solution)/shard_map/ppermute | solution.py:429
  24.5 1.8 collective-permute-start.2
  26.4 16.8 %copy-start.23 = (bf16[768,512]{1,0:T(8,128)(2,1)S(1)}, bf16[768,512]{1,0:T(8,128)(2,1)}, u32[]{:S(2)}) copy-start(bf16[768,512]{1,0:T(8,128)(2,1)} %wu.1) | copy-start | bytes 2359300
  28.2 13.2 %copy-start.55 = (bf16[256,768]{1,0:T(8,128)(2,1)}, bf16[256,768]{1,0:T(8,128)(2,1)S(1)}, u32[]{:S(2)}) copy-start(bf16[256,768]{1,0:T(8,128)(2,1)S(1)} %get-tuple-element.132.normed) | copy-start | bytes 1179652
  28.2 31.8 %copy-start.40 = (bf16[256,192]{1,0:T(8,128)(2,1)}, bf16[256,192]{1,0:T(8,128)(2,1)S(1)}, u32[]{:S(2)}) copy-start(bf16[256,192]{1,0:T(8,128)(2,1)S(1)} %get-tuple-element.126.query) | copy-start | bytes 294916
  28.2 31.8 %copy-start.42 = (bf16[256,192]{1,0:T(8,128)(2,1)}, bf16[256,192]{1,0:T(8,128)(2,1)S(1)}, u32[]{:S(2)}) copy-start(bf16[256,192]{1,0:T(8,128)(2,1)S(1)} %get-tuple-element.127.mix) | copy-start | bytes 294916
  28.2 1.8 collective-permute-start.3
  30.0 13.2 %copy-start.69 = (f32[768]{0:T(1024)S(1)}, f32[768]{0:T(1024)}, u32[]{:S(2)}) copy-start(f32[768]{0:T(1024)} %gain.9) | copy-start | bytes 9220
  30.1 11.2 %collective-permute-start.4 = (f32[128,768]{1,0:T(8,128)S(1)}, f32[128,768]{1,0:T(8,128)S(1)}, u32[]{:S(2)}, u32[]{:S(2)}) collective-permute-start(f32[128,768]{1,0:T(8,128)S(1)} %add.352), channel_id=1, source_target_pairs={{0,2},{1,3},{2,0},{3,1},{4,6},{5,7},{6,4},{7,5},{8,10},{9,11},{10,... | collective-permute-start | bytes 1179656 | tf_op jit(solution)/shard_map/ppermute | solution.py:429
  41.4 1.8 collective-permute-start.5
  45.1 1.8 collective-permute-start.6
  46.2 13.8 %copy-start.77 = (f32[4,96,512]{2,1,0:T(8,128)}, f32[4,96,512]{2,1,0:T(8,128)S(1)}, u32[]{:S(2)}) copy-start(f32[4,96,512]{2,1,0:T(8,128)S(1)} %get-tuple-element.172) | copy-start | bytes 2359300
  46.9 11.2 %collective-permute-start.8 = (f32[128,768]{1,0:T(8,128)S(1)}, f32[128,768]{1,0:T(8,128)S(1)}, u32[]{:S(2)}, u32[]{:S(2)}) collective-permute-start(f32[128,768]{1,0:T(8,128)S(1)} %add.354), channel_id=1, source_target_pairs={{0,2},{1,3},{2,0},{3,1},{4,6},{5,7},{6,4},{7,5},{8,10},{9,11},{10,... | collective-permute-start | bytes 1179656 | tf_op jit(solution)/shard_map/ppermute | solution.py:429
  58.2 1.8 collective-permute-start.9
  66.8 2.1 collective-permute-start.11
  66.9 20.7 %collective-permute-start.18 = (f32[4,96,512]{2,1,0:T(8,128)}, f32[4,96,512]{2,1,0:T(8,128)}, u32[]{:S(2)}, u32[]{:S(2)}) collective-permute-start(f32[4,96,512]{2,1,0:T(8,128)} %copy-done.78), channel_id=1, source_target_pairs={{0,4},{4,0},{8,12},{12,8},{16,20},{20,16},{24,28},{28,24},{1,5},{5... | collective-permute-start | bytes 2359304 | tf_op jit(solution)/shard_map/ppermute | solution.py:429
  70.2 11.2 %collective-permute-start.12 = (f32[128,768]{1,0:T(8,128)S(1)}, f32[128,768]{1,0:T(8,128)S(1)}, u32[]{:S(2)}, u32[]{:S(2)}) collective-permute-start(f32[128,768]{1,0:T(8,128)S(1)} %add.360), channel_id=1, source_target_pairs={{0,2},{1,3},{2,0},{3,1},{4,6},{5,7},{6,4},{7,5},{8,10},{9,11},{10,... | collective-permute-start | bytes 1179656 | tf_op jit(solution)/shard_map/ppermute | solution.py:429
  72.9 19.6 %collective-permute-start.16 = (f32[4,96,512]{2,1,0:T(8,128)}, f32[4,96,512]{2,1,0:T(8,128)}, u32[]{:S(2)}, u32[]{:S(2)}) collective-permute-start(f32[4,96,512]{2,1,0:T(8,128)} %bitcast.8), channel_id=1, source_target_pairs={{0,8},{4,12},{8,0},{12,4},{16,24},{20,28},{24,16},{28,20},{1,9},{5... | collective-permute-start | bytes 2359304 | tf_op jit(solution)/shard_map/ppermute | solution.py:429
  81.5 11.1 %collective-permute-start.13 = (f32[128,768]{1,0:T(8,128)S(1)}, f32[128,768]{1,0:T(8,128)}, u32[]{:S(2)}, u32[]{:S(2)}) collective-permute-start(f32[128,768]{1,0:T(8,128)S(1)} %add.361.own), channel_id=1, source_target_pairs={{0,1},{1,0},{2,3},{3,2},{4,5},{5,4},{6,7},{7,6},{8,9},{9,8},{10,11... | collective-permute-start | bytes 1179656 | tf_op jit(solution)/shard_map/ppermute | solution.py:429
  81.6 28.0 %collective-permute-start.7 = (f32[2,192,256]{2,1,0:T(8,128)}, f32[2,192,256]{2,1,0:T(8,128)}, u32[]{:S(2)}, u32[]{:S(2)}) collective-permute-start(f32[2,192,256]{2,1,0:T(8,128)} %get-tuple-element.123), channel_id=1, source_target_pairs={{0,1},{1,0},{2,3},{3,2},{4,5},{5,4},{6,7},{7,6},{8,9},{9,8},{10,11... | collective-permute-start | bytes 1179656 | tf_op jit(solution)/shard_map/ppermute | solution.py:429
  82.1 54.7 %collective-permute-start.28 = (f32[4,96,512]{2,1,0:T(8,128)}, f32[4,96,512]{2,1,0:T(8,128)}, u32[]{:S(2)}, u32[]{:S(2)}) collective-permute-start(f32[4,96,512]{2,1,0:T(8,128)} %copy-done.77), channel_id=1, source_target_pairs={{0,4},{4,0},{8,12},{12,8},{16,20},{20,16},{24,28},{28,24},{1,5},{5... | collective-permute-start | bytes 2359304 | tf_op jit(solution)/shard_map/ppermute | solution.py:429
  87.6 29.0 %collective-permute-start.21 = (f32[2,192,256]{2,1,0:T(8,128)}, f32[2,192,256]{2,1,0:T(8,128)}, u32[]{:S(2)}, u32[]{:S(2)}) collective-permute-start(f32[2,192,256]{2,1,0:T(8,128)} %copy-done.80), channel_id=1, source_target_pairs={{0,1},{1,0},{2,3},{3,2},{4,5},{5,4},{6,7},{7,6},{8,9},{9,8},{10,11... | collective-permute-start | bytes 1179656 | tf_op jit(solution)/shard_map/ppermute | solution.py:429
  103.6 8.6 %collective-permute-start.14 = (f32[128,768]{1,0:T(8,128)}, f32[128,768]{1,0:T(8,128)S(1)}, u32[]{:S(2)}, u32[]{:S(2)}) collective-permute-start(f32[128,768]{1,0:T(8,128)} %get-tuple-element.143), channel_id=1, source_target_pairs={{0,1},{1,0},{2,3},{3,2},{4,5},{5,4},{6,7},{7,6},{8,9},{9,8},{10,11... | collective-permute-start | bytes 1179656 | tf_op jit(solution)/shard_map/ppermute | solution.py:429
  105.8 17.6 %collective-permute-start.19 = (f32[2,96,512]{2,1,0:T(8,128)}, f32[2,96,512]{2,1,0:T(8,128)}, u32[]{:S(2)}, u32[]{:S(2)}) collective-permute-start(f32[2,96,512]{2,1,0:T(8,128)} %fusion.2), channel_id=1, source_target_pairs={{0,8},{4,12},{8,0},{12,4},{16,24},{20,28},{24,16},{28,20},{1,9},{5... | collective-permute-start | bytes 1179656 | tf_op jit(solution)/shard_map/ppermute | solution.py:429
  109.6 20.6 %collective-permute-start.17 = (f32[2,96,512]{2,1,0:T(8,128)}, f32[2,96,512]{2,1,0:T(8,128)S(1)}, u32[]{:S(2)}, u32[]{:S(2)}) collective-permute-start(f32[2,96,512]{2,1,0:T(8,128)} %get-tuple-element.229), channel_id=1, source_target_pairs={{0,16},{4,20},{8,24},{12,28},{16,0},{20,4},{24,8},{28,12},{1,17},{... | collective-permute-start | bytes 1179656 | tf_op jit(solution)/shard_map/ppermute | solution.py:429
  113.3 21.4 %collective-permute-start.15 = (f32[128,768]{1,0:T(8,128)S(1)}, f32[128,768]{1,0:T(8,128)S(1)}, u32[]{:S(2)}, u32[]{:S(2)}) collective-permute-start(f32[128,768]{1,0:T(8,128)S(1)} %add.362), channel_id=1, source_target_pairs={{0,2},{1,3},{2,0},{3,1},{4,6},{5,7},{6,4},{7,5},{8,10},{9,11},{10,... | collective-permute-start | bytes 1179656 | tf_op jit(solution)/shard_map/ppermute | solution.py:429
  115.5 15.7 %copy-start.81 = (f32[1,1,2,96,512]{4,3,2,1,0:T(8,128)S(1)}, f32[1,1,2,96,512]{4,3,2,1,0:T(8,128)}, u32[]{:S(2)}) copy-start(f32[1,1,2,96,512]{4,3,2,1,0:T(8,128)} %get-tuple-element.228) | copy-start | bytes 1179652
  116.6 40.7 %collective-permute-start.10 = (f32[1,192,256]{2,1,0:T(8,128)}, f32[1,192,256]{2,1,0:T(8,128)}, u32[]{:S(2)}, u32[]{:S(2)}) collective-permute-start(f32[1,192,256]{2,1,0:T(8,128)} %dynamic-slice_add_fusion.7), channel_id=1, source_target_pairs={{0,2},{1,3},{2,0},{3,1},{4,6},{5,7},{6,4},{7,5},{8,10},{9,11},{10,... | collective-permute-start | bytes 589832 | tf_op jit(solution)/shard_map/ppermute | solution.py:429
  123.4 39.3 %collective-permute-start.32 = (f32[4,96,768]{2,1,0:T(8,128)}, f32[4,96,768]{2,1,0:T(8,128)}, u32[]{:S(2)}, u32[]{:S(2)}) collective-permute-start(f32[4,96,768]{2,1,0:T(8,128)} %get-tuple-element.177), channel_id=1, source_target_pairs={{0,4},{4,0},{8,12},{12,8},{16,20},{20,16},{24,28},{28,24},{1,5},{5... | collective-permute-start | bytes 3538952 | tf_op jit(solution)/shard_map/ppermute | solution.py:429
  134.8 9.6 %collective-permute-start.20 = (f32[128,768]{1,0:T(8,128)S(1)}, f32[128,768]{1,0:T(8,128)S(1)}, u32[]{:S(2)}, u32[]{:S(2)}) collective-permute-start(f32[128,768]{1,0:T(8,128)S(1)} %add.376.own), channel_id=1, source_target_pairs={{0,1},{1,0},{2,3},{3,2},{4,5},{5,4},{6,7},{7,6},{8,9},{9,8},{10,11... | collective-permute-start | bytes 1179656 | tf_op jit(solution)/shard_map/ppermute | solution.py:429
  136.8 12.0 %collective-permute-start.25 = (f32[1,96,512]{2,1,0:T(8,128)S(1)}, f32[1,96,512]{2,1,0:T(8,128)S(1)}, u32[]{:S(2)}, u32[]{:S(2)}) collective-permute-start(f32[1,96,512]{2,1,0:T(8,128)S(1)} %get-tuple-element.234), channel_id=1, source_target_pairs={{0,16},{4,20},{8,24},{12,28},{16,0},{20,4},{24,8},{28,12},{1,17},{... | collective-permute-start | bytes 589832 | tf_op jit(solution)/shard_map/ppermute | solution.py:429
  138.7 16.6 %collective-permute-start.29 = (f32[2,96,512]{2,1,0:T(8,128)}, f32[2,96,512]{2,1,0:T(8,128)}, u32[]{:S(2)}, u32[]{:S(2)}) collective-permute-start(f32[2,96,512]{2,1,0:T(8,128)} %fusion.1), channel_id=1, source_target_pairs={{0,8},{4,12},{8,0},{12,4},{16,24},{20,28},{24,16},{28,20},{1,9},{5... | collective-permute-start | bytes 1179656 | tf_op jit(solution)/shard_map/ppermute | solution.py:429
  144.4 15.2 %collective-permute-start.22 = (f32[1,192,256]{2,1,0:T(8,128)}, f32[1,192,256]{2,1,0:T(8,128)}, u32[]{:S(2)}, u32[]{:S(2)}) collective-permute-start(f32[1,192,256]{2,1,0:T(8,128)} %dynamic-slice_add_fusion.6), channel_id=1, source_target_pairs={{0,2},{1,3},{2,0},{3,1},{4,6},{5,7},{6,4},{7,5},{8,10},{9,11},{10,... | collective-permute-start | bytes 589832 | tf_op jit(solution)/shard_map/ppermute | solution.py:429
  146.3 16.4 %copy-start.9 = (f32[4,96,768]{2,1,0:T(8,128)S(1)}, f32[4,96,768]{2,1,0:T(8,128)}, u32[]{:S(2)}) copy-start(f32[4,96,768]{2,1,0:T(8,128)} %copy-done.8) | copy-start | bytes 3538948
  148.8 7.0 %collective-permute-start.24 = (f32[1,96,512]{2,1,0:T(8,128)}, f32[1,96,512]{2,1,0:T(8,128)S(1)}, u32[]{:S(2)}, u32[]{:S(2)}) collective-permute-start(f32[1,96,512]{2,1,0:T(8,128)} %get-tuple-element.236), channel_id=1, source_target_pairs={{0,4},{4,0},{8,12},{12,8},{16,20},{20,16},{24,28},{28,24},{1,5},{5... | collective-permute-start | bytes 589832 | tf_op jit(solution)/shard_map/ppermute | solution.py:429
  155.3 20.7 %collective-permute-start.27 = (f32[4,96,384]{2,1,0:T(8,128)}, f32[4,96,384]{2,1,0:T(8,128)}, u32[]{:S(2)}, u32[]{:S(2)}) collective-permute-start(f32[4,96,384]{2,1,0:T(8,128)} %bitcast.172), channel_id=1, source_target_pairs={{0,8},{4,12},{8,0},{12,4},{16,24},{20,28},{24,16},{28,20},{1,9},{5... | collective-permute-start | bytes 1769480 | tf_op jit(solution)/shard_map/ppermute | solution.py:429
  155.9 35.6 %collective-permute-start.35 = (f32[4,96,384]{2,1,0:T(8,128)}, f32[4,96,384]{2,1,0:T(8,128)}, u32[]{:S(2)}, u32[]{:S(2)}) collective-permute-start(f32[4,96,384]{2,1,0:T(8,128)} %copy-done.79), channel_id=1, source_target_pairs={{0,4},{4,0},{8,12},{12,8},{16,20},{20,16},{24,28},{28,24},{1,5},{5... | collective-permute-start | bytes 1769480 | tf_op jit(solution)/shard_map/ppermute | solution.py:429
  157.4 13.4 %collective-permute-start.23 = (f32[4,384]{1,0:T(4,128)S(1)}, f32[4,384]{1,0:T(4,128)}, u32[]{:S(2)}, u32[]{:S(2)}) collective-permute-start(f32[4,384]{1,0:T(4,128)S(1)} %bitcast.174), channel_id=1, source_target_pairs={{0,4},{4,0},{8,12},{12,8},{16,20},{20,16},{24,28},{28,24},{1,5},{5... | collective-permute-start | bytes 18440 | tf_op jit(solution)/shard_map/ppermute | solution.py:429
  159.6 13.9 %collective-permute-start.30 = (f32[1,96,512]{2,1,0:T(8,128)}, f32[1,96,512]{2,1,0:T(8,128)}, u32[]{:S(2)}, u32[]{:S(2)}) collective-permute-start(f32[1,96,512]{2,1,0:T(8,128)} %bitcast_add_fusion.6), channel_id=1, source_target_pairs={{0,16},{4,20},{8,24},{12,28},{16,0},{20,4},{24,8},{28,12},{1,17},{... | collective-permute-start | bytes 589832 | tf_op jit(solution)/shard_map/ppermute | solution.py:429
  164.7 22.7 %collective-permute-start.33 = (f32[2,96,768]{2,1,0:T(8,128)}, f32[2,96,768]{2,1,0:T(8,128)}, u32[]{:S(2)}, u32[]{:S(2)}) collective-permute-start(f32[2,96,768]{2,1,0:T(8,128)} %fusion), channel_id=1, source_target_pairs={{0,8},{4,12},{8,0},{12,4},{16,24},{20,28},{24,16},{28,20},{1,9},{5... | collective-permute-start | bytes 1769480 | tf_op jit(solution)/shard_map/ppermute | solution.py:429
  171.5 15.5 %collective-permute-start.26 = (f32[2,384]{1,0:T(2,128)S(1)}, f32[2,384]{1,0:T(2,128)S(1)}, u32[]{:S(2)}, u32[]{:S(2)}) collective-permute-start(f32[2,384]{1,0:T(2,128)S(1)} %bitcast.175), channel_id=1, source_target_pairs={{0,8},{4,12},{8,0},{12,4},{16,24},{20,28},{24,16},{28,20},{1,9},{5... | collective-permute-start | bytes 9224 | tf_op jit(solution)/shard_map/ppermute | solution.py:429
  187.1 28.1 %collective-permute-start.37 = (f32[2,96,384]{2,1,0:T(8,128)S(1)}, f32[2,96,384]{2,1,0:T(8,128)S(1)}, u32[]{:S(2)}, u32[]{:S(2)}) collective-permute-start(f32[2,96,384]{2,1,0:T(8,128)S(1)} %get-tuple-element.230), channel_id=1, source_target_pairs={{0,16},{4,20},{8,24},{12,28},{16,0},{20,4},{24,8},{28,12},{1,17},{... | collective-permute-start | bytes 884744 | tf_op jit(solution)/shard_map/ppermute | solution.py:429
  188.5 25.9 %collective-permute-start.34 = (f32[1,96,768]{2,1,0:T(8,128)S(1)}, f32[1,96,768]{2,1,0:T(8,128)S(1)}, u32[]{:S(2)}, u32[]{:S(2)}) collective-permute-start(f32[1,96,768]{2,1,0:T(8,128)S(1)} %get-tuple-element.232), channel_id=1, source_target_pairs={{0,16},{4,20},{8,24},{12,28},{16,0},{20,4},{24,8},{28,12},{1,17},{... | collective-permute-start | bytes 884744 | tf_op jit(solution)/shard_map/ppermute | solution.py:429
  191.2 24.0 %collective-permute-start.31 = (f32[1,384]{1,0:T(1,128)S(1)}, f32[1,384]{1,0:T(1,128)S(1)}, u32[]{:S(2)}, u32[]{:S(2)}) collective-permute-start(f32[1,384]{1,0:T(1,128)S(1)} %fusion.13), channel_id=1, source_target_pairs={{0,16},{4,20},{8,24},{12,28},{16,0},{20,4},{24,8},{28,12},{1,17},{... | collective-permute-start | bytes 4616 | tf_op jit(solution)/shard_map/ppermute | solution.py:429
  193.5 28.2 %collective-permute-start.36 = (f32[2,96,384]{2,1,0:T(8,128)S(1)}, f32[2,96,384]{2,1,0:T(8,128)S(1)}, u32[]{:S(2)}, u32[]{:S(2)}) collective-permute-start(f32[2,96,384]{2,1,0:T(8,128)S(1)} %fusion.3), channel_id=1, source_target_pairs={{0,8},{4,12},{8,0},{12,4},{16,24},{20,28},{24,16},{28,20},{1,9},{5... | collective-permute-start | bytes 884744 | tf_op jit(solution)/shard_map/ppermute | solution.py:429
  215.2 5.8 %collective-permute-start.38 = (f32[1,96,384]{2,1,0:T(8,128)S(1)}, f32[1,96,384]{2,1,0:T(8,128)S(1)}, u32[]{:S(2)}, u32[]{:S(2)}) collective-permute-start(f32[1,96,384]{2,1,0:T(8,128)S(1)} %get-tuple-element.240), channel_id=1, source_target_pairs={{0,4},{4,0},{8,12},{12,8},{16,20},{20,16},{24,28},{28,24},{1,5},{5... | collective-permute-start | bytes 442376 | tf_op jit(solution)/shard_map/ppermute | solution.py:429
  221.7 7.9 %collective-permute-start.39 = (f32[1,96,384]{2,1,0:T(8,128)S(1)}, f32[1,96,384]{2,1,0:T(8,128)S(1)}, u32[]{:S(2)}, u32[]{:S(2)}) collective-permute-start(f32[1,96,384]{2,1,0:T(8,128)S(1)} %get-tuple-element.238), channel_id=1, source_target_pairs={{0,16},{4,20},{8,24},{12,28},{16,0},{20,4},{24,8},{28,12},{1,17},{... | collective-permute-start | bytes 442376 | tf_op jit(solution)/shard_map/ppermute | solution.py:429
  (75 other events, 374.4 us)
